TPU v7x, 32 devices: a whole 2x2x4 slice. The times are simulated.
32 devices in a mesh: gx: 4 (over y, x), gy: 8 (over z, core).
Axes of the slice: x: 2, y: 2, z: 4, core: 2. Of those that a mesh axis runs over, the one named last changes fastest.
Arguments:
- inputs: bfloat16 [16, 16, 32, 512], P('gx', 'gy'), may hold values from -6 to 6
- cotangent: bfloat16 [16, 16, 32, 512], P('gx', 'gy'), may hold values from -6 to 6
- point_weight: bfloat16 [32, 32], replicated, may hold values from -1 to 1
- spectral_weight: bfloat16 [2304, 24, 2048], P(('gx', 'gy')), may hold values from -0.75 to 0.75
Outputs:
- grad_input: bfloat16 [16, 16, 32, 512], P('gx', 'gy')
- grad_spectral: float32 [2304, 24, 2048], P(('gx', 'gy'))
All inputs are finite; a program needn't handle non-finite values.
Results may differ from a plain program's by a relative error of at most 0.034.
Values may be sent and summed in bfloat16 or wider, within the bound.
No kernel may reach another device: no remote copies, remote signals or barrier semaphores. Data moves between devices by JAX's collectives and lax.ppermute only.
A program may use at most 192 MiB of HBM per device.

v0:
```python
import math

import jax
import jax.numpy as jnp
from jax import lax
from jax.sharding import PartitionSpec as P

NZ = 64
NT = 8
KX = 24
KY = 24
KZ = 12
KT = 8


def kept_angles(positions, kept_count, length):
    index = jnp.arange(kept_count, dtype=jnp.int32)
    frequency = jnp.where(index < kept_count // 2, index, index - kept_count)
    turns = positions[:, None] * frequency[None, :] % length
    return turns.astype(jnp.float32) * (2.0 * math.pi / length)


def axis_tables(positions, kept_count, length):
    angles = kept_angles(positions, kept_count, length)
    return (jnp.cos(angles), jnp.sin(angles))


def depth_tables():
    angle_depth = kept_angles(jnp.arange(NZ, dtype=jnp.int32), KZ, NZ)
    angle_time = kept_angles(jnp.arange(NT, dtype=jnp.int32), KT, NT)
    angles = (angle_depth[:, None, :, None] + angle_time[None, :, None, :]).reshape(
        NZ * NT, KZ * KT
    )
    return (jnp.cos(angles), jnp.sin(angles))


def settle(values):
    return lax.optimization_barrier(values.astype(jnp.bfloat16))


def rotate(spectra, cosine_table, sine_table, pattern, turn_sign):
    half_width = spectra.shape[-1] // 2
    with_cosine = jnp.einsum(pattern, spectra, cosine_table, precision=lax.Precision.HIGHEST)
    with_sine = jnp.einsum(pattern, spectra, sine_table, precision=lax.Precision.HIGHEST)
    real_part = with_cosine[..., :half_width] + turn_sign * with_sine[..., half_width:]
    imag_part = with_cosine[..., half_width:] - turn_sign * with_sine[..., :half_width]
    return jnp.concatenate([real_part, imag_part], -1)


def depth_forward(field_in, tables, factor):
    widened = field_in.astype(jnp.float32)
    with_cosine = jnp.einsum("xycs,sk->kxyc", widened, tables[0], precision=lax.Precision.HIGHEST)
    with_sine = jnp.einsum("xycs,sk->kxyc", widened, tables[1], precision=lax.Precision.HIGHEST)
    return jnp.concatenate([with_cosine, -with_sine], -1) * factor


def depth_inverse(spectra, tables, factor):
    half_width = spectra.shape[-1] // 2
    with_cosine = jnp.einsum(
        "kxyc,sk->xycs", spectra[..., :half_width], tables[0], precision=lax.Precision.HIGHEST
    )
    with_sine = jnp.einsum(
        "kxyc,sk->xycs", spectra[..., half_width:], tables[1], precision=lax.Precision.HIGHEST
    )
    return (with_cosine - with_sine) * factor


def contract_in(left, right):
    return jnp.einsum("mkc,mkco->mko", left, right, precision=lax.Precision.HIGHEST)


def contract_out(left, right):
    return jnp.einsum("mko,mkco->mkc", left, right, precision=lax.Precision.HIGHEST)


def partial_outer(left, right):
    return jnp.einsum("mkc,mko->mkco", left, right, precision=lax.Precision.HIGHEST)


def mix_modes(spectra, weight):
    half_width = spectra.shape[-1] // 2
    weight_wide = weight.astype(jnp.float32)
    weight_real, weight_imag = (weight_wide[..., :half_width], weight_wide[..., half_width:])
    real_in, imag_in = (spectra[..., :half_width], spectra[..., half_width:])
    real_out = contract_in(real_in, weight_real) - contract_in(imag_in, weight_imag)
    imag_out = contract_in(real_in, weight_imag) + contract_in(imag_in, weight_real)
    return jnp.concatenate([real_out, imag_out], -1)


def adjoint_modes(spectra, weight):
    half_width = spectra.shape[-1] // 2
    weight_wide = weight.astype(jnp.float32)
    weight_real, weight_imag = (weight_wide[..., :half_width], weight_wide[..., half_width:])
    real_in, imag_in = (spectra[..., :half_width], spectra[..., half_width:])
    real_out = contract_out(real_in, weight_real) + contract_out(imag_in, weight_imag)
    imag_out = contract_out(imag_in, weight_real) - contract_out(real_in, weight_imag)
    return jnp.concatenate([real_out, imag_out], -1)


def weight_grad(spectra_in, spectra_back):
    half_width = spectra_in.shape[-1] // 2
    real_in, imag_in = (spectra_in[..., :half_width], spectra_in[..., half_width:])
    real_back, imag_back = (spectra_back[..., :half_width], spectra_back[..., half_width:])
    real_part = partial_outer(real_in, real_back) + partial_outer(imag_in, imag_back)
    imag_part = partial_outer(real_in, imag_back) - partial_outer(imag_in, real_back)
    return jnp.concatenate([real_part, imag_part], -1)


def exact_gelu(values):
    return jax.nn.gelu(values, approximate=False)


def per_device(inputs, cotangent, point_weight, spectral_weight):
    rows_x, rows_y, channels, cells = inputs.shape
    mode_rows, mode_cols, flat_width = spectral_weight.shape
    weight_blocks = spectral_weight.reshape(mode_rows, mode_cols, channels, 2 * channels)
    count_gx = lax.axis_size("gx")
    count_gy = lax.axis_size("gy")
    length_x = rows_x * count_gx
    length_y = rows_y * count_gy
    depth_pair = depth_tables()
    own_x = lax.axis_index("gx") * rows_x + jnp.arange(rows_x, dtype=jnp.int32)
    local_x = axis_tables(own_x, KX, length_x)
    whole_y = axis_tables(jnp.arange(length_y, dtype=jnp.int32), KY, length_y)
    total_cells = length_x * length_y * cells
    kept_total = KX * KY * KZ * KT

    def to_modes(field_in, factor):
        depth_spec = settle(depth_forward(field_in, depth_pair, factor))
        share = depth_spec.shape[0] // count_gx
        first_spectra = lax.psum_scatter(
            rotate(
                depth_spec.astype(jnp.float32), local_x[0], local_x[1], "rxyc,xk->rkyc", 1.0
            ).astype(jnp.bfloat16),
            "gx",
            scatter_dimension=0,
            tiled=True,
        ).astype(jnp.float32)
        first_spectra = settle(first_spectra).reshape(share * KX, rows_y, 2 * channels)
        arrived_modes = lax.all_to_all(first_spectra, "gy", split_axis=0, concat_axis=1, tiled=True)
        return rotate(arrived_modes.astype(jnp.float32), whole_y[0], whole_y[1], "myc,yk->mkc", 1.0)

    def to_space(spectra, factor):
        back_rows = settle(rotate(spectra, whole_y[0], whole_y[1], "mkc,yk->myc", -1.0))
        returned = lax.all_to_all(back_rows, "gy", split_axis=1, concat_axis=0, tiled=True)
        share = returned.shape[0] // KX
        returned = returned.reshape(share, KX, rows_y, 2 * channels)
        back_depth = settle(
            rotate(
                lax.all_gather(returned, "gx", axis=0, tiled=True).astype(jnp.float32),
                local_x[0],
                local_x[1],
                "rkyc,xk->rxyc",
                -1.0,
            )
        )
        return depth_inverse(back_depth.astype(jnp.float32), depth_pair, factor)

    spectra_in = to_modes(inputs, 1.0 / math.sqrt(total_cells))
    mixed = mix_modes(spectra_in, weight_blocks)
    spectral_out = to_space(mixed, 1.0 / math.sqrt(kept_total))
    pointwise = jnp.einsum(
        "xycs,co->xyos", inputs, point_weight, preferred_element_type=jnp.float32
    )
    before = spectral_out + pointwise
    unused_out, pullback = jax.vjp(exact_gelu, before)
    slope = settle(pullback(cotangent.astype(jnp.float32))[0])
    spectra_back = to_modes(slope, 1.0 / math.sqrt(kept_total))
    grad_spectral = weight_grad(spectra_in, spectra_back).reshape(mode_rows, mode_cols, flat_width)
    adjoint = adjoint_modes(spectra_back, weight_blocks)
    spectral_grad = to_space(adjoint, 1.0 / math.sqrt(total_cells))
    pointwise_grad = jnp.einsum(
        "xyos,co->xycs", slope, point_weight, preferred_element_type=jnp.float32
    )
    grad_input = (pointwise_grad + spectral_grad).astype(jnp.bfloat16)
    return (grad_input, grad_spectral)


def solution(mesh):
    placed = (
        P("gx", "gy", None, None),
        P("gx", "gy", None, None),
        P(),
        P(("gx", "gy"), None, None),
    )
    return jax.shard_map(
        per_device,
        mesh=mesh,
        in_specs=placed,
        out_specs=(P("gx", "gy", None, None), P(("gx", "gy"), None, None)),
        check_vma=False,
    )
```

profile of v0, /device:TPU:0, one launch (start us, length us, event | category | flops | bytes accessed | tf_op | source)
XLA Modules:
  0.0 453.2 jit_solution(6818993007358127799)
XLA Ops:
  7.4 12.3 %add_sine_fusion = (f32[64,8,12,8]{1,0,3,2:T(8,128)}, f32[64,8,12,8]{1,0,3,2:T(8,128)S(1)}) fusion(f32[8,8]{0,1:T(8,128)S(1)} %fusion.94, f32[64,12]{0,1:T(8,128)S(1)} %fusion.75), kind=kLoop, calls=%fused_computation.19 | loop fusion | flops 49152 | bytes 396544 | tf_op jit(solution)/shard_map/sin | solution.py:34
  19.8 3.9 reshape.129
  23.7 2.8 reshape.128
  31.4 1.6 copy.73
  33.1 31.4 %reduce-scatter.3.cloned.1.call-done = bf16[24,24,2,64]{3,1,2,0:T(8,128)(2,1)} async-done(((bf16[96,24,2,64]{3,1,2,0:T(8,128)(2,1)}), bf16[24,24,2,64]{3,1,2,0:T(8,128)(2,1)}) %reduce-scatter.3.cloned.1.call-update) | async-done | bytes 147472 | tf_op jit(solution)/shard_map/reduce_scatter | solution.py:131
  66.7 4.6 %all-to-all-start = ((bf16[8,2,4608]{2,1,0:T(2,128)(2,1)}), bf16[8,2,4608]{2,1,0:T(2,128)(2,1)S(1)}, u32[]{:S(2)}, u32[]{:S(2)}) async-start(bf16[8,2,4608]{2,1,0:T(2,128)(2,1)} %reshape.154), calls=%async_computation.1 | async-start | bytes 294912 | tf_op jit(solution)/shard_map/all_to_all | solution.py:140
  71.5 20.8 %reshape.123 = bf16[72,24,32,64]{3,2,1,0:T(8,128)(2,1)} reshape(bf16[72,24,2048]{2,1,0:T(8,128)(2,1)} %param.7) | data formatting | bytes 14155776 | tf_op jit(solution)/shard_map/reshape | solution.py:116
  95.0 34.3 %fusion.2 = (f32[72,24,32]{2,1,0:T(8,128)}, f32[72,24,32]{2,1,0:T(8,128)}, f32[72,24,32]{2,1,0:T(8,128)}, f32[72,24,32]{2,1,0:T(8,128)S(1)}) fusion(f32[72,24,32]{2,1,0:T(8,128)S(1)} %copy.146, bf16[72,24,32,64]{3,2,1,0:T(8,128)(2,1)} %reshape.123, f32[72,24,32]{2,1,0:T(8,128)S(1)} %copy.145), kind=kLoop, calls=%fused_computation.10 | loop fusion | flops 17473536 | bytes 8404992
  129.3 2.3 copy.111
  131.6 2.2 copy.119
  133.8 2.2 copy.115
  140.8 14.6 %all_to_all.66 = bf16[72,16,64]{0,2,1:T(8,128)(2,1)S(1)} all-to-all(bf16[72,16,64]{0,2,1:T(8,128)(2,1)S(1)} %copy.78), channel_id=1, replica_groups=mesh['gx'=4,'gy'=8] {'gy'}, dimensions={1} | all-to-all | bytes 294912 | tf_op jit(solution)/shard_map/all_to_all | solution.py:145
  157.7 38.3 %all_gather.6 = bf16[96,24,2,64]{1,0,3,2:T(8,128)(2,1)S(1)} all-gather(bf16[24,24,2,64]{1,0,3,2:T(8,128)(2,1)S(1)} %copy.80), channel_id=1, replica_groups=mesh['gx'=4,'gy'=8] {'gx'}, dimensions={0}, use_global_device_ids=true | all-gather | bytes 737280 | tf_op jit(solution)/shard_map/all_gather | solution.py:150
  196.0 5.8 %convolution_bitcast_fusion.16 = f32[96,4,2,64]{0,1,3,2:T(4,128)S(1)} fusion(bf16[96,24,2,64]{1,0,3,2:T(8,128)(2,1)S(1)} %all_gather.6, s32[24]{0:T(128)S(1)} %compare_select_fusion.2, s32[4]{0:T(128)S(1)} %iota_add_fusion), kind=kOutput, calls=%fused_computation.44 | convolution fusion | flops 14157120 | bytes 786544 | tf_op jit(solution)/shard_map/rkyc,xk->rxyc/dot_general | solution.py:44
  201.8 5.8 %convolution_bitcast_fusion.17 = f32[96,4,2,64]{0,1,3,2:T(4,128)S(1)} fusion(bf16[96,24,2,64]{1,0,3,2:T(8,128)(2,1)S(1)} %all_gather.6, s32[24]{0:T(128)S(1)} %compare_select_fusion.2, s32[4]{0:T(128)S(1)} %iota_add_fusion), kind=kOutput, calls=%fused_computation.45 | convolution fusion | flops 14157120 | bytes 786544 | tf_op jit(solution)/shard_map/rkyc,xk->rxyc/dot_general | solution.py:43
  208.8 2.4 fusion.22
  214.3 1.7 copy.86
  216.0 27.9 %reduce-scatter.5.cloned.1.call-done = bf16[24,24,2,64]{3,1,2,0:T(8,128)(2,1)} async-done(((bf16[96,24,2,64]{3,1,2,0:T(8,128)(2,1)}), bf16[24,24,2,64]{3,1,2,0:T(8,128)(2,1)}) %reduce-scatter.5.cloned.1.call-update) | async-done | bytes 147472 | tf_op jit(solution)/shard_map/reduce_scatter | solution.py:131
  245.4 11.6 %all_to_all.67 = bf16[8,2,4608]{2,1,0:T(2,128)(2,1)S(1)} all-to-all(bf16[8,2,4608]{2,1,0:T(2,128)(2,1)S(1)} %reshape.156), channel_id=1, replica_groups=mesh['gx'=4,'gy'=8] {'gy'}, dimensions={0} | all-to-all | bytes 294912 | tf_op jit(solution)/shard_map/all_to_all | solution.py:140
  261.2 2.3 copy.148
  263.4 38.7 %fusion.6 = (f32[72,24,32]{2,1,0:T(8,128)}, f32[72,24,32]{2,1,0:T(8,128)}, f32[72,24,32]{2,1,0:T(8,128)}, f32[72,24,32]{2,1,0:T(8,128)}) fusion(f32[72,24,32]{2,1,0:T(8,128)} %copy.148, bf16[72,24,32,64]{3,2,1,0:T(8,128)(2,1)} %reshape.123, f32[72,24,32]{2,1,0:T(8,128)S(1)} %copy.147), kind=kLoop, calls=%fused_computation.14 | loop fusion | flops 17473536 | bytes 8404992
  302.1 2.2 copy.131
  304.3 2.2 copy.136
  306.5 2.2 copy.141
  308.7 2.2 copy.126
  314.5 20.0 %multiply_add_fusion = (f32[72,24,32,32]{3,2,1,0:T(8,128)}, f32[72,24,32,32]{3,2,1,0:T(8,128)}) fusion(f32[72,24,32]{2,1,0:T(8,128)S(1)} %copy.146, f32[72,24,32]{2,1,0:T(8,128)S(1)} %copy.145, f32[72,24,32]{2,1,0:T(8,128)} %copy.148, f32[72,24,32]{2,1,0:T(8,128)S(1)} %copy.147), kind=kLoop, calls=%fused_computation.18 | loop fusion | flops 10616832 | bytes 15040512 | tf_op jit(solution)/shard_map/add | solution.py:104
  335.4 3.6 all-to-all-start.3
  339.0 28.5 %pad_maximum_fusion = f32[72,24,32,64]{3,2,1,0:T(8,128)} fusion(f32[72,24,32,32]{3,2,1,0:T(8,128)} %get-tuple-element.15, f32[72,24,32,32]{3,2,1,0:T(8,128)} %get-tuple-element.14), kind=kLoop, calls=%fused_computation.16 | loop fusion | flops 3538944 | bytes 28311552 | tf_op jit(solution)/shard_map/concatenate | solution.py:106
  367.5 24.3 %reshape.127 = f32[72,24,2048]{2,1,0:T(8,128)} reshape(f32[72,24,32,64]{3,2,1,0:T(8,128)} %pad_maximum_fusion) | data formatting | bytes 28311552 | tf_op jit(solution)/shard_map/reshape | solution.py:169
  392.5 40.0 %all_gather.7 = bf16[96,24,2,64]{1,0,3,2:T(8,128)(2,1)S(1)} all-gather(bf16[24,24,2,64]{1,0,3,2:T(8,128)(2,1)S(1)} %copy.93), channel_id=1, replica_groups=mesh['gx'=4,'gy'=8] {'gx'}, dimensions={0}, use_global_device_ids=true | all-gather | bytes 737280 | tf_op jit(solution)/shard_map/all_gather | solution.py:150
  432.5 5.8 %convolution_bitcast_fusion.14 = f32[96,4,2,64]{0,1,3,2:T(4,128)S(1)} fusion(bf16[96,24,2,64]{1,0,3,2:T(8,128)(2,1)S(1)} %all_gather.7, s32[24]{0:T(128)S(1)} %compare_select_fusion.2, s32[4]{0:T(128)S(1)} %iota_add_fusion), kind=kOutput, calls=%fused_computation.42 | convolution fusion | flops 14157120 | bytes 786544 | tf_op jit(solution)/shard_map/rkyc,xk->rxyc/dot_general | solution.py:44
  438.3 5.8 %convolution_bitcast_fusion.15 = f32[96,4,2,64]{0,1,3,2:T(4,128)S(1)} fusion(bf16[96,24,2,64]{1,0,3,2:T(8,128)(2,1)S(1)} %all_gather.7, s32[24]{0:T(128)S(1)} %compare_select_fusion.2, s32[4]{0:T(128)S(1)} %iota_add_fusion), kind=kOutput, calls=%fused_computation.43 | convolution fusion | flops 14157120 | bytes 786544 | tf_op jit(solution)/shard_map/rkyc,xk->rxyc/dot_general | solution.py:43
  (91 shorter events, 34.0 us)
Async XLA Ops:
  7.2 19.3 %copy-start = (bf16[4,2,32,512]{3,2,1,0:T(8,128)(2,1)S(1)}, bf16[4,2,32,512]{3,2,1,0:T(8,128)(2,1)}, u32[]{:S(2)}) copy-start(bf16[4,2,32,512]{3,2,1,0:T(8,128)(2,1)} %param.4) | copy-start | bytes 786436
  7.2 57.3 %reduce-scatter.3.cloned.1.call-start = ((), (), s32[]{:S(2)}) async-start(), calls=%async_computation.6 | async-start | bytes 1474560 | tf_op jit(solution)/shard_map/reduce_scatter | solution.py:131
  66.7 25.7 %all-to-all-start = ((bf16[8,2,4608]{2,1,0:T(2,128)(2,1)}), bf16[8,2,4608]{2,1,0:T(2,128)(2,1)S(1)}, u32[]{:S(2)}, u32[]{:S(2)}) async-start(bf16[8,2,4608]{2,1,0:T(2,128)(2,1)} %reshape.154), calls=%async_computation.1 | async-start | bytes 294912 | tf_op jit(solution)/shard_map/all_to_all | solution.py:140
  71.3 172.7 %reduce-scatter.5.cloned.1.call-start = ((), (), s32[]{:S(2)}) async-start(), calls=%async_computation.7 | async-start | bytes 1474560 | tf_op jit(solution)/shard_map/reduce_scatter | solution.py:131
  129.3 78.6 %copy-start.3 = (f32[512,96,1,1]{0,1,2,3:T(8,128)S(1)}, f32[512,96,1,1]{0,1,2,3:T(8,128)}, u32[]{:S(2)}) copy-start(f32[512,96,1,1]{0,1,2,3:T(8,128)} %reshape.128) | copy-start | bytes 589828
  129.3 79.0 %copy-start.2 = (f32[512,96,1,1]{0,1,2,3:T(8,128)S(1)}, f32[512,96,1,1]{0,1,2,3:T(8,128)}, u32[]{:S(2)}) copy-start(f32[512,96,1,1]{0,1,2,3:T(8,128)} %reshape.129) | copy-start | bytes 589828
  129.3 79.4 %copy-start.6 = (bf16[32,32]{1,0:T(8,128)(2,1)S(1)}, bf16[32,32]{1,0:T(8,128)(2,1)}, u32[]{:S(2)}) copy-start(bf16[32,32]{1,0:T(8,128)(2,1)} %param.6) | copy-start | bytes 6148
  211.2 3.0 copy-start.4
  335.4 56.5 %all-to-all-start.3 = ((bf16[72,16,64]{0,2,1:T(8,128)(2,1)}), bf16[72,16,64]{0,2,1:T(8,128)(2,1)S(1)}, u32[]{:S(2)}, u32[]{:S(2)}) async-start(bf16[72,16,64]{0,2,1:T(8,128)(2,1)} %copy.91), calls=%async_computation.5 | async-start | bytes 524288 | tf_op jit(solution)/shard_map/all_to_all | solution.py:145
  367.5 78.6 %copy-start.1 = (bf16[4,2,32,512]{3,2,1,0:T(8,128)(2,1)S(1)}, bf16[4,2,32,512]{3,2,1,0:T(8,128)(2,1)}, u32[]{:S(2)}) copy-start(bf16[4,2,32,512]{3,2,1,0:T(8,128)(2,1)} %param.4) | copy-start | bytes 786436
  391.9 53.4 %copy-start.5 = (bf16[4,2,32,512]{3,2,1,0:T(8,128)(2,1)S(1)}, bf16[4,2,32,512]{3,2,1,0:T(8,128)(2,1)}, u32[]{:S(2)}) copy-start(bf16[4,2,32,512]{3,2,1,0:T(8,128)(2,1)} %copy-done.4) | copy-start | bytes 786436
Sparse Core Ops, SparseCore 0:
  33.2 31.2 reduce-scatter.2
  216.1 27.7 reduce-scatter.4
where the time goes:
time: 462 us; the launch traced here: 453 us
  other arithmetic  141 us (31%)
  blocking collectives  104 us (23%)
  local copies, waits for them, and re-layouts  84.9 us (18%)
  waiting for transfers between devices  59.4 us (13%)
  matrix products  40.2 us (9%)
  between operations  14.8 us (3%)
  starting transfers between devices  8.51 us (2%)
    all_gather x2, blocking collectives, to_space(): lax.all_gather(returned, 'gx', axis=0, tiled=True).astype(jnp.float32)  78.3 us
    unnamed x2, other arithmetic  73 us
    reduce_scatter x2, waiting for transfers between devices, to_modes(): lax.psum_scatter(rotate(depth_spec.astype(jnp.float32), local_x[0], local...  59.3 us
    concatenate x1, other arithmetic, weight_grad(): return jnp.concatenate([real_part, imag_part], -1)  28.5 us
    reshape x1, local copies, waits for them, and re-layouts, per_device(): weight_grad(spectra_in, spectra_back)  24.3 us
    reshape x1, local copies, waits for them, and re-layouts, per_device(): spectral_weight.reshape(mode_rows, mode_cols, channels, 2 * channels)  20.8 us
    add x1, other arithmetic, weight_grad(): partial_outer(real_in, real_back) + partial_outer(imag_in, imag_back)  20 us
    dot_general x8, matrix products, rotate(): jnp.einsum(pattern, spectra, cosine_table, precision=lax.Precision.HIGHEST)  16 us
  transfers between devices with their start and end apart: 4, of which 2 were waited for; matrix products, arithmetic and copies ran while one was open for 16% of the time, Pallas kernels for 0%

commit v1 on v0

--- a/solution.py
+++ b/solution.py
@@ -1,8 +1,12 @@
+import functools
 import math
 
 import jax
 import jax.numpy as jnp
+import numpy as np
 from jax import lax
+from jax.experimental import pallas as pl
+from jax.experimental.pallas import tpu as pltpu
 from jax.sharding import PartitionSpec as P
 
 NZ = 64
@@ -11,6 +15,347 @@
 KY = 24
 KZ = 12
 KT = 8
+SLOTS = 8
+GRID_AXES = ("gx", "gy")
+VMEM_BYTES = 56 * 1024 * 1024
+
+
+def table_angles(positions, kept_count, length):
+    index = np.arange(kept_count)
+    frequency = np.where(index < kept_count // 2, index, index - kept_count)
+    turns = (np.asarray(positions)[:, None] * frequency[None, :]) % length
+    return 2.0 * np.pi * turns / length
+
+
+def depth_table(share):
+    angles = (
+        table_angles(np.arange(NZ), KZ, NZ)[:, None, :, None]
+        + table_angles(np.arange(NT), KT, NT)[None, :, None, :]
+    ).reshape(NZ * NT, KZ * KT)
+    parts = np.stack([np.cos(angles), -np.sin(angles)], -1)
+    owners = KZ * KT // share
+    rows = np.zeros((owners, SLOTS, NZ * NT))
+    rows[:, : 2 * share] = parts.reshape(NZ * NT, owners, 2 * share).transpose(1, 2, 0)
+    return rows.reshape(owners * SLOTS, NZ * NT).astype(jnp.bfloat16)
+
+
+def plane_tables(count_gx, count_gy, rows_x, rows_y):
+    length_x, length_y = count_gx * rows_x, count_gy * rows_y
+    angle_x = table_angles(np.arange(length_x), KX, length_x).T.reshape(KX, 1, count_gx, 1, rows_x, 1)
+    angle_y = table_angles(np.arange(length_y), KY, length_y).T.reshape(1, KY, 1, count_gy, 1, rows_y)
+    angles = (angle_x + angle_y).transpose(0, 1, 4, 5, 2, 3).reshape(KX * KY, length_x * length_y)
+    forward = np.concatenate([np.cos(angles), np.sin(angles)], 1)
+    inverse = np.concatenate([np.cos(angles.T), np.sin(angles.T)], 1)
+    return forward.astype(jnp.bfloat16), inverse.astype(jnp.bfloat16)
+
+
+def dot(left, right, left_dim=1, right_dim=0):
+    return lax.dot_general(
+        left, right, (((left_dim,), (right_dim,)), ((), ())), preferred_element_type=jnp.float32
+    )
+
+
+def depth_kernel(factor, table_ref, field_ref, sent_ref):
+    spectra = dot(table_ref[...], field_ref[...], 1, 1)
+    sent_ref[...] = (spectra * factor).astype(jnp.bfloat16)
+
+
+def gather_cells(mode, wide_ref, channels):
+    halves, rows, lanes = wide_ref.shape
+    devices = rows // SLOTS
+    parts = []
+    for part in range(2):
+        pieces = []
+        for h in range(halves):
+            piece = wide_ref[h, pl.ds(mode * 2 + part, devices, stride=SLOTS), :]
+            pieces += [piece[:, c * channels : (c + 1) * channels] for c in range(lanes // channels)]
+        parts.append(jnp.concatenate(pieces, 0))
+    return parts
+
+
+def scatter_cells(mode, spectra, out_ref, channels):
+    halves, rows, lanes = out_ref.shape
+    devices = rows // SLOTS
+    each = lanes // channels
+    for part in range(2):
+        columns = slice(part * channels, (part + 1) * channels)
+        for h in range(halves):
+            pieces = [spectra[c * devices : (c + 1) * devices, columns] for c in range(h * each, (h + 1) * each)]
+            out_ref[h, pl.ds(mode * 2 + part, devices, stride=SLOTS), :] = jnp.concatenate(pieces, 1)
+
+
+def spread_matrix(channels):
+    wide = 2 * channels
+    row = lax.broadcasted_iota(jnp.int32, (wide, wide * wide), 0)
+    column = lax.broadcasted_iota(jnp.int32, (wide, wide * wide), 1)
+    return jnp.where(column // wide == row, 1.0, 0.0).astype(jnp.bfloat16)
+
+
+def mix_kernel(
+    channels, arrived_ref, weight_ref, forward_ref, inverse_ref, sent_ref, kept_ref,
+    wide_ref, plane_ref, modes_ref, pair_ref, spread_ref, out_ref,
+):
+    mode, block = pl.program_id(0), pl.program_id(1)
+    rows_x, rows_y, flat = weight_ref.shape
+    block_rows = rows_x * rows_y
+    plane = modes_ref.shape[0]
+    tiles = flat // 128
+
+    @pl.when((mode == 0) & (block == 0))
+    def _():
+        for h in range(wide_ref.shape[0]):
+            wide_ref[h] = arrived_ref[:, h * 128 : (h + 1) * 128].astype(jnp.float32)
+        out_ref[...] = jnp.zeros_like(out_ref)
+        spread_ref[...] = spread_matrix(channels)
+
+    @pl.when(block == 0)
+    def _():
+        real, imag = gather_cells(mode, wide_ref, channels)
+        half = real.shape[0]
+        plane_ref[:half, :] = jnp.concatenate([real, imag], 1).astype(jnp.bfloat16)
+        plane_ref[half:, :] = jnp.concatenate([imag, -real], 1).astype(jnp.bfloat16)
+        modes_ref[...] = dot(forward_ref[...], plane_ref[...])
+        kept_ref[...] = modes_ref[...].astype(jnp.bfloat16)
+
+    for r in range(rows_x):
+        start = block * block_rows + r * rows_y
+        start = pl.multiple_of(start, 8)
+        entries = modes_ref[pl.ds(start, rows_y), :].astype(jnp.bfloat16)
+        spread = dot(entries, spread_ref[...])
+        weight = weight_ref[r].astype(jnp.float32)
+        by_real = jnp.zeros((rows_y, 128), jnp.float32)
+        by_imag = jnp.zeros((rows_y, 128), jnp.float32)
+        for t in range(tiles):
+            tile = weight[:, t * 128 : (t + 1) * 128]
+            by_real += spread[:, t * 128 : (t + 1) * 128] * tile
+            by_imag += spread[:, flat + t * 128 : flat + (t + 1) * 128] * tile
+        pair_ref[pl.ds(start, rows_y), :] = jnp.concatenate([by_real, by_imag], 1)
+        pair_ref[pl.ds(plane + start, rows_y), :] = jnp.concatenate([-by_imag, by_real], 1)
+
+    @pl.when(block == pl.num_programs(1) - 1)
+    def _():
+        total = dot(inverse_ref[...], pair_ref[...].astype(jnp.bfloat16))
+        first, second = total[:, :128], total[:, 128:]
+        first = first[:, :64] + first[:, 64:]
+        second = second[:, :64] + second[:, 64:]
+        turned = jnp.concatenate([-second[:, channels:], second[:, :channels]], 1)
+        scatter_cells(mode, first + turned, out_ref, channels)
+
+    @pl.when((mode == pl.num_programs(0) - 1) & (block == pl.num_programs(1) - 1))
+    def _():
+        for h in range(out_ref.shape[0]):
+            sent_ref[:, h * 128 : (h + 1) * 128] = out_ref[h].astype(jnp.bfloat16)
+
+
+def adjoint_kernel(
+    channels, arrived_ref, weight_ref, forward_ref, inverse_ref, sent_ref, kept_ref,
+    wide_ref, plane_ref, modes_ref, pair_ref, sum_ref, product_ref, out_ref,
+):
+    mode, block = pl.program_id(0), pl.program_id(1)
+    rows_x, rows_y, flat = weight_ref.shape
+    block_rows = rows_x * rows_y
+    plane = modes_ref.shape[0]
+    tiles = flat // 128
+    wide = 2 * channels
+
+    @pl.when((mode == 0) & (block == 0))
+    def _():
+        for h in range(wide_ref.shape[0]):
+            wide_ref[h] = arrived_ref[:, h * 128 : (h + 1) * 128].astype(jnp.float32)
+        out_ref[...] = jnp.zeros_like(out_ref)
+        row = lax.broadcasted_iota(jnp.int32, (2 * flat, 2 * wide), 0)
+        column = lax.broadcasted_iota(jnp.int32, (2 * flat, 2 * wide), 1)
+        own = (row % flat) // wide == column % channels
+        slot = column // channels
+        real = jnp.where(own & ((slot == 0) | (slot == 3)), 1.0, 0.0)
+        imag = jnp.where(own & (slot == 1), 1.0, jnp.where(own & (slot == 2), -1.0, 0.0))
+        sum_ref[...] = jnp.where(row < flat, real, imag).astype(jnp.bfloat16)
+
+    @pl.when(block == 0)
+    def _():
+        real, imag = gather_cells(mode, wide_ref, channels)
+        half = real.shape[0]
+        once = jnp.concatenate([real, imag], 1)
+        turn = jnp.concatenate([imag, -real], 1)
+        plane_ref[:half, :] = jnp.concatenate([once, once, turn, turn], 1).astype(jnp.bfloat16)
+        plane_ref[half:, :] = jnp.concatenate([turn, turn, -once, -once], 1).astype(jnp.bfloat16)
+        modes_ref[...] = dot(forward_ref[...], plane_ref[...])
+        kept_ref[...] = modes_ref[...].astype(jnp.bfloat16)
+
+    for r in range(rows_x):
+        start = block * block_rows + r * rows_y
+        start = pl.multiple_of(start, 8)
+        entries = modes_ref[pl.ds(start, rows_y), :].astype(jnp.bfloat16)
+        here, turned = entries[:, :128], entries[:, 128:]
+        weight = weight_ref[r]
+        for t in range(tiles):
+            tile = weight[:, t * 128 : (t + 1) * 128]
+            product_ref[:, t * 128 : (t + 1) * 128] = here * tile
+            product_ref[:, flat + t * 128 : flat + (t + 1) * 128] = turned * tile
+        summed = dot(product_ref[...], sum_ref[...])
+        pair_ref[pl.ds(start, rows_y), :] = summed[:, :wide]
+        pair_ref[pl.ds(plane + start, rows_y), :] = summed[:, wide:]
+
+    @pl.when(block == pl.num_programs(1) - 1)
+    def _():
+        total = dot(inverse_ref[...], pair_ref[...].astype(jnp.bfloat16))
+        scatter_cells(mode, total, out_ref, channels)
+
+    @pl.when((mode == pl.num_programs(0) - 1) & (block == pl.num_programs(1) - 1))
+    def _():
+        for h in range(out_ref.shape[0]):
+            sent_ref[:, h * 128 : (h + 1) * 128] = out_ref[h].astype(jnp.bfloat16)
+
+
+def outer_kernel(channels, in_ref, back_ref, grad_ref, spread_ref):
+    rows_x, rows_y, flat = grad_ref.shape
+    tiles = flat // 128
+
+    @pl.when(pl.program_id(0) == 0)
+    def _():
+        spread_ref[...] = spread_matrix(channels)
+
+    for r in range(rows_x):
+        entries = in_ref[r * rows_y : (r + 1) * rows_y, :]
+        back = back_ref[r * rows_y : (r + 1) * rows_y, :].astype(jnp.float32)
+        here, turned = back[:, :128], back[:, 128:]
+        spread = dot(entries, spread_ref[...])
+        for t in range(tiles):
+            grad_ref[r, :, t * 128 : (t + 1) * 128] = (
+                spread[:, t * 128 : (t + 1) * 128] * here
+                + spread[:, flat + t * 128 : flat + (t + 1) * 128] * turned
+            )
+
+
+def slope_kernel(
+    cells, channels, factor, arrived_ref, table_ref, field_ref, cotangent_ref, point_ref, slope_ref, sent_ref
+):
+    spectral = dot(arrived_ref[...], table_ref[...], 0, 0)
+    for c in range(cells):
+        rows = slice(c * channels, (c + 1) * channels)
+        before = spectral[rows] * factor + dot(point_ref[...], field_ref[rows, :], 0, 0)
+        cumulative = 0.5 + 0.5 * lax.erf(before * math.sqrt(0.5))
+        density = jnp.exp(-0.5 * before * before) * (1.0 / math.sqrt(2.0 * math.pi))
+        slope = cotangent_ref[rows, :].astype(jnp.float32) * (cumulative + before * density)
+        slope_ref[rows, :] = slope.astype(jnp.bfloat16)
+    sent = dot(table_ref[...], slope_ref[...], 1, 1)
+    sent_ref[...] = (sent * factor).astype(jnp.bfloat16)
+
+
+def final_kernel(cells, channels, factor, arrived_ref, table_ref, slope_ref, point_ref, grad_ref):
+    spectral = dot(arrived_ref[...], table_ref[...], 0, 0)
+    for c in range(cells):
+        rows = slice(c * channels, (c + 1) * channels)
+        pointwise = dot(point_ref[...], slope_ref[rows, :])
+        grad_ref[rows, :] = (pointwise + spectral[rows] * factor).astype(jnp.bfloat16)
+
+
+def params(semantics=None):
+    return pltpu.CompilerParams(dimension_semantics=semantics, vmem_limit_bytes=VMEM_BYTES)
+
+
+def shape(dims, dtype=jnp.bfloat16):
+    return jax.ShapeDtypeStruct(dims, dtype)
+
+
+def per_device(inputs, cotangent, point_weight, spectral_weight):
+    rows_x, rows_y, channels, depth = inputs.shape
+    mode_rows, mode_cols, flat = spectral_weight.shape
+    count_gx, count_gy = lax.axis_size("gx"), lax.axis_size("gy")
+    devices = count_gx * count_gy
+    share = mode_rows // KX
+    cells = rows_x * rows_y
+    lanes = cells * channels
+    wide = 2 * channels
+    plane = KX * KY
+    points = cells * devices
+    slots = devices * SLOTS
+    inner = 1.0 / math.sqrt(points * depth)
+    outer = 1.0 / math.sqrt(plane * KZ * KT)
+
+    table = jnp.asarray(depth_table(share))
+    forward, inverse = (jnp.asarray(t) for t in plane_tables(count_gx, count_gy, rows_x, rows_y))
+    field = inputs.reshape(lanes, depth)
+    seed = cotangent.reshape(lanes, depth)
+
+    def exchange(sent):
+        blocks = sent.reshape(devices, SLOTS, lanes)
+        return lax.all_to_all(blocks, GRID_AXES, split_axis=0, concat_axis=0, tiled=True).reshape(slots, lanes)
+
+    steps = 2
+    block_x = KX // steps
+    whole = lambda dims: pl.BlockSpec(dims, lambda k, b: (0,) * len(dims))
+    weight_spec = pl.BlockSpec((block_x, mode_cols, flat), lambda k, b: (k * steps + b, 0, 0))
+
+    sent = pl.pallas_call(
+        functools.partial(depth_kernel, inner), out_shape=shape((slots, lanes)), compiler_params=params(),
+        name="depth",
+    )(table, field)
+    arrived = exchange(sent)
+    sent, kept_in = pl.pallas_call(
+        functools.partial(mix_kernel, channels),
+        grid=(share, steps),
+        in_specs=[whole((slots, lanes)), weight_spec, whole((plane, 2 * points)), whole((points, 2 * plane))],
+        out_specs=[whole((slots, lanes)), pl.BlockSpec((plane, wide), lambda k, b: (k, 0))],
+        out_shape=[shape((slots, lanes)), shape((share * plane, wide))],
+        scratch_shapes=[
+            pltpu.VMEM((lanes // 128, slots, 128), jnp.float32),
+            pltpu.VMEM((2 * points, wide), jnp.bfloat16),
+            pltpu.VMEM((plane, wide), jnp.float32),
+            pltpu.VMEM((2 * plane, 256), jnp.float32),
+            pltpu.VMEM((wide, wide * wide), jnp.bfloat16),
+            pltpu.VMEM((lanes // 128, slots, 128), jnp.float32),
+        ],
+        compiler_params=params(("arbitrary", "arbitrary")),
+        name="mix",
+    )(arrived, spectral_weight, forward, inverse)
+    arrived = exchange(sent)
+    slope, sent = pl.pallas_call(
+        functools.partial(slope_kernel, cells, channels, outer),
+        out_shape=[shape((lanes, depth)), shape((slots, lanes))], compiler_params=params(),
+        name="slope",
+    )(arrived, table, field, seed, point_weight)
+    arrived = exchange(sent)
+    sent, kept_back = pl.pallas_call(
+        functools.partial(adjoint_kernel, channels),
+        grid=(share, steps),
+        in_specs=[whole((slots, lanes)), weight_spec, whole((plane, 2 * points)), whole((points, 2 * plane))],
+        out_specs=[whole((slots, lanes)), pl.BlockSpec((plane, 256), lambda k, b: (k, 0))],
+        out_shape=[shape((slots, lanes)), shape((share * plane, 256))],
+        scratch_shapes=[
+            pltpu.VMEM((lanes // 128, slots, 128), jnp.float32),
+            pltpu.VMEM((2 * points, 256), jnp.bfloat16),
+            pltpu.VMEM((plane, 256), jnp.float32),
+            pltpu.VMEM((2 * plane, wide), jnp.float32),
+            pltpu.VMEM((2 * flat, 2 * wide), jnp.bfloat16),
+            pltpu.VMEM((mode_cols, 2 * flat), jnp.bfloat16),
+            pltpu.VMEM((lanes // 128, slots, 128), jnp.float32),
+        ],
+        compiler_params=params(("arbitrary", "arbitrary")),
+        name="adjoint",
+    )(arrived, spectral_weight, forward, inverse)
+    arrived = exchange(sent)
+    grad_x = 6
+    grad_spectral = pl.pallas_call(
+        functools.partial(outer_kernel, channels),
+        grid=(mode_rows // grad_x,),
+        in_specs=[
+            pl.BlockSpec((grad_x * mode_cols, wide), lambda i: (i, 0)),
+            pl.BlockSpec((grad_x * mode_cols, 256), lambda i: (i, 0)),
+        ],
+        out_specs=pl.BlockSpec((grad_x, mode_cols, flat), lambda i: (i, 0, 0)),
+        out_shape=shape((mode_rows, mode_cols, flat), jnp.float32),
+        scratch_shapes=[pltpu.VMEM((wide, wide * wide), jnp.bfloat16)],
+        compiler_params=params(("arbitrary",)),
+        cost_estimate=pl.CostEstimate(flops=2 * mode_rows * mode_cols * flat * wide * 2, transcendentals=0,
+                                      bytes_accessed=mode_rows * mode_cols * flat * 4),
+        name="outer",
+    )(kept_in, kept_back)
+    grad_input = pl.pallas_call(
+        functools.partial(final_kernel, cells, channels, inner), out_shape=shape((lanes, depth)),
+        compiler_params=params(), name="final",
+    )(arrived, table, slope, point_weight)
+    return grad_input.reshape(inputs.shape), grad_spectral
 
 
 def kept_angles(positions, kept_count, length):
@@ -110,7 +455,7 @@
     return jax.nn.gelu(values, approximate=False)
 
 
-def per_device(inputs, cotangent, point_weight, spectral_weight):
+def general_per_device(inputs, cotangent, point_weight, spectral_weight):
     rows_x, rows_y, channels, cells = inputs.shape
     mode_rows, mode_cols, flat_width = spectral_weight.shape
     weight_blocks = spectral_weight.reshape(mode_rows, mode_cols, channels, 2 * channels)
@@ -177,16 +522,25 @@
 
 
 def solution(mesh):
+    count_gx, count_gy = mesh.shape["gx"], mesh.shape["gy"]
     placed = (
         P("gx", "gy", None, None),
         P("gx", "gy", None, None),
         P(),
         P(("gx", "gy"), None, None),
     )
-    return jax.shard_map(
-        per_device,
-        mesh=mesh,
-        in_specs=placed,
-        out_specs=(P("gx", "gy", None, None), P(("gx", "gy"), None, None)),
-        check_vma=False,
-    )
+
+    def program(inputs, cotangent, point_weight, spectral_weight):
+        cells = inputs.shape[0] * inputs.shape[1] // (count_gx * count_gy)
+        whole_modes = KZ * KT % (count_gx * count_gy) == 0
+        fits = whole_modes and 2 * KZ * KT // (count_gx * count_gy) <= SLOTS
+        fits = fits and inputs.shape[2] == 32 and cells * inputs.shape[2] == 256
+        return jax.shard_map(
+            per_device if fits else general_per_device,
+            mesh=mesh,
+            in_specs=placed,
+            out_specs=(P("gx", "gy", None, None), P(("gx", "gy"), None, None)),
+            check_vma=False,
+        )(inputs, cotangent, point_weight, spectral_weight)
+
+    return program

time: 462 us -> 92.3 us (0.20); the launches traced: 453 us -> 91.3 us
  other arithmetic: 141 us -> 0 us
  local copies, waits for them, and re-layouts: 84.9 us -> 0.64 us
  blocking collectives: 104 us -> 38.5 us
  waiting for transfers between devices: 59.4 us -> 0.01 us
  Pallas kernels: 0 us -> 49 us
  matrix products: 40.2 us -> 0 us
  between operations: 14.8 us -> 0.64 us
  starting transfers between devices: 8.51 us -> 2.58 us
    all_gather x2 -> x0, blocking collectives: 78.3 us -> none  [to_space(): lax.all_gather(returned, 'gx', axis=0, tiled=True).astype(jnp.float32)]
    unnamed x2 -> x0, other arithmetic: 73 us -> none
    reduce_scatter x2 -> x0, waiting for transfers between devices: 59.3 us -> none  [to_modes(): lax.psum_scatter(rotate(depth_spec.astype(jnp.float32), local_x[0], local...]
    pallas_call x0 -> x6, Pallas kernels: none -> 49 us  [the longest x1 18.6 us: per_device(): pl.pallas_call(functools.partial(adjoint_kernel, channels), grid=(share,...]
    reshape x6 -> x0, local copies, waits for them, and re-layouts: 47.6 us -> none  [the longest x1 24.3 us: per_device(): weight_grad(spectra_in, spectra_back)]
    dot_general x26 -> x0, matrix products: 40.2 us -> none  [the longest x8 16 us: rotate(): jnp.einsum(pattern, spectra, cosine_table, precision=lax.Precision.HIGHEST)]
    concatenate x7 -> x0, other arithmetic: 29.2 us -> none  [the longest x1 28.5 us: weight_grad(): return jnp.concatenate([real_part, imag_part], -1)]
    add x6 -> x0, other arithmetic: 23.3 us -> none  [the longest x1 20 us: weight_grad(): partial_outer(real_in, real_back) + partial_outer(imag_in, imag_back)]
  transfers between devices with their start and end apart: 4 -> 1, of which waited for: 2 -> 0; matrix products, arithmetic and copies ran while one was open for 16% -> 0% of each run, Pallas kernels for 0% -> 13%
where the time goes in v1:
time: 92.3 us; the launch traced here: 91.3 us
  Pallas kernels  49 us (53%)
  blocking collectives  38.5 us (42%)
  starting transfers between devices  2.58 us (3%)
    all_to_all x3, blocking collectives, exchange(): lax.all_to_all(blocks, GRID_AXES, split_axis=0, concat_axis=0, tiled=True)  38.5 us
    pallas_call x1, Pallas kernels, per_device(): pl.pallas_call(functools.partial(adjoint_kernel, channels), grid=(share,...  18.6 us
    pallas_call x1, Pallas kernels, per_device(): pl.pallas_call(functools.partial(outer_kernel, channels), grid=(mode_rows...  12 us
    pallas_call x1, Pallas kernels, per_device(): pl.pallas_call(functools.partial(mix_kernel, channels), grid=(share, step...  11.9 us
    all_to_all x1, starting transfers between devices, exchange(): lax.all_to_all(blocks, GRID_AXES, split_axis=0, concat_axis=0, tiled=True)  2.58 us
    pallas_call x1, Pallas kernels, per_device(): pl.pallas_call(functools.partial(slope_kernel, cells, channels, outer), o...  2.52 us
    pallas_call x1, Pallas kernels, per_device(): pl.pallas_call(functools.partial(final_kernel, cells, channels, inner), o...  2.12 us
    pallas_call x1, Pallas kernels, per_device(): pl.pallas_call(functools.partial(depth_kernel, inner), out_shape=shape((s...  1.95 us
  transfers between devices with their start and end apart: 1, of which 0 were waited for; matrix products, arithmetic and copies ran while one was open for 0% of the time, Pallas kernels for 13%

profile of v1, /device:TPU:0, one launch (start us, length us, event | category | flops | bytes accessed | tf_op | source)
XLA Modules:
  0.0 91.3 jit_solution(2440751546324780918)
XLA Ops:
  0.6 2.0 %depth.1 = bf16[256,256]{1,0:T(8,128)(2,1)} custom-call(bf16[256,512]{1,0:T(8,128)(2,1)} %constant.6.clone.table_ref, bf16[256,512]{1,0:T(8,128)(2,1)} %bitcast.11), custom_call_target="tpu_custom_call" | custom-call | tf_op jit(solution)/shard_map/depth/pallas_call | solution.py:290
  2.6 15.6 %all_to_all.20 = bf16[32,8,256]{2,1,0:T(8,128)(2,1)} all-to-all(bf16[32,8,256]{2,1,0:T(8,128)(2,1)} %bitcast.17), channel_id=1, replica_groups=mesh['gx'=4,'gy'=8] {'gx','gy'}, dimensions={0} | all-to-all | bytes 262144 | tf_op jit(solution)/shard_map/all_to_all | solution.py:283
  18.2 11.9 %mix.1 = (bf16[256,256]{1,0:T(8,128)(2,1)}, bf16[1728,64]{1,0:T(8,128)(2,1)}) custom-call(bf16[256,256]{1,0:T(8,128)(2,1)} %bitcast.14, bf16[72,24,2048]{2,1,0:T(8,128)(2,1)} %weight_ref.3, bf16[576,512]{1,0:T(8,128)(2,1)} %constant.7.clone.forward_ref, bf16[256,1152]{1,0:T(8,128)(2,1)} %constant.8.clone.inverse_ref), custom_call_target="tpu_custom_call" | custom-call | tf_op jit(solution)/shard_map/mix/pallas_call | solution.py:295
  30.0 11.4 %all_to_all.21 = bf16[32,8,256]{2,1,0:T(8,128)(2,1)} all-to-all(bf16[32,8,256]{2,1,0:T(8,128)(2,1)} %bitcast.21), channel_id=1, replica_groups=mesh['gx'=4,'gy'=8] {'gx','gy'}, dimensions={0} | all-to-all | bytes 262144 | tf_op jit(solution)/shard_map/all_to_all | solution.py:283
  41.5 2.5 %slope.1 = (bf16[256,512]{1,0:T(8,128)(2,1)}, bf16[256,256]{1,0:T(8,128)(2,1)}) custom-call(bf16[256,256]{1,0:T(8,128)(2,1)} %bitcast.16, bf16[256,512]{1,0:T(8,128)(2,1)} %constant.6.clone.table_ref, bf16[256,512]{1,0:T(8,128)(2,1)} %bitcast.12, bf16[256,512]{1,0:T(8,128)(2,1)} %bitcast.18, bf16[32,32]{1,0:T(8,128)(2,1)} %point_ref.3), custom_call_target="tpu_custom_call" | custom-call | tf_op jit(solution)/shard_map/slope/pallas_call | solution.py:313
  44.0 11.4 %all_to_all.22 = bf16[32,8,256]{2,1,0:T(8,128)(2,1)} all-to-all(bf16[32,8,256]{2,1,0:T(8,128)(2,1)} %bitcast.22), channel_id=1, replica_groups=mesh['gx'=4,'gy'=8] {'gx','gy'}, dimensions={0} | all-to-all | bytes 262144 | tf_op jit(solution)/shard_map/all_to_all | solution.py:283
  55.4 18.6 %adjoint.1 = (bf16[256,256]{1,0:T(8,128)(2,1)}, bf16[1728,256]{1,0:T(8,128)(2,1)}) custom-call(bf16[256,256]{1,0:T(8,128)(2,1)} %bitcast.13, bf16[72,24,2048]{2,1,0:T(8,128)(2,1)} %weight_ref.3, bf16[576,512]{1,0:T(8,128)(2,1)} %constant.7.clone.forward_ref, bf16[256,1152]{1,0:T(8,128)(2,1)} %constant.8.clone.inverse_ref), custom_call_target="tpu_custom_call" | custom-call | tf_op jit(solution)/shard_map/adjoint/pallas_call | solution.py:319
  74.0 2.6 %all-to-all-start.3 = ((bf16[32,8,256]{2,1,0:T(8,128)(2,1)}), bf16[32,8,256]{2,1,0:T(8,128)(2,1)S(1)}, u32[]{:S(2)}, u32[]{:S(2)}) async-start(bf16[32,8,256]{2,1,0:T(8,128)(2,1)} %bitcast.20), calls=%async_computation.3 | async-start | bytes 262144 | tf_op jit(solution)/shard_map/all_to_all | solution.py:283
  76.6 12.0 %outer.1 = f32[72,24,2048]{2,1,0:T(8,128)} custom-call(bf16[1728,64]{1,0:T(8,128)(2,1)} %get-tuple-element.12.in_ref, bf16[1728,256]{1,0:T(8,128)(2,1)} %get-tuple-element.13.back_ref), custom_call_target="tpu_custom_call" | custom-call | flops 905969664 | bytes 14155776 | tf_op jit(solution)/shard_map/outer/pallas_call | solution.py:339
  88.6 0.0 all-to-all-done.3
  88.6 0.0 copy-start
  88.6 0.6 copy-done
  89.2 2.1 %final.1 = bf16[256,512]{1,0:T(8,128)(2,1)} custom-call(bf16[256,256]{1,0:T(8,128)(2,1)} %bitcast.15, bf16[256,512]{1,0:T(8,128)(2,1)} %constant.6.clone.table_ref, bf16[256,512]{1,0:T(8,128)(2,1)} %get-tuple-element.11.slope_ref, bf16[32,32]{1,0:T(8,128)(2,1)} %point_ref.3), custom_call_target="tpu_custom_call" | custom-call | tf_op jit(solution)/shard_map/final/pallas_call | solution.py:354
Async XLA Ops:
  74.0 14.6 %all-to-all-start.3 = ((bf16[32,8,256]{2,1,0:T(8,128)(2,1)}), bf16[32,8,256]{2,1,0:T(8,128)(2,1)S(1)}, u32[]{:S(2)}, u32[]{:S(2)}) async-start(bf16[32,8,256]{2,1,0:T(8,128)(2,1)} %bitcast.20), calls=%async_computation.3 | async-start | bytes 262144 | tf_op jit(solution)/shard_map/all_to_all | solution.py:283
  88.6 0.6 copy-start

commit v2 on v0

--- a/solution.py
+++ b/solution.py
@@ -1,8 +1,12 @@
+import functools
 import math
 
 import jax
 import jax.numpy as jnp
+import numpy as np
 from jax import lax
+from jax.experimental import pallas as pl
+from jax.experimental.pallas import tpu as pltpu
 from jax.sharding import PartitionSpec as P
 
 NZ = 64
@@ -11,6 +15,335 @@
 KY = 24
 KZ = 12
 KT = 8
+SLOTS = 8
+LANES = 128
+GROUP = 4
+ROWS = 16
+READ_AHEAD_FLOPS = 10**11
+GRID_AXES = ("gx", "gy")
+
+
+def table_angles(positions, kept_count, length):
+    index = np.arange(kept_count)
+    frequency = np.where(index < kept_count // 2, index, index - kept_count)
+    turns = (np.asarray(positions)[:, None] * frequency[None, :]) % length
+    return 2.0 * np.pi * turns / length
+
+
+def depth_table(share):
+    angles = (
+        table_angles(np.arange(NZ), KZ, NZ)[:, None, :, None]
+        + table_angles(np.arange(NT), KT, NT)[None, :, None, :]
+    ).reshape(NZ * NT, KZ * KT)
+    parts = np.stack([np.cos(angles), -np.sin(angles)], -1)
+    owners = KZ * KT // share
+    rows = np.zeros((owners, SLOTS, NZ * NT))
+    rows[:, : 2 * share] = parts.reshape(NZ * NT, owners, 2 * share).transpose(1, 2, 0)
+    return rows.reshape(owners * SLOTS, NZ * NT).astype(jnp.bfloat16)
+
+
+def plane_tables(count_gx, count_gy, rows_x, rows_y):
+    length_x, length_y = count_gx * rows_x, count_gy * rows_y
+    angle_x = table_angles(np.arange(length_x), KX, length_x).T.reshape(KX, 1, 1, 1, count_gx, 1, rows_x, 1)
+    angle_y = table_angles(np.arange(length_y), KY, length_y).T.reshape(1, KY, 1, 1, 1, count_gy, 1, rows_y)
+    angles = (angle_x + angle_y).transpose(0, 1, 2, 3, 6, 7, 4, 5).reshape(KX * KY, length_x * length_y)
+    pad = ((0, -KX * KY % LANES), (0, 0))
+    cosine, sine = np.pad(np.cos(angles), pad), np.pad(np.sin(angles), pad)
+    forward = np.concatenate([cosine.T, sine.T], 0)
+    inverse = np.concatenate([cosine.T, sine.T], 1)
+    return forward.astype(jnp.bfloat16), inverse.astype(jnp.bfloat16)
+
+
+def dot(left, right, left_dim=1, right_dim=0):
+    return lax.dot_general(
+        left, right, (((left_dim,), (right_dim,)), ((), ())), preferred_element_type=jnp.float32
+    )
+
+
+def depth_kernel(factor, table_ref, field_ref, sent_ref):
+    spectra = dot(table_ref[...], field_ref[...], 1, 1)
+    sent_ref[...] = (spectra * factor).astype(jnp.bfloat16)
+
+
+def to_plane_modes(share, channels, arrived_ref, forward_ref, wide_ref, modes_ref):
+    halves, rows, lanes = wide_ref.shape
+    devices = rows // SLOTS
+    for h in range(halves):
+        wide_ref[h] = arrived_ref[:, h * LANES : (h + 1) * LANES].astype(jnp.float32)
+    columns = []
+    for slot in range(2 * share):
+        pieces = []
+        for h in range(halves):
+            piece = wide_ref[h, pl.ds(slot, devices, stride=SLOTS), :]
+            pieces += [piece[:, c * channels : (c + 1) * channels] for c in range(lanes // channels)]
+        columns.append(jnp.concatenate(pieces, 0))
+    cells = jnp.concatenate(columns, 1).T
+    blocks = []
+    for k in range(share):
+        real = cells[2 * k * channels : (2 * k + 1) * channels]
+        imag = cells[(2 * k + 1) * channels : (2 * k + 2) * channels]
+        blocks += [jnp.concatenate([real, imag], 1), jnp.concatenate([imag, -real], 1)]
+    modes = dot(jnp.concatenate(blocks, 0).astype(jnp.bfloat16), forward_ref[...])
+    each = modes_ref.shape[0] // share
+    for k in range(share):
+        for j in range(each):
+            modes_ref[k * each + j] = modes[2 * k * channels : (2 * k + 2) * channels, j * LANES : (j + 1) * LANES]
+
+
+def store_pair(tile, share, channels, real, imag, pair_ref):
+    pair_ref[tile, :channels, :LANES] = real.astype(jnp.bfloat16)
+    pair_ref[tile, channels:, :LANES] = imag.astype(jnp.bfloat16)
+    pair_ref[tile, :channels, LANES:] = (-imag).astype(jnp.bfloat16)
+    pair_ref[tile, channels:, LANES:] = real.astype(jnp.bfloat16)
+
+
+def to_cells(share, channels, pair_ref, inverse_ref, out_ref, sent_ref):
+    halves, rows, lanes = out_ref.shape
+    devices = rows // SLOTS
+    each = pair_ref.shape[0] // share
+    padded = each * LANES
+    out_ref[...] = jnp.zeros_like(out_ref)
+    spectra = []
+    for k in range(share):
+        cosine = jnp.concatenate([pair_ref[k * each + j, :, :LANES] for j in range(each)], 1)
+        sine = jnp.concatenate([pair_ref[k * each + j, :, LANES:] for j in range(each)], 1)
+        spectra.append(jnp.concatenate([cosine, sine], 1))
+    total = dot(inverse_ref[...], jnp.concatenate(spectra, 0), 1, 1)
+    per_half = lanes // channels
+    for slot in range(2 * share):
+        columns = slice(slot * channels, (slot + 1) * channels)
+        for h in range(halves):
+            pieces = [total[c * devices : (c + 1) * devices, columns] for c in range(h * per_half, (h + 1) * per_half)]
+            out_ref[h, pl.ds(slot, devices, stride=SLOTS), :] = jnp.concatenate(pieces, 1)
+    for h in range(halves):
+        sent_ref[:, h * LANES : (h + 1) * LANES] = out_ref[h].astype(jnp.bfloat16)
+
+
+def mix_kernel(
+    share, channels, plane, arrived_ref, weight_ref, forward_ref, inverse_ref, sent_ref, modes_ref, turned_ref,
+    wide_ref, pair_ref,
+):
+    to_plane_modes(share, channels, arrived_ref, forward_ref, wide_ref, modes_ref)
+    wide = 2 * channels
+    each = modes_ref.shape[0] // share
+
+    @pl.loop(0, share)
+    def _(k):
+        for j in range(each):
+            tile = k * each + j
+            count = min(LANES, plane - j * LANES)
+            rows = pl.ds(pl.multiple_of(k * plane + j * LANES, 64), count)
+            by_real = jnp.zeros((wide, LANES), jnp.float32)
+            by_imag = jnp.zeros((wide, LANES), jnp.float32)
+            for first in range(0, channels, GROUP):
+                real_sum, imag_sum = None, None
+                for c in range(first, first + GROUP, LANES // wide):
+                    block = weight_ref[rows, c * wide : c * wide + LANES].T
+                    if count < LANES:
+                        block = jnp.concatenate([block, jnp.zeros((LANES, LANES - count), jnp.bfloat16)], 1)
+                    turned_ref[tile, c * wide : c * wide + LANES, :] = block
+                    for h in range(LANES // wide):
+                        weight = block[h * wide : (h + 1) * wide]
+                        real = jnp.broadcast_to(modes_ref[tile, c + h : c + h + 1, :], (wide, LANES))
+                        imag = jnp.broadcast_to(
+                            modes_ref[tile, channels + c + h : channels + c + h + 1, :], (wide, LANES)
+                        )
+                        real, imag = real.astype(jnp.bfloat16) * weight, imag.astype(jnp.bfloat16) * weight
+                        real_sum = real if real_sum is None else real_sum + real
+                        imag_sum = imag if imag_sum is None else imag_sum + imag
+                by_real += real_sum.astype(jnp.float32)
+                by_imag += imag_sum.astype(jnp.float32)
+            store_pair(
+                tile, share, channels, by_real[:channels] - by_imag[channels:],
+                by_real[channels:] + by_imag[:channels], pair_ref,
+            )
+
+    to_cells(share, channels, pair_ref, inverse_ref, wide_ref, sent_ref)
+
+
+def adjoint_kernel(
+    share, channels, arrived_ref, turned_ref, forward_ref, inverse_ref, sent_ref, modes_ref, wide_ref, pair_ref,
+    part_ref,
+):
+    to_plane_modes(share, channels, arrived_ref, forward_ref, wide_ref, modes_ref)
+    wide = 2 * channels
+    tiles = modes_ref.shape[0]
+
+    @pl.loop(0, tiles)
+    def _(tile):
+        real, imag = modes_ref[tile, :channels, :], modes_ref[tile, channels:, :]
+        here = jnp.concatenate([real, imag], 0).astype(jnp.bfloat16)
+        turn = jnp.concatenate([imag, -real], 0).astype(jnp.bfloat16)
+        for c in range(channels):
+            weight = turned_ref[tile, c * wide : (c + 1) * wide, :]
+            for part, factor in enumerate((here, turn)):
+                product = factor * weight
+                while product.shape[0] > ROWS:
+                    half = product.shape[0] // 2
+                    product = product[:half] + product[half:]
+                part_ref[tile, (part * channels + c) * ROWS : (part * channels + c + 1) * ROWS, :] = product
+
+    row = lax.broadcasted_iota(jnp.int32, (wide, ROWS * wide), 0)
+    column = lax.broadcasted_iota(jnp.int32, (wide, ROWS * wide), 1)
+    groups = jnp.where(column // ROWS == row, 1.0, 0.0).astype(jnp.bfloat16)
+    for tile in range(tiles):
+        summed = dot(groups, part_ref[tile])
+        store_pair(tile, share, channels, summed[:channels], summed[channels:], pair_ref)
+
+    to_cells(share, channels, pair_ref, inverse_ref, wide_ref, sent_ref)
+
+
+def outer_kernel(share, channels, plane, in_ref, back_ref, grad_ref, held_ref, sems):
+    wide = 2 * channels
+    each = in_ref.shape[0] // share
+    per_block = LANES // wide
+
+    def copy(k, j):
+        rows = pl.ds(pl.multiple_of(k * plane + j * LANES, 64), min(LANES, plane - j * LANES))
+        return pltpu.make_async_copy(held_ref.at[rows], grad_ref.at[rows], sems.at[k * each + j])
+
+    @pl.loop(0, share)
+    def _(k):
+        for j in range(each):
+            tile = k * each + j
+            count = min(LANES, plane - j * LANES)
+            rows = pl.ds(pl.multiple_of(k * plane + j * LANES, 64), count)
+            real, imag = back_ref[tile, :channels, :], back_ref[tile, channels:, :]
+            here = jnp.concatenate([real, imag], 0)
+            turn = jnp.concatenate([imag, -real], 0)
+            for c in range(0, channels, per_block):
+                parts = [
+                    in_ref[tile, c + h : c + h + 1, :] * here
+                    + in_ref[tile, channels + c + h : channels + c + h + 1, :] * turn
+                    for h in range(per_block)
+                ]
+                block = jnp.concatenate(parts, 0).T
+                held_ref[rows, c * wide : c * wide + LANES] = block[:count]
+            copy(k, j).start()
+
+    @pl.loop(0, share)
+    def _(k):
+        for j in range(each):
+            copy(k, j).wait()
+
+
+def slope_kernel(
+    cells, channels, factor, arrived_ref, table_ref, field_ref, cotangent_ref, point_ref, slope_ref, sent_ref
+):
+    spectral = dot(arrived_ref[...], table_ref[...], 0, 0)
+    for c in range(cells):
+        rows = slice(c * channels, (c + 1) * channels)
+        before = spectral[rows] * factor + dot(point_ref[...], field_ref[rows, :], 0, 0)
+        cumulative = 0.5 + 0.5 * lax.erf(before * math.sqrt(0.5))
+        density = jnp.exp(-0.5 * before * before) * (1.0 / math.sqrt(2.0 * math.pi))
+        slope = cotangent_ref[rows, :].astype(jnp.float32) * (cumulative + before * density)
+        slope_ref[rows, :] = slope.astype(jnp.bfloat16)
+    sent = dot(table_ref[...], slope_ref[...], 1, 1)
+    sent_ref[...] = (sent * factor).astype(jnp.bfloat16)
+
+
+def final_kernel(cells, channels, factor, arrived_ref, table_ref, slope_ref, point_ref, grad_ref):
+    spectral = dot(arrived_ref[...], table_ref[...], 0, 0)
+    for c in range(cells):
+        rows = slice(c * channels, (c + 1) * channels)
+        pointwise = dot(point_ref[...], slope_ref[rows, :])
+        grad_ref[rows, :] = (pointwise + spectral[rows] * factor).astype(jnp.bfloat16)
+
+
+def params(mebibytes, semantics=None):
+    return pltpu.CompilerParams(dimension_semantics=semantics, vmem_limit_bytes=mebibytes * 1024 * 1024)
+
+
+def on_chip(value):
+    return pltpu.with_memory_space_constraint(value, pltpu.VMEM)
+
+
+def off_chip(value):
+    return pltpu.with_memory_space_constraint(value, pltpu.HBM)
+
+
+IN_VMEM = pl.BlockSpec(memory_space=pltpu.VMEM)
+
+
+def per_device(inputs, cotangent, point_weight, spectral_weight):
+    rows_x, rows_y, channels, depth = inputs.shape
+    mode_rows, mode_cols, flat = spectral_weight.shape
+    count_gx, count_gy = lax.axis_size("gx"), lax.axis_size("gy")
+    devices = count_gx * count_gy
+    share = mode_rows // KX
+    cells = rows_x * rows_y
+    lanes = cells * channels
+    wide = 2 * channels
+    plane = KX * KY
+    each = -(-plane // LANES)
+    tiles = share * each
+    points = cells * devices
+    slots = devices * SLOTS
+    inner = 1.0 / math.sqrt(points * depth)
+    outer = 1.0 / math.sqrt(plane * KZ * KT)
+
+    table = on_chip(jnp.asarray(depth_table(share)))
+    forward, inverse = (on_chip(jnp.asarray(t)) for t in plane_tables(count_gx, count_gy, rows_x, rows_y))
+    field = on_chip(inputs.reshape(lanes, depth))
+    seed = on_chip(cotangent.reshape(lanes, depth))
+    point = on_chip(point_weight)
+
+    def exchange(sent):
+        blocks = sent.reshape(devices, SLOTS, lanes)
+        arrived = lax.all_to_all(blocks, GRID_AXES, split_axis=0, concat_axis=0, tiled=True)
+        return on_chip(arrived.reshape(slots, lanes))
+
+    packet = pltpu.VMEM((slots, lanes), jnp.bfloat16)
+    spectra = pltpu.VMEM((tiles, wide, LANES), jnp.float32)
+
+    sent = pl.pallas_call(
+        functools.partial(depth_kernel, inner), in_specs=[IN_VMEM] * 2, out_specs=IN_VMEM, out_shape=packet,
+        compiler_params=params(2),
+        cost_estimate=pl.CostEstimate(flops=READ_AHEAD_FLOPS, transcendentals=0, bytes_accessed=0),
+        name="depth",
+    )(off_chip(jnp.asarray(depth_table(share))), off_chip(inputs.reshape(lanes, depth)))
+    arrived = exchange(sent)
+    scratch = [
+        pltpu.VMEM((lanes // LANES, slots, LANES), jnp.float32),
+        pltpu.VMEM((tiles, wide, 2 * LANES), jnp.bfloat16),
+    ]
+    sent, modes_in, turned = pl.pallas_call(
+        functools.partial(mix_kernel, share, channels, plane),
+        in_specs=[IN_VMEM] * 4, out_specs=[IN_VMEM] * 3,
+        out_shape=[packet, spectra, pltpu.VMEM((tiles, flat, LANES), jnp.bfloat16)],
+        scratch_shapes=scratch, compiler_params=params(6), name="mix",
+    )(arrived, on_chip(spectral_weight.reshape(share * plane, flat)), forward, inverse)
+    arrived = exchange(sent)
+    slope, sent = pl.pallas_call(
+        functools.partial(slope_kernel, cells, channels, outer),
+        in_specs=[IN_VMEM] * 5, out_specs=[IN_VMEM] * 2, out_shape=[pltpu.VMEM((lanes, depth), jnp.bfloat16), packet],
+        compiler_params=params(8), name="slope",
+    )(arrived, table, field, seed, point)
+    arrived = exchange(sent)
+    sent, modes_back = pl.pallas_call(
+        functools.partial(adjoint_kernel, share, channels),
+        in_specs=[IN_VMEM] * 4, out_specs=[IN_VMEM] * 2, out_shape=[packet, spectra],
+        scratch_shapes=scratch + [pltpu.VMEM((tiles, ROWS * wide, LANES), jnp.bfloat16)],
+        compiler_params=params(12), name="adjoint",
+    )(arrived, on_chip(turned), forward, inverse)
+    arrived = exchange(sent)
+    grad_spectral = pl.pallas_call(
+        functools.partial(outer_kernel, share, channels, plane),
+        in_specs=[IN_VMEM] * 2, out_specs=pl.BlockSpec(memory_space=pl.ANY),
+        out_shape=jax.ShapeDtypeStruct((share * plane, flat), jnp.float32),
+        scratch_shapes=[pltpu.VMEM((share * plane, flat), jnp.float32), pltpu.SemaphoreType.DMA((tiles,))],
+        compiler_params=params(24),
+        cost_estimate=pl.CostEstimate(
+            flops=4 * share * plane * flat * wide, transcendentals=0, bytes_accessed=4 * share * plane * flat
+        ),
+        name="outer",
+    )(on_chip(modes_in), on_chip(modes_back))
+    grad_input = pl.pallas_call(
+        functools.partial(final_kernel, cells, channels, inner),
+        in_specs=[IN_VMEM] * 4, out_specs=IN_VMEM, out_shape=jax.ShapeDtypeStruct((lanes, depth), jnp.bfloat16),
+        compiler_params=params(8), name="final",
+    )(arrived, table, on_chip(slope), point)
+    return grad_input.reshape(inputs.shape), grad_spectral.reshape(spectral_weight.shape)
 
 
 def kept_angles(positions, kept_count, length):
@@ -110,7 +443,7 @@
     return jax.nn.gelu(values, approximate=False)
 
 
-def per_device(inputs, cotangent, point_weight, spectral_weight):
+def general_per_device(inputs, cotangent, point_weight, spectral_weight):
     rows_x, rows_y, channels, cells = inputs.shape
     mode_rows, mode_cols, flat_width = spectral_weight.shape
     weight_blocks = spectral_weight.reshape(mode_rows, mode_cols, channels, 2 * channels)
@@ -177,16 +510,25 @@
 
 
 def solution(mesh):
+    count_gx, count_gy = mesh.shape["gx"], mesh.shape["gy"]
     placed = (
         P("gx", "gy", None, None),
         P("gx", "gy", None, None),
         P(),
         P(("gx", "gy"), None, None),
     )
-    return jax.shard_map(
-        per_device,
-        mesh=mesh,
-        in_specs=placed,
-        out_specs=(P("gx", "gy", None, None), P(("gx", "gy"), None, None)),
-        check_vma=False,
-    )
+
+    def program(inputs, cotangent, point_weight, spectral_weight):
+        cells = inputs.shape[0] * inputs.shape[1] // (count_gx * count_gy)
+        whole_modes = KZ * KT % (count_gx * count_gy) == 0
+        fits = whole_modes and 2 * KZ * KT // (count_gx * count_gy) <= SLOTS
+        fits = fits and inputs.shape[2] == 32 and cells * inputs.shape[2] == 256
+        return jax.shard_map(
+            per_device if fits else general_per_device,
+            mesh=mesh,
+            in_specs=placed,
+            out_specs=(P("gx", "gy", None, None), P(("gx", "gy"), None, None)),
+            check_vma=False,
+        )(inputs, cotangent, point_weight, spectral_weight)
+
+    return program

time: 462 us -> 57.9 us (0.13); the launches traced: 453 us -> 57.7 us
  other arithmetic: 141 us -> 0 us
  local copies, waits for them, and re-layouts: 84.9 us -> 0.04 us
  blocking collectives: 104 us -> 35 us
  waiting for transfers between devices: 59.4 us -> 2.68 us
  matrix products: 40.2 us -> 0 us
  Pallas kernels: 0 us -> 16.6 us
  between operations: 14.8 us -> 0.74 us
  starting transfers between devices: 8.51 us -> 2.58 us
    all_gather x2 -> x0, blocking collectives: 78.3 us -> none  [to_space(): lax.all_gather(returned, 'gx', axis=0, tiled=True).astype(jnp.float32)]
    unnamed x2 -> x0, other arithmetic: 73 us -> none
    reduce_scatter x2 -> x0, waiting for transfers between devices: 59.3 us -> none  [to_modes(): lax.psum_scatter(rotate(depth_spec.astype(jnp.float32), local_x[0], local...]
    reshape x6 -> x0, local copies, waits for them, and re-layouts: 47.6 us -> none  [the longest x1 24.3 us: per_device(): weight_grad(spectra_in, spectra_back)]
    dot_general x26 -> x0, matrix products: 40.2 us -> none  [the longest x8 16 us: rotate(): jnp.einsum(pattern, spectra, cosine_table, precision=lax.Precision.HIGHEST)]
    concatenate x7 -> x0, other arithmetic: 29.2 us -> none  [the longest x1 28.5 us: weight_grad(): return jnp.concatenate([real_part, imag_part], -1)]
    add x6 -> x0, other arithmetic: 23.3 us -> none  [the longest x1 20 us: weight_grad(): partial_outer(real_in, real_back) + partial_outer(imag_in, imag_back)]
    pallas_call x0 -> x6, Pallas kernels: none -> 16.6 us  [the longest x1 5.49 us: per_device(): pl.pallas_call(functools.partial(outer_kernel, share, channels, plane), i...]
  transfers between devices with their start and end apart: 4 -> 1, of which waited for: 2 -> 1; matrix products, arithmetic and copies ran while one was open for 16% -> 0% of each run, Pallas kernels for 0% -> 10%
where the time goes in v2:
time: 57.9 us; the launch traced here: 57.7 us
  blocking collectives  35 us (60%)
  Pallas kernels  16.6 us (29%)
  waiting for transfers between devices  2.68 us (5%)
  starting transfers between devices  2.58 us (4%)
  between operations  0.74 us (1%)
    all_to_all x3, blocking collectives, exchange(): lax.all_to_all(blocks, GRID_AXES, split_axis=0, concat_axis=0, tiled=True)  35 us
    pallas_call x1, Pallas kernels, per_device(): pl.pallas_call(functools.partial(outer_kernel, share, channels, plane), i...  5.49 us
    pallas_call x1, Pallas kernels, per_device(): pl.pallas_call(functools.partial(mix_kernel, share, channels, plane), in_...  3.99 us
    pallas_call x1, Pallas kernels, per_device(): pl.pallas_call(functools.partial(adjoint_kernel, share, channels), in_spe...  3.92 us
    all_to_all x1, waiting for transfers between devices, exchange(): lax.all_to_all(blocks, GRID_AXES, split_axis=0, concat_axis=0, tiled=True)  2.68 us
    all_to_all x1, starting transfers between devices, exchange(): lax.all_to_all(blocks, GRID_AXES, split_axis=0, concat_axis=0, tiled=True)  2.58 us
    pallas_call x1, Pallas kernels, per_device(): pl.pallas_call(functools.partial(depth_kernel, inner), in_specs=[IN_VMEM]...  1.44 us
  transfers between devices with their start and end apart: 1, of which 1 were waited for; matrix products, arithmetic and copies ran while one was open for 0% of the time, Pallas kernels for 10%

profile of v2, /device:TPU:0, one launch (start us, length us, event | category | flops | bytes accessed | tf_op | source)
XLA Modules:
  0.0 57.7 jit_solution(2639914793543709929)
XLA Ops:
  0.6 0.0 copy-start
  0.6 0.0 copy-start.1
  0.7 0.0 copy-start.2
  0.7 1.4 %depth.1 = bf16[256,256]{1,0:T(8,128)(2,1)S(1)} custom-call(bf16[256,512]{1,0:T(8,128)(2,1)} %constant.6.clone.table_ref, bf16[256,512]{1,0:T(8,128)(2,1)} %bitcast.18), custom_call_target="tpu_custom_call" | custom-call | flops 99999997952 | tf_op jit(solution)/shard_map/depth/pallas_call | solution.py:299
  2.1 0.0 copy-start.3
  2.1 0.0 copy-start.4
  2.1 0.0 copy-start.5
  2.1 0.0 copy-start.6
  2.2 15.3 %all_to_all.20 = bf16[32,8,256]{2,1,0:T(8,128)(2,1)S(1)} all-to-all(bf16[32,8,256]{2,1,0:T(8,128)(2,1)S(1)} %bitcast.23), channel_id=1, replica_groups=mesh['gx'=4,'gy'=8] {'gx','gy'}, dimensions={0} | all-to-all | bytes 262144 | tf_op jit(solution)/shard_map/all_to_all | solution.py:293
  17.4 0.0 copy-done
  17.4 0.0 copy-done.1
  17.4 0.0 copy-done.2
  17.4 4.0 %mix.1 = (bf16[256,256]{1,0:T(8,128)(2,1)S(1)}, f32[15,64,128]{2,1,0:T(8,128)S(1)}, bf16[15,2048,128]{2,1,0:T(8,128)(2,1)S(1)}) custom-call(bf16[256,256]{1,0:T(8,128)(2,1)S(1)} %bitcast.15, bf16[1728,2048]{1,0:T(8,128)(2,1)S(1)} %bitcast.13, bf16[512,640]{1,0:T(8,128)(2,1)S(1)} %copy-done.2, bf16[256,1280]{1,0:T(8,128)(2,1)S(1)} %copy-done.1), custom_call_target="tpu_custom_call" | custom-call | tf_op jit(solution)/shard_map/mix/pallas_call | solution.py:310
  21.4 9.9 %all_to_all.21 = bf16[32,8,256]{2,1,0:T(8,128)(2,1)S(1)} all-to-all(bf16[32,8,256]{2,1,0:T(8,128)(2,1)S(1)} %bitcast.21), channel_id=1, replica_groups=mesh['gx'=4,'gy'=8] {'gx','gy'}, dimensions={0} | all-to-all | bytes 262144 | tf_op jit(solution)/shard_map/all_to_all | solution.py:293
  31.3 0.0 copy-done.3
  31.3 0.0 copy-done.4
  31.3 0.0 copy-done.5
  31.3 0.0 copy-done.6
  31.4 0.7 %slope.1 = (bf16[256,512]{1,0:T(8,128)(2,1)S(1)}, bf16[256,256]{1,0:T(8,128)(2,1)S(1)}) custom-call(bf16[256,256]{1,0:T(8,128)(2,1)S(1)} %bitcast.17, bf16[256,512]{1,0:T(8,128)(2,1)S(1)} %copy-done.3, bf16[256,512]{1,0:T(8,128)(2,1)S(1)} %bitcast.19, bf16[256,512]{1,0:T(8,128)(2,1)S(1)} %bitcast.20, bf16[32,32]{1,0:T(8,128)(2,1)S(1)} %copy-done.6), custom_call_target="tpu_custom_call" | custom-call | tf_op jit(solution)/shard_map/slope/pallas_call | solution.py:317
  32.1 9.9 %all_to_all.22 = bf16[32,8,256]{2,1,0:T(8,128)(2,1)S(1)} all-to-all(bf16[32,8,256]{2,1,0:T(8,128)(2,1)S(1)} %bitcast.22), channel_id=1, replica_groups=mesh['gx'=4,'gy'=8] {'gx','gy'}, dimensions={0} | all-to-all | bytes 262144 | tf_op jit(solution)/shard_map/all_to_all | solution.py:293
  42.0 3.9 %adjoint.1 = (bf16[256,256]{1,0:T(8,128)(2,1)}, f32[15,64,128]{2,1,0:T(8,128)S(1)}) custom-call(bf16[256,256]{1,0:T(8,128)(2,1)S(1)} %bitcast.14, bf16[15,2048,128]{2,1,0:T(8,128)(2,1)S(1)} %get-tuple-element.11.turned_ref, bf16[512,640]{1,0:T(8,128)(2,1)S(1)} %copy-done.2, bf16[256,1280]{1,0:T(8,128)(2,1)S(1)} %copy-done.1), custom_call_target="tpu_custom_call" | custom-call | tf_op jit(solution)/shard_map/adjoint/pallas_call | solution.py:323
  45.9 2.6 %all-to-all-start.3 = ((bf16[32,8,256]{2,1,0:T(8,128)(2,1)}), bf16[32,8,256]{2,1,0:T(8,128)(2,1)S(1)}, u32[]{:S(2)}, u32[]{:S(2)}) async-start(bf16[32,8,256]{2,1,0:T(8,128)(2,1)} %bitcast.9), calls=%async_computation.3 | async-start | bytes 262144 | tf_op jit(solution)/shard_map/all_to_all | solution.py:293
  48.5 5.5 %outer.1 = f32[1728,2048]{1,0:T(8,128)} custom-call(f32[15,64,128]{2,1,0:T(8,128)S(1)} %get-tuple-element.14.in_ref, f32[15,64,128]{2,1,0:T(8,128)S(1)} %get-tuple-element.15.back_ref), custom_call_target="tpu_custom_call" | custom-call | flops 905969664 | bytes 14155776 | tf_op jit(solution)/shard_map/outer/pallas_call | solution.py:330
  54.0 2.7 %all-to-all-done.3 = bf16[32,8,256]{2,1,0:T(8,128)(2,1)S(1)} async-done(((bf16[32,8,256]{2,1,0:T(8,128)(2,1)}), bf16[32,8,256]{2,1,0:T(8,128)(2,1)S(1)}, u32[]{:S(2)}, u32[]{:S(2)}) %all-to-all-start.3) | async-done | bytes 131104 | tf_op jit(solution)/shard_map/all_to_all | solution.py:293
  56.6 1.0 %final.1 = bf16[256,512]{1,0:T(8,128)(2,1)} custom-call(bf16[256,256]{1,0:T(8,128)(2,1)S(1)} %bitcast.16, bf16[256,512]{1,0:T(8,128)(2,1)S(1)} %copy-done.3, bf16[256,512]{1,0:T(8,128)(2,1)S(1)} %get-tuple-element.13.slope_ref, bf16[32,32]{1,0:T(8,128)(2,1)S(1)} %copy-done.6), custom_call_target="tpu_custom_call" | custom-call | tf_op jit(solution)/shard_map/final/pallas_call | solution.py:341
Async XLA Ops:
  0.6 16.8 %copy-start = (bf16[72,24,2048]{2,1,0:T(8,128)(2,1)S(1)}, bf16[72,24,2048]{2,1,0:T(8,128)(2,1)}, u32[]{:S(2)}) copy-start(bf16[72,24,2048]{2,1,0:T(8,128)(2,1)} %param.11) | copy-start | bytes 21233668
  0.6 16.8 %copy-start.1 = (bf16[256,1280]{1,0:T(8,128)(2,1)S(1)}, bf16[256,1280]{1,0:T(8,128)(2,1)}, u32[]{:S(2)}) copy-start(bf16[256,1280]{1,0:T(8,128)(2,1)} %constant.8.clone.inverse_ref) | copy-start | bytes 1966084
  0.7 16.8 %copy-start.2 = (bf16[512,640]{1,0:T(8,128)(2,1)S(1)}, bf16[512,640]{1,0:T(8,128)(2,1)}, u32[]{:S(2)}) copy-start(bf16[512,640]{1,0:T(8,128)(2,1)} %constant.7.clone.forward_ref) | copy-start | bytes 1966084
  2.1 29.2 %copy-start.3 = (bf16[256,512]{1,0:T(8,128)(2,1)S(1)}, bf16[256,512]{1,0:T(8,128)(2,1)}, u32[]{:S(2)}) copy-start(bf16[256,512]{1,0:T(8,128)(2,1)} %constant.6.clone.table_ref) | copy-start | bytes 786436
  2.1 29.2 %copy-start.4 = (bf16[4,2,32,512]{3,2,1,0:T(8,128)(2,1)S(1)}, bf16[4,2,32,512]{3,2,1,0:T(8,128)(2,1)}, u32[]{:S(2)}) copy-start(bf16[4,2,32,512]{3,2,1,0:T(8,128)(2,1)} %param.8) | copy-start | bytes 786436
  2.1 29.2 %copy-start.5 = (bf16[4,2,32,512]{3,2,1,0:T(8,128)(2,1)S(1)}, bf16[4,2,32,512]{3,2,1,0:T(8,128)(2,1)}, u32[]{:S(2)}) copy-start(bf16[4,2,32,512]{3,2,1,0:T(8,128)(2,1)} %param.9) | copy-start | bytes 786436
  2.1 29.2 %copy-start.6 = (bf16[32,32]{1,0:T(8,128)(2,1)S(1)}, bf16[32,32]{1,0:T(8,128)(2,1)}, u32[]{:S(2)}) copy-start(bf16[32,32]{1,0:T(8,128)(2,1)} %point_ref.3) | copy-start | bytes 6148
  45.9 10.8 %all-to-all-start.3 = ((bf16[32,8,256]{2,1,0:T(8,128)(2,1)}), bf16[32,8,256]{2,1,0:T(8,128)(2,1)S(1)}, u32[]{:S(2)}, u32[]{:S(2)}) async-start(bf16[32,8,256]{2,1,0:T(8,128)(2,1)} %bitcast.9), calls=%async_computation.3 | async-start | bytes 262144 | tf_op jit(solution)/shard_map/all_to_all | solution.py:293

commit v3 on v2

--- a/solution.py
+++ b/solution.py
@@ -17,6 +17,7 @@
 KT = 8
 SLOTS = 8
 LANES = 128
+LENGTH = 16
 GROUP = 4
 ROWS = 16
 READ_AHEAD_FLOPS = 10**11
@@ -44,14 +45,23 @@
 
 def plane_tables(count_gx, count_gy, rows_x, rows_y):
     length_x, length_y = count_gx * rows_x, count_gy * rows_y
-    angle_x = table_angles(np.arange(length_x), KX, length_x).T.reshape(KX, 1, 1, 1, count_gx, 1, rows_x, 1)
-    angle_y = table_angles(np.arange(length_y), KY, length_y).T.reshape(1, KY, 1, 1, 1, count_gy, 1, rows_y)
-    angles = (angle_x + angle_y).transpose(0, 1, 2, 3, 6, 7, 4, 5).reshape(KX * KY, length_x * length_y)
-    pad = ((0, -KX * KY % LANES), (0, 0))
-    cosine, sine = np.pad(np.cos(angles), pad), np.pad(np.sin(angles), pad)
+    turns_x = np.outer(np.arange(length_x), np.arange(length_x)) % length_x / length_x
+    turns_y = np.outer(np.arange(length_y), np.arange(length_y)) % length_y / length_y
+    turns_x = turns_x.reshape(length_x, 1, count_gx, 1, rows_x, 1)
+    turns_y = turns_y.reshape(1, length_y, 1, count_gy, 1, rows_y)
+    turns = (turns_x + turns_y).transpose(0, 1, 4, 5, 2, 3).reshape(length_x * length_y, length_x * length_y)
+    cosine, sine = np.cos(2.0 * np.pi * turns), np.sin(2.0 * np.pi * turns)
     forward = np.concatenate([cosine.T, sine.T], 0)
     inverse = np.concatenate([cosine.T, sine.T], 1)
     return forward.astype(jnp.bfloat16), inverse.astype(jnp.bfloat16)
+
+
+def residue_of(mode):
+    return (mode if mode < KX // 2 else mode - KX) % LENGTH
+
+
+def modes_of(residue):
+    return [mode for mode in range(KX) if residue_of(mode) == residue]
 
 
 def dot(left, right, left_dim=1, right_dim=0):
@@ -119,29 +129,42 @@
         sent_ref[:, h * LANES : (h + 1) * LANES] = out_ref[h].astype(jnp.bfloat16)
 
 
+def fold_rows(weight_ref, mode, first, count, columns):
+    row = lax.broadcasted_iota(jnp.int32, (8, LANES), 0)
+    low = jnp.where(row < 4, 1.0, 0.0)
+    high = 1.0 - low
+    folded = []
+    for residue in range(first, first + count):
+        total = None
+        for kx in modes_of(residue):
+            rows = pl.ds(pl.multiple_of((mode * KX + kx) * KY, 8), KY)
+            block = weight_ref[rows, columns].astype(jnp.float32)
+            total = block if total is None else total + block
+        folded += [total[:8] + high * total[8:16], total[16:] + low * total[8:16]]
+    return jnp.concatenate(folded, 0).astype(jnp.bfloat16)
+
+
 def mix_kernel(
-    share, channels, plane, arrived_ref, weight_ref, forward_ref, inverse_ref, sent_ref, modes_ref, turned_ref,
+    share, channels, arrived_ref, weight_ref, forward_ref, inverse_ref, sent_ref, modes_ref, turned_ref,
     wide_ref, pair_ref,
 ):
     to_plane_modes(share, channels, arrived_ref, forward_ref, wide_ref, modes_ref)
     wide = 2 * channels
     each = modes_ref.shape[0] // share
+    per_tile = LANES // LENGTH
 
     @pl.loop(0, share)
     def _(k):
         for j in range(each):
             tile = k * each + j
-            count = min(LANES, plane - j * LANES)
-            rows = pl.ds(pl.multiple_of(k * plane + j * LANES, 64), count)
             by_real = jnp.zeros((wide, LANES), jnp.float32)
             by_imag = jnp.zeros((wide, LANES), jnp.float32)
             for first in range(0, channels, GROUP):
                 real_sum, imag_sum = None, None
                 for c in range(first, first + GROUP, LANES // wide):
-                    block = weight_ref[rows, c * wide : c * wide + LANES].T
-                    if count < LANES:
-                        block = jnp.concatenate([block, jnp.zeros((LANES, LANES - count), jnp.bfloat16)], 1)
-                    turned_ref[tile, c * wide : c * wide + LANES, :] = block
+                    columns = slice(c * wide, c * wide + LANES)
+                    block = fold_rows(weight_ref, k, j * per_tile, per_tile, columns).T
+                    turned_ref[tile, columns, :] = block
                     for h in range(LANES // wide):
                         weight = block[h * wide : (h + 1) * wide]
                         real = jnp.broadcast_to(modes_ref[tile, c + h : c + h + 1, :], (wide, LANES))
@@ -193,21 +216,38 @@
     to_cells(share, channels, pair_ref, inverse_ref, wide_ref, sent_ref)
 
 
-def outer_kernel(share, channels, plane, in_ref, back_ref, grad_ref, held_ref, sems):
+def outer_kernel(share, channels, in_ref, back_ref, grad_ref, held_ref, sems):
     wide = 2 * channels
     each = in_ref.shape[0] // share
     per_block = LANES // wide
-
-    def copy(k, j):
-        rows = pl.ds(pl.multiple_of(k * plane + j * LANES, 64), min(LANES, plane - j * LANES))
-        return pltpu.make_async_copy(held_ref.at[rows], grad_ref.at[rows], sems.at[k * each + j])
+    per_tile = LANES // LENGTH
+
+    def runs(j):
+        inside = [kx for kx in range(KX) if residue_of(kx) // per_tile == j]
+        found = []
+        for kx in inside:
+            if found and found[-1][0] + found[-1][2] == kx and found[-1][1] + found[-1][2] == residue_of(kx):
+                found[-1][2] += 1
+            else:
+                found.append([kx, residue_of(kx), 1])
+        return found
+
+    def copies(k, j):
+        made = []
+        for place, (mode, residue, count) in enumerate(runs(j)):
+            source = pl.ds(pl.multiple_of((k * LENGTH + residue) * KY, 8), count * KY)
+            target = pl.ds(pl.multiple_of((k * KX + mode) * KY, 8), count * KY)
+            made.append(
+                pltpu.make_async_copy(held_ref.at[source], grad_ref.at[target], sems.at[k * each + j, place])
+            )
+        return made
+
+    low = lax.broadcasted_iota(jnp.int32, (8, LANES), 0) < 4
 
     @pl.loop(0, share)
     def _(k):
         for j in range(each):
             tile = k * each + j
-            count = min(LANES, plane - j * LANES)
-            rows = pl.ds(pl.multiple_of(k * plane + j * LANES, 64), count)
             real, imag = back_ref[tile, :channels, :], back_ref[tile, channels:, :]
             here = jnp.concatenate([real, imag], 0)
             turn = jnp.concatenate([imag, -real], 0)
@@ -218,13 +258,21 @@
                     for h in range(per_block)
                 ]
                 block = jnp.concatenate(parts, 0).T
-                held_ref[rows, c * wide : c * wide + LANES] = block[:count]
-            copy(k, j).start()
+                for i in range(per_tile):
+                    first = block[i * LENGTH : i * LENGTH + 8]
+                    second = block[i * LENGTH + 8 : (i + 1) * LENGTH]
+                    rows = pl.ds(pl.multiple_of((k * LENGTH + j * per_tile + i) * KY, 8), KY)
+                    held_ref[rows, c * wide : c * wide + LANES] = jnp.concatenate(
+                        [first, jnp.where(low, second, first), second], 0
+                    )
+            for copy in copies(k, j):
+                copy.start()
 
     @pl.loop(0, share)
     def _(k):
         for j in range(each):
-            copy(k, j).wait()
+            for copy in copies(k, j):
+                copy.wait()
 
 
 def slope_kernel(
@@ -275,9 +323,9 @@
     lanes = cells * channels
     wide = 2 * channels
     plane = KX * KY
-    each = -(-plane // LANES)
+    points = cells * devices
+    each = points // LANES
     tiles = share * each
-    points = cells * devices
     slots = devices * SLOTS
     inner = 1.0 / math.sqrt(points * depth)
     outer = 1.0 / math.sqrt(plane * KZ * KT)
@@ -308,7 +356,7 @@
         pltpu.VMEM((tiles, wide, 2 * LANES), jnp.bfloat16),
     ]
     sent, modes_in, turned = pl.pallas_call(
-        functools.partial(mix_kernel, share, channels, plane),
+        functools.partial(mix_kernel, share, channels),
         in_specs=[IN_VMEM] * 4, out_specs=[IN_VMEM] * 3,
         out_shape=[packet, spectra, pltpu.VMEM((tiles, flat, LANES), jnp.bfloat16)],
         scratch_shapes=scratch, compiler_params=params(6), name="mix",
@@ -328,10 +376,12 @@
     )(arrived, on_chip(turned), forward, inverse)
     arrived = exchange(sent)
     grad_spectral = pl.pallas_call(
-        functools.partial(outer_kernel, share, channels, plane),
+        functools.partial(outer_kernel, share, channels),
         in_specs=[IN_VMEM] * 2, out_specs=pl.BlockSpec(memory_space=pl.ANY),
         out_shape=jax.ShapeDtypeStruct((share * plane, flat), jnp.float32),
-        scratch_shapes=[pltpu.VMEM((share * plane, flat), jnp.float32), pltpu.SemaphoreType.DMA((tiles,))],
+        scratch_shapes=[
+            pltpu.VMEM((share * LENGTH * KY, flat), jnp.float32), pltpu.SemaphoreType.DMA((tiles, 2)),
+        ],
         compiler_params=params(24),
         cost_estimate=pl.CostEstimate(
             flops=4 * share * plane * flat * wide, transcendentals=0, bytes_accessed=4 * share * plane * flat
@@ -522,7 +572,7 @@
         cells = inputs.shape[0] * inputs.shape[1] // (count_gx * count_gy)
         whole_modes = KZ * KT % (count_gx * count_gy) == 0
         fits = whole_modes and 2 * KZ * KT // (count_gx * count_gy) <= SLOTS
-        fits = fits and inputs.shape[2] == 32 and cells * inputs.shape[2] == 256
+        fits = fits and inputs.shape[2] == 32 and cells * inputs.shape[2] == 256 and inputs.shape[0] == inputs.shape[1] == LENGTH
         return jax.shard_map(
             per_device if fits else general_per_device,
             mesh=mesh,

time: 57.9 us -> 55.5 us (0.959)
  Pallas kernels: 16.6 us -> 14.3 us
    pallas_call x1, Pallas kernels: 3.92 us -> 2.59 us  [per_device(): pl.pallas_call(functools.partial(adjoint_kernel, share, channels), in_spe...]
    pallas_call x2, Pallas kernels: 9.48 us -> 8.55 us  [the longest x1 5.56 us: per_device(): pl.pallas_call(functools.partial(outer_kernel, share, channels), in_specs...]
where the time goes in v3:
time: 55.5 us; the launch traced here: 55.3 us
  blocking collectives  35 us (63%)
  Pallas kernels  14.3 us (26%)
  waiting for transfers between devices  2.6 us (5%)
  starting transfers between devices  2.58 us (5%)
  between operations  0.74 us (1%)
    all_to_all x3, blocking collectives, exchange(): lax.all_to_all(blocks, GRID_AXES, split_axis=0, concat_axis=0, tiled=True)  35 us
    pallas_call x1, Pallas kernels, per_device(): pl.pallas_call(functools.partial(outer_kernel, share, channels), in_specs...  5.56 us
    pallas_call x1, Pallas kernels, per_device(): pl.pallas_call(functools.partial(mix_kernel, share, channels), in_specs=[...  2.98 us
    all_to_all x1, waiting for transfers between devices, exchange(): lax.all_to_all(blocks, GRID_AXES, split_axis=0, concat_axis=0, tiled=True)  2.6 us
    pallas_call x1, Pallas kernels, per_device(): pl.pallas_call(functools.partial(adjoint_kernel, share, channels), in_spe...  2.59 us
    all_to_all x1, starting transfers between devices, exchange(): lax.all_to_all(blocks, GRID_AXES, split_axis=0, concat_axis=0, tiled=True)  2.58 us
    pallas_call x1, Pallas kernels, per_device(): pl.pallas_call(functools.partial(depth_kernel, inner), in_specs=[IN_VMEM]...  1.44 us
  transfers between devices with their start and end apart: 1, of which 1 were waited for; matrix products, arithmetic and copies ran while one was open for 0% of the time, Pallas kernels for 10%

profile of v3, /device:TPU:0, one launch (start us, length us, event | category | flops | bytes accessed | tf_op | source)
XLA Modules:
  0.0 55.3 jit_solution(7073073519773162720)
XLA Ops:
  0.6 0.0 copy-start
  0.6 0.0 copy-start.2
  0.7 0.0 copy-start.3
  0.7 1.4 %depth.1 = bf16[256,256]{1,0:T(8,128)(2,1)S(1)} custom-call(bf16[256,512]{1,0:T(8,128)(2,1)} %constant.6.clone.table_ref, bf16[256,512]{1,0:T(8,128)(2,1)} %bitcast.18), custom_call_target="tpu_custom_call" | custom-call | flops 99999997952 | tf_op jit(solution)/shard_map/depth/pallas_call | solution.py:347
  2.1 0.0 copy-start.1
  2.1 0.0 copy-start.4
  2.1 0.0 copy-start.5
  2.1 0.0 copy-start.6
  2.2 15.3 %all_to_all.20 = bf16[32,8,256]{2,1,0:T(8,128)(2,1)S(1)} all-to-all(bf16[32,8,256]{2,1,0:T(8,128)(2,1)S(1)} %bitcast.23), channel_id=1, replica_groups=mesh['gx'=4,'gy'=8] {'gx','gy'}, dimensions={0} | all-to-all | bytes 262144 | tf_op jit(solution)/shard_map/all_to_all | solution.py:341
  17.4 0.0 copy-done
  17.4 0.0 copy-done.2
  17.4 0.0 copy-done.3
  17.4 3.0 %mix.1 = (bf16[256,256]{1,0:T(8,128)(2,1)S(1)}, f32[6,64,128]{2,1,0:T(8,128)S(1)}, bf16[6,2048,128]{2,1,0:T(8,128)(2,1)S(1)}) custom-call(bf16[256,256]{1,0:T(8,128)(2,1)S(1)} %bitcast.14, bf16[1728,2048]{1,0:T(8,128)(2,1)S(1)} %bitcast.13, bf16[512,256]{1,0:T(8,128)(2,1)S(1)} %copy-done.3, bf16[256,512]{1,0:T(8,128)(2,1)S(1)} %copy-done.2), custom_call_target="tpu_custom_call" | custom-call | tf_op jit(solution)/shard_map/mix/pallas_call | solution.py:358
  20.4 9.9 %all_to_all.21 = bf16[32,8,256]{2,1,0:T(8,128)(2,1)S(1)} all-to-all(bf16[32,8,256]{2,1,0:T(8,128)(2,1)S(1)} %bitcast.21), channel_id=1, replica_groups=mesh['gx'=4,'gy'=8] {'gx','gy'}, dimensions={0} | all-to-all | bytes 262144 | tf_op jit(solution)/shard_map/all_to_all | solution.py:341
  30.3 0.0 copy-done.1
  30.3 0.0 copy-done.4
  30.3 0.0 copy-done.5
  30.3 0.0 copy-done.6
  30.3 0.7 %slope.1 = (bf16[256,512]{1,0:T(8,128)(2,1)S(1)}, bf16[256,256]{1,0:T(8,128)(2,1)S(1)}) custom-call(bf16[256,256]{1,0:T(8,128)(2,1)S(1)} %bitcast.16, bf16[256,512]{1,0:T(8,128)(2,1)S(1)} %copy-done.1, bf16[256,512]{1,0:T(8,128)(2,1)S(1)} %bitcast.19, bf16[256,512]{1,0:T(8,128)(2,1)S(1)} %bitcast.20, bf16[32,32]{1,0:T(8,128)(2,1)S(1)} %copy-done.6), custom_call_target="tpu_custom_call" | custom-call | tf_op jit(solution)/shard_map/slope/pallas_call | solution.py:365
  31.1 9.9 %all_to_all.22 = bf16[32,8,256]{2,1,0:T(8,128)(2,1)S(1)} all-to-all(bf16[32,8,256]{2,1,0:T(8,128)(2,1)S(1)} %bitcast.22), channel_id=1, replica_groups=mesh['gx'=4,'gy'=8] {'gx','gy'}, dimensions={0} | all-to-all | bytes 262144 | tf_op jit(solution)/shard_map/all_to_all | solution.py:341
  40.9 2.6 %adjoint.1 = (bf16[256,256]{1,0:T(8,128)(2,1)}, f32[6,64,128]{2,1,0:T(8,128)S(1)}) custom-call(bf16[256,256]{1,0:T(8,128)(2,1)S(1)} %bitcast.17, bf16[6,2048,128]{2,1,0:T(8,128)(2,1)S(1)} %get-tuple-element.11.turned_ref, bf16[512,256]{1,0:T(8,128)(2,1)S(1)} %copy-done.3, bf16[256,512]{1,0:T(8,128)(2,1)S(1)} %copy-done.2), custom_call_target="tpu_custom_call" | custom-call | tf_op jit(solution)/shard_map/adjoint/pallas_call | solution.py:371
  43.5 2.6 %all-to-all-start.3 = ((bf16[32,8,256]{2,1,0:T(8,128)(2,1)}), bf16[32,8,256]{2,1,0:T(8,128)(2,1)S(1)}, u32[]{:S(2)}, u32[]{:S(2)}) async-start(bf16[32,8,256]{2,1,0:T(8,128)(2,1)} %bitcast.9), calls=%async_computation.3 | async-start | bytes 262144 | tf_op jit(solution)/shard_map/all_to_all | solution.py:341
  46.1 5.6 %outer.1 = f32[1728,2048]{1,0:T(8,128)} custom-call(f32[6,64,128]{2,1,0:T(8,128)S(1)} %get-tuple-element.14.in_ref, f32[6,64,128]{2,1,0:T(8,128)S(1)} %get-tuple-element.15.back_ref), custom_call_target="tpu_custom_call" | custom-call | flops 905969664 | bytes 14155776 | tf_op jit(solution)/shard_map/outer/pallas_call | solution.py:378
  51.7 2.6 %all-to-all-done.3 = bf16[32,8,256]{2,1,0:T(8,128)(2,1)S(1)} async-done(((bf16[32,8,256]{2,1,0:T(8,128)(2,1)}), bf16[32,8,256]{2,1,0:T(8,128)(2,1)S(1)}, u32[]{:S(2)}, u32[]{:S(2)}) %all-to-all-start.3) | async-done | bytes 131104 | tf_op jit(solution)/shard_map/all_to_all | solution.py:341
  54.3 1.0 %final.1 = bf16[256,512]{1,0:T(8,128)(2,1)} custom-call(bf16[256,256]{1,0:T(8,128)(2,1)S(1)} %bitcast.15, bf16[256,512]{1,0:T(8,128)(2,1)S(1)} %copy-done.1, bf16[256,512]{1,0:T(8,128)(2,1)S(1)} %get-tuple-element.13.slope_ref, bf16[32,32]{1,0:T(8,128)(2,1)S(1)} %copy-done.6), custom_call_target="tpu_custom_call" | custom-call | tf_op jit(solution)/shard_map/final/pallas_call | solution.py:391
Async XLA Ops:
  0.6 16.8 %copy-start = (bf16[72,24,2048]{2,1,0:T(8,128)(2,1)S(1)}, bf16[72,24,2048]{2,1,0:T(8,128)(2,1)}, u32[]{:S(2)}) copy-start(bf16[72,24,2048]{2,1,0:T(8,128)(2,1)} %param.11) | copy-start | bytes 21233668
  0.6 16.8 %copy-start.2 = (bf16[256,512]{1,0:T(8,128)(2,1)S(1)}, bf16[256,512]{1,0:T(8,128)(2,1)}, u32[]{:S(2)}) copy-start(bf16[256,512]{1,0:T(8,128)(2,1)} %constant.8.clone.inverse_ref) | copy-start | bytes 786436
  0.7 16.8 %copy-start.3 = (bf16[512,256]{1,0:T(8,128)(2,1)S(1)}, bf16[512,256]{1,0:T(8,128)(2,1)}, u32[]{:S(2)}) copy-start(bf16[512,256]{1,0:T(8,128)(2,1)} %constant.7.clone.forward_ref) | copy-start | bytes 786436
  2.1 28.2 %copy-start.1 = (bf16[256,512]{1,0:T(8,128)(2,1)S(1)}, bf16[256,512]{1,0:T(8,128)(2,1)}, u32[]{:S(2)}) copy-start(bf16[256,512]{1,0:T(8,128)(2,1)} %constant.6.clone.table_ref) | copy-start | bytes 786436
  2.1 28.2 %copy-start.4 = (bf16[4,2,32,512]{3,2,1,0:T(8,128)(2,1)S(1)}, bf16[4,2,32,512]{3,2,1,0:T(8,128)(2,1)}, u32[]{:S(2)}) copy-start(bf16[4,2,32,512]{3,2,1,0:T(8,128)(2,1)} %param.8) | copy-start | bytes 786436
  2.1 28.2 %copy-start.5 = (bf16[4,2,32,512]{3,2,1,0:T(8,128)(2,1)S(1)}, bf16[4,2,32,512]{3,2,1,0:T(8,128)(2,1)}, u32[]{:S(2)}) copy-start(bf16[4,2,32,512]{3,2,1,0:T(8,128)(2,1)} %param.9) | copy-start | bytes 786436
  2.1 28.2 %copy-start.6 = (bf16[32,32]{1,0:T(8,128)(2,1)S(1)}, bf16[32,32]{1,0:T(8,128)(2,1)}, u32[]{:S(2)}) copy-start(bf16[32,32]{1,0:T(8,128)(2,1)} %point_ref.3) | copy-start | bytes 6148
  43.5 10.8 %all-to-all-start.3 = ((bf16[32,8,256]{2,1,0:T(8,128)(2,1)}), bf16[32,8,256]{2,1,0:T(8,128)(2,1)S(1)}, u32[]{:S(2)}, u32[]{:S(2)}) async-start(bf16[32,8,256]{2,1,0:T(8,128)(2,1)} %bitcast.9), calls=%async_computation.3 | async-start | bytes 262144 | tf_op jit(solution)/shard_map/all_to_all | solution.py:341

commit v4 on v3

--- a/solution.py
+++ b/solution.py
@@ -15,11 +15,9 @@
 KY = 24
 KZ = 12
 KT = 8
-SLOTS = 8
 LANES = 128
 LENGTH = 16
 GROUP = 4
-ROWS = 16
 READ_AHEAD_FLOPS = 10**11
 GRID_AXES = ("gx", "gy")
 
@@ -38,9 +36,8 @@
     ).reshape(NZ * NT, KZ * KT)
     parts = np.stack([np.cos(angles), -np.sin(angles)], -1)
     owners = KZ * KT // share
-    rows = np.zeros((owners, SLOTS, NZ * NT))
-    rows[:, : 2 * share] = parts.reshape(NZ * NT, owners, 2 * share).transpose(1, 2, 0)
-    return rows.reshape(owners * SLOTS, NZ * NT).astype(jnp.bfloat16)
+    rows = parts.reshape(NZ * NT, owners, 2 * share).transpose(2, 1, 0)
+    return rows.reshape(2 * share * owners, NZ * NT).astype(jnp.bfloat16)
 
 
 def plane_tables(count_gx, count_gy, rows_x, rows_y):
@@ -70,63 +67,82 @@
     )
 
 
-def depth_kernel(factor, table_ref, field_ref, sent_ref):
+def unit_rows(unit, wide_ref, units):
+    return pl.ds(unit, wide_ref.shape[0] // units, stride=units)
+
+
+def send_slots(spectra, units, wide_ref, sent_ref):
+    devices = wide_ref.shape[0] // units
+    halves = spectra.shape[1] // LANES
+    for unit in range(units):
+        slot, h = divmod(unit, halves)
+        wide_ref[unit_rows(unit, wide_ref, units), :] = spectra[
+            slot * devices : (slot + 1) * devices, h * LANES : (h + 1) * LANES
+        ]
+    sent_ref[...] = wide_ref[...].astype(jnp.bfloat16)
+
+
+def received_slots(arrived_ref, halves, units, wide_ref):
+    wide_ref[...] = arrived_ref[...].astype(jnp.float32)
+    slots = []
+    for slot in range(units // halves):
+        pieces = [wide_ref[unit_rows(slot * halves + h, wide_ref, units), :] for h in range(halves)]
+        slots.append(jnp.concatenate(pieces, 1))
+    return jnp.concatenate(slots, 0)
+
+
+def depth_kernel(factor, units, table_ref, field_ref, sent_ref, wide_ref):
     spectra = dot(table_ref[...], field_ref[...], 1, 1)
-    sent_ref[...] = (spectra * factor).astype(jnp.bfloat16)
-
-
-def to_plane_modes(share, channels, arrived_ref, forward_ref, wide_ref, modes_ref):
-    halves, rows, lanes = wide_ref.shape
-    devices = rows // SLOTS
-    for h in range(halves):
-        wide_ref[h] = arrived_ref[:, h * LANES : (h + 1) * LANES].astype(jnp.float32)
-    columns = []
+    send_slots(spectra * factor, units, wide_ref, sent_ref)
+
+
+def to_plane_modes(share, channels, halves, arrived_ref, forward_ref, wide_ref, modes_ref):
+    slots = received_slots(arrived_ref, halves, 2 * share * halves, wide_ref)
+    devices = wide_ref.shape[0] // (2 * share * halves)
+    lanes = slots.shape[1]
+    turned = slots.T
+    blocks = []
     for slot in range(2 * share):
-        pieces = []
-        for h in range(halves):
-            piece = wide_ref[h, pl.ds(slot, devices, stride=SLOTS), :]
-            pieces += [piece[:, c * channels : (c + 1) * channels] for c in range(lanes // channels)]
-        columns.append(jnp.concatenate(pieces, 0))
-    cells = jnp.concatenate(columns, 1).T
-    blocks = []
+        pieces = [
+            turned[c * channels : (c + 1) * channels, slot * devices : (slot + 1) * devices]
+            for c in range(lanes // channels)
+        ]
+        blocks.append(jnp.concatenate(pieces, 1))
+    rows = []
     for k in range(share):
-        real = cells[2 * k * channels : (2 * k + 1) * channels]
-        imag = cells[(2 * k + 1) * channels : (2 * k + 2) * channels]
-        blocks += [jnp.concatenate([real, imag], 1), jnp.concatenate([imag, -real], 1)]
-    modes = dot(jnp.concatenate(blocks, 0).astype(jnp.bfloat16), forward_ref[...])
+        real, imag = blocks[2 * k], blocks[2 * k + 1]
+        rows += [jnp.concatenate([real, imag], 1), jnp.concatenate([imag, -real], 1)]
+    modes = dot(jnp.concatenate(rows, 0).astype(jnp.bfloat16), forward_ref[...])
     each = modes_ref.shape[0] // share
     for k in range(share):
         for j in range(each):
             modes_ref[k * each + j] = modes[2 * k * channels : (2 * k + 2) * channels, j * LANES : (j + 1) * LANES]
 
 
-def store_pair(tile, share, channels, real, imag, pair_ref):
+def store_pair(tile, channels, real, imag, pair_ref):
     pair_ref[tile, :channels, :LANES] = real.astype(jnp.bfloat16)
     pair_ref[tile, channels:, :LANES] = imag.astype(jnp.bfloat16)
     pair_ref[tile, :channels, LANES:] = (-imag).astype(jnp.bfloat16)
     pair_ref[tile, channels:, LANES:] = real.astype(jnp.bfloat16)
 
 
-def to_cells(share, channels, pair_ref, inverse_ref, out_ref, sent_ref):
-    halves, rows, lanes = out_ref.shape
-    devices = rows // SLOTS
+def to_cells(share, channels, halves, pair_ref, inverse_ref, wide_ref, sent_ref):
+    units = 2 * share * halves
+    devices = wide_ref.shape[0] // units
     each = pair_ref.shape[0] // share
-    padded = each * LANES
-    out_ref[...] = jnp.zeros_like(out_ref)
     spectra = []
     for k in range(share):
         cosine = jnp.concatenate([pair_ref[k * each + j, :, :LANES] for j in range(each)], 1)
         sine = jnp.concatenate([pair_ref[k * each + j, :, LANES:] for j in range(each)], 1)
         spectra.append(jnp.concatenate([cosine, sine], 1))
     total = dot(inverse_ref[...], jnp.concatenate(spectra, 0), 1, 1)
-    per_half = lanes // channels
-    for slot in range(2 * share):
+    per_half = LANES // channels
+    for unit in range(units):
+        slot, h = divmod(unit, halves)
         columns = slice(slot * channels, (slot + 1) * channels)
-        for h in range(halves):
-            pieces = [total[c * devices : (c + 1) * devices, columns] for c in range(h * per_half, (h + 1) * per_half)]
-            out_ref[h, pl.ds(slot, devices, stride=SLOTS), :] = jnp.concatenate(pieces, 1)
-    for h in range(halves):
-        sent_ref[:, h * LANES : (h + 1) * LANES] = out_ref[h].astype(jnp.bfloat16)
+        pieces = [total[c * devices : (c + 1) * devices, columns] for c in range(h * per_half, (h + 1) * per_half)]
+        wide_ref[unit_rows(unit, wide_ref, units), :] = jnp.concatenate(pieces, 1)
+    sent_ref[...] = wide_ref[...].astype(jnp.bfloat16)
 
 
 def fold_rows(weight_ref, mode, first, count, columns):
@@ -145,10 +161,10 @@
 
 
 def mix_kernel(
-    share, channels, arrived_ref, weight_ref, forward_ref, inverse_ref, sent_ref, modes_ref, turned_ref,
+    share, channels, halves, arrived_ref, weight_ref, forward_ref, inverse_ref, sent_ref, modes_ref, turned_ref,
     wide_ref, pair_ref,
 ):
-    to_plane_modes(share, channels, arrived_ref, forward_ref, wide_ref, modes_ref)
+    to_plane_modes(share, channels, halves, arrived_ref, forward_ref, wide_ref, modes_ref)
     wide = 2 * channels
     each = modes_ref.shape[0] // share
     per_tile = LANES // LENGTH
@@ -177,46 +193,57 @@
                 by_real += real_sum.astype(jnp.float32)
                 by_imag += imag_sum.astype(jnp.float32)
             store_pair(
-                tile, share, channels, by_real[:channels] - by_imag[channels:],
+                tile, channels, by_real[:channels] - by_imag[channels:],
                 by_real[channels:] + by_imag[:channels], pair_ref,
             )
 
-    to_cells(share, channels, pair_ref, inverse_ref, wide_ref, sent_ref)
+    to_cells(share, channels, halves, pair_ref, inverse_ref, wide_ref, sent_ref)
+
+
+def row_sums(blocks):
+    row = lax.broadcasted_iota(jnp.int32, (8, LANES), 0)
+    for shift in (4, 2, 1):
+        merged = []
+        clear = row % (2 * shift) < shift
+        for i in range(shift):
+            first, second = blocks[i], blocks[i + shift]
+            merged.append(
+                jnp.where(clear, first + pltpu.roll(first, 8 - shift, 0), second + pltpu.roll(second, shift, 0))
+            )
+        blocks = merged
+    return blocks[0]
 
 
 def adjoint_kernel(
-    share, channels, arrived_ref, turned_ref, forward_ref, inverse_ref, sent_ref, modes_ref, wide_ref, pair_ref,
-    part_ref,
+    share, channels, halves, arrived_ref, turned_ref, forward_ref, inverse_ref, sent_ref, modes_ref, wide_ref,
+    pair_ref,
 ):
-    to_plane_modes(share, channels, arrived_ref, forward_ref, wide_ref, modes_ref)
+    to_plane_modes(share, channels, halves, arrived_ref, forward_ref, wide_ref, modes_ref)
     wide = 2 * channels
-    tiles = modes_ref.shape[0]
-
-    @pl.loop(0, tiles)
+
+    @pl.loop(0, modes_ref.shape[0])
     def _(tile):
         real, imag = modes_ref[tile, :channels, :], modes_ref[tile, channels:, :]
         here = jnp.concatenate([real, imag], 0).astype(jnp.bfloat16)
         turn = jnp.concatenate([imag, -real], 0).astype(jnp.bfloat16)
-        for c in range(channels):
-            weight = turned_ref[tile, c * wide : (c + 1) * wide, :]
-            for part, factor in enumerate((here, turn)):
-                product = factor * weight
-                while product.shape[0] > ROWS:
-                    half = product.shape[0] // 2
-                    product = product[:half] + product[half:]
-                part_ref[tile, (part * channels + c) * ROWS : (part * channels + c + 1) * ROWS, :] = product
-
-    row = lax.broadcasted_iota(jnp.int32, (wide, ROWS * wide), 0)
-    column = lax.broadcasted_iota(jnp.int32, (wide, ROWS * wide), 1)
-    groups = jnp.where(column // ROWS == row, 1.0, 0.0).astype(jnp.bfloat16)
-    for tile in range(tiles):
-        summed = dot(groups, part_ref[tile])
-        store_pair(tile, share, channels, summed[:channels], summed[channels:], pair_ref)
-
-    to_cells(share, channels, pair_ref, inverse_ref, wide_ref, sent_ref)
-
-
-def outer_kernel(share, channels, in_ref, back_ref, grad_ref, held_ref, sems):
+        sums = ([], [])
+        for first in range(0, channels, 8):
+            blocks = ([], [])
+            for c in range(first, first + 8):
+                weight = turned_ref[tile, c * wide : (c + 1) * wide, :]
+                for part, factor in enumerate((here, turn)):
+                    product = factor * weight
+                    product = product[: wide // 2] + product[wide // 2 :]
+                    product = (product[: wide // 4] + product[wide // 4 :]).astype(jnp.float32)
+                    blocks[part].append(product[:8] + product[8:])
+            for part in range(2):
+                sums[part].append(row_sums(blocks[part]))
+        store_pair(tile, channels, jnp.concatenate(sums[0], 0), jnp.concatenate(sums[1], 0), pair_ref)
+
+    to_cells(share, channels, halves, pair_ref, inverse_ref, wide_ref, sent_ref)
+
+
+def outer_kernel(share, channels, in_ref, back_ref, slope_ref, point_ref, grad_ref, pointwise_ref, held_ref, sems):
     wide = 2 * channels
     each = in_ref.shape[0] // share
     per_block = LANES // wide
@@ -268,6 +295,10 @@
             for copy in copies(k, j):
                 copy.start()
 
+    for first in range(0, slope_ref.shape[0], channels):
+        rows = slice(first, first + channels)
+        pointwise_ref[rows, :] = dot(point_ref[...], slope_ref[rows, :])
+
     @pl.loop(0, share)
     def _(k):
         for j in range(each):
@@ -276,9 +307,11 @@
 
 
 def slope_kernel(
-    cells, channels, factor, arrived_ref, table_ref, field_ref, cotangent_ref, point_ref, slope_ref, sent_ref
+    cells, channels, factor, units, arrived_ref, table_ref, field_ref, cotangent_ref, point_ref, slope_ref, sent_ref,
+    wide_ref,
 ):
-    spectral = dot(arrived_ref[...], table_ref[...], 0, 0)
+    arrived = received_slots(arrived_ref, cells * channels // LANES, units, wide_ref)
+    spectral = dot(arrived.astype(jnp.bfloat16), table_ref[...], 0, 0)
     for c in range(cells):
         rows = slice(c * channels, (c + 1) * channels)
         before = spectral[rows] * factor + dot(point_ref[...], field_ref[rows, :], 0, 0)
@@ -287,15 +320,13 @@
         slope = cotangent_ref[rows, :].astype(jnp.float32) * (cumulative + before * density)
         slope_ref[rows, :] = slope.astype(jnp.bfloat16)
     sent = dot(table_ref[...], slope_ref[...], 1, 1)
-    sent_ref[...] = (sent * factor).astype(jnp.bfloat16)
-
-
-def final_kernel(cells, channels, factor, arrived_ref, table_ref, slope_ref, point_ref, grad_ref):
-    spectral = dot(arrived_ref[...], table_ref[...], 0, 0)
-    for c in range(cells):
-        rows = slice(c * channels, (c + 1) * channels)
-        pointwise = dot(point_ref[...], slope_ref[rows, :])
-        grad_ref[rows, :] = (pointwise + spectral[rows] * factor).astype(jnp.bfloat16)
+    send_slots(sent * factor, units, wide_ref, sent_ref)
+
+
+def final_kernel(factor, halves, units, arrived_ref, table_ref, pointwise_ref, grad_ref, wide_ref):
+    arrived = received_slots(arrived_ref, halves, units, wide_ref)
+    spectral = dot(arrived.astype(jnp.bfloat16), table_ref[...], 0, 0)
+    grad_ref[...] = (pointwise_ref[...] + spectral * factor).astype(jnp.bfloat16)
 
 
 def params(mebibytes, semantics=None):
@@ -326,7 +357,8 @@
     points = cells * devices
     each = points // LANES
     tiles = share * each
-    slots = devices * SLOTS
+    halves = lanes // LANES
+    units = 2 * share * halves
     inner = 1.0 / math.sqrt(points * depth)
     outer = 1.0 / math.sqrt(plane * KZ * KT)
 
@@ -337,48 +369,50 @@
     point = on_chip(point_weight)
 
     def exchange(sent):
-        blocks = sent.reshape(devices, SLOTS, lanes)
+        blocks = sent.reshape(devices * units // 4, 4, LANES)
         arrived = lax.all_to_all(blocks, GRID_AXES, split_axis=0, concat_axis=0, tiled=True)
-        return on_chip(arrived.reshape(slots, lanes))
-
-    packet = pltpu.VMEM((slots, lanes), jnp.bfloat16)
+        return on_chip(arrived.reshape(devices * units, LANES))
+
+    packet = pltpu.VMEM((devices * units, LANES), jnp.bfloat16)
+    unpacked = pltpu.VMEM((devices * units, LANES), jnp.float32)
     spectra = pltpu.VMEM((tiles, wide, LANES), jnp.float32)
 
     sent = pl.pallas_call(
-        functools.partial(depth_kernel, inner), in_specs=[IN_VMEM] * 2, out_specs=IN_VMEM, out_shape=packet,
+        functools.partial(depth_kernel, inner, units),
+        in_specs=[IN_VMEM] * 2, out_specs=IN_VMEM, out_shape=packet, scratch_shapes=[unpacked],
         compiler_params=params(2),
         cost_estimate=pl.CostEstimate(flops=READ_AHEAD_FLOPS, transcendentals=0, bytes_accessed=0),
         name="depth",
     )(off_chip(jnp.asarray(depth_table(share))), off_chip(inputs.reshape(lanes, depth)))
     arrived = exchange(sent)
-    scratch = [
-        pltpu.VMEM((lanes // LANES, slots, LANES), jnp.float32),
-        pltpu.VMEM((tiles, wide, 2 * LANES), jnp.bfloat16),
-    ]
+    scratch = [unpacked, pltpu.VMEM((tiles, wide, 2 * LANES), jnp.bfloat16)]
     sent, modes_in, turned = pl.pallas_call(
-        functools.partial(mix_kernel, share, channels),
+        functools.partial(mix_kernel, share, channels, halves),
         in_specs=[IN_VMEM] * 4, out_specs=[IN_VMEM] * 3,
         out_shape=[packet, spectra, pltpu.VMEM((tiles, flat, LANES), jnp.bfloat16)],
         scratch_shapes=scratch, compiler_params=params(6), name="mix",
     )(arrived, on_chip(spectral_weight.reshape(share * plane, flat)), forward, inverse)
     arrived = exchange(sent)
     slope, sent = pl.pallas_call(
-        functools.partial(slope_kernel, cells, channels, outer),
+        functools.partial(slope_kernel, cells, channels, outer, units),
         in_specs=[IN_VMEM] * 5, out_specs=[IN_VMEM] * 2, out_shape=[pltpu.VMEM((lanes, depth), jnp.bfloat16), packet],
+        scratch_shapes=[unpacked],
         compiler_params=params(8), name="slope",
     )(arrived, table, field, seed, point)
     arrived = exchange(sent)
     sent, modes_back = pl.pallas_call(
-        functools.partial(adjoint_kernel, share, channels),
+        functools.partial(adjoint_kernel, share, channels, halves),
         in_specs=[IN_VMEM] * 4, out_specs=[IN_VMEM] * 2, out_shape=[packet, spectra],
-        scratch_shapes=scratch + [pltpu.VMEM((tiles, ROWS * wide, LANES), jnp.bfloat16)],
+        scratch_shapes=scratch,
         compiler_params=params(12), name="adjoint",
     )(arrived, on_chip(turned), forward, inverse)
     arrived = exchange(sent)
-    grad_spectral = pl.pallas_call(
+    grad_spectral, pointwise = pl.pallas_call(
         functools.partial(outer_kernel, share, channels),
-        in_specs=[IN_VMEM] * 2, out_specs=pl.BlockSpec(memory_space=pl.ANY),
-        out_shape=jax.ShapeDtypeStruct((share * plane, flat), jnp.float32),
+        in_specs=[IN_VMEM] * 4, out_specs=[pl.BlockSpec(memory_space=pl.ANY), IN_VMEM],
+        out_shape=[
+            jax.ShapeDtypeStruct((share * plane, flat), jnp.float32), pltpu.VMEM((lanes, depth), jnp.float32),
+        ],
         scratch_shapes=[
             pltpu.VMEM((share * LENGTH * KY, flat), jnp.float32), pltpu.SemaphoreType.DMA((tiles, 2)),
         ],
@@ -387,12 +421,13 @@
             flops=4 * share * plane * flat * wide, transcendentals=0, bytes_accessed=4 * share * plane * flat
         ),
         name="outer",
-    )(on_chip(modes_in), on_chip(modes_back))
+    )(on_chip(modes_in), on_chip(modes_back), on_chip(slope), point)
     grad_input = pl.pallas_call(
-        functools.partial(final_kernel, cells, channels, inner),
-        in_specs=[IN_VMEM] * 4, out_specs=IN_VMEM, out_shape=jax.ShapeDtypeStruct((lanes, depth), jnp.bfloat16),
+        functools.partial(final_kernel, inner, halves, units),
+        in_specs=[IN_VMEM] * 3, out_specs=IN_VMEM, out_shape=jax.ShapeDtypeStruct((lanes, depth), jnp.bfloat16),
+        scratch_shapes=[unpacked],
         compiler_params=params(8), name="final",
-    )(arrived, table, on_chip(slope), point)
+    )(arrived, table, on_chip(pointwise))
     return grad_input.reshape(inputs.shape), grad_spectral.reshape(spectral_weight.shape)
 
 
@@ -571,7 +606,7 @@
     def program(inputs, cotangent, point_weight, spectral_weight):
         cells = inputs.shape[0] * inputs.shape[1] // (count_gx * count_gy)
         whole_modes = KZ * KT % (count_gx * count_gy) == 0
-        fits = whole_modes and 2 * KZ * KT // (count_gx * count_gy) <= SLOTS
+        fits = whole_modes and KZ * KT // (count_gx * count_gy) == 3
         fits = fits and inputs.shape[2] == 32 and cells * inputs.shape[2] == 256 and inputs.shape[0] == inputs.shape[1] == LENGTH
         return jax.shard_map(
             per_device if fits else general_per_device,

time: 55.5 us -> 53.4 us (0.962)
  blocking collectives: 35 us -> 33.8 us
    all_to_all x3, blocking collectives: 35 us -> 33.8 us  [exchange(): lax.all_to_all(blocks, GRID_AXES, split_axis=0, concat_axis=0, tiled=True)]
where the time goes in v4:
time: 53.4 us; the launch traced here: 53.2 us
  blocking collectives  33.8 us (63%)
  Pallas kernels  13.8 us (26%)
  starting transfers between devices  2.57 us (5%)
  waiting for transfers between devices  2.21 us (4%)
  between operations  0.74 us (1%)
    all_to_all x3, blocking collectives, exchange(): lax.all_to_all(blocks, GRID_AXES, split_axis=0, concat_axis=0, tiled=True)  33.8 us
    pallas_call x1, Pallas kernels, per_device(): pl.pallas_call(functools.partial(outer_kernel, share, channels), in_specs...  5.57 us
    pallas_call x1, Pallas kernels, per_device(): pl.pallas_call(functools.partial(mix_kernel, share, channels, halves), in...  2.8 us
    all_to_all x1, starting transfers between devices, exchange(): lax.all_to_all(blocks, GRID_AXES, split_axis=0, concat_axis=0, tiled=True)  2.57 us
    pallas_call x1, Pallas kernels, per_device(): pl.pallas_call(functools.partial(adjoint_kernel, share, channels, halves)...  2.28 us
    all_to_all x1, waiting for transfers between devices, exchange(): lax.all_to_all(blocks, GRID_AXES, split_axis=0, concat_axis=0, tiled=True)  2.21 us
    pallas_call x1, Pallas kernels, per_device(): pl.pallas_call(functools.partial(depth_kernel, inner, units), in_specs=[I...  1.45 us
  transfers between devices with their start and end apart: 1, of which 1 were waited for; matrix products, arithmetic and copies ran while one was open for 0% of the time, Pallas kernels for 10%

profile of v4, /device:TPU:0, one launch (start us, length us, event | category | flops | bytes accessed | tf_op | source)
XLA Modules:
  0.0 53.2 jit_solution(16618308041052599397)
XLA Ops:
  0.6 0.0 copy-start
  0.6 0.0 copy-start.1
  0.7 0.0 copy-start.2
  0.7 1.4 %depth.1 = bf16[384,128]{1,0:T(8,128)(2,1)S(1)} custom-call(bf16[192,512]{1,0:T(8,128)(2,1)} %constant.6.clone.table_ref, bf16[256,512]{1,0:T(8,128)(2,1)} %bitcast.18), custom_call_target="tpu_custom_call" | custom-call | flops 99999997952 | tf_op jit(solution)/shard_map/depth/pallas_call | solution.py:380
  2.1 0.0 copy-start.3
  2.1 0.0 copy-start.4
  2.1 0.0 copy-start.5
  2.2 0.0 copy-start.6
  2.2 14.9 %all_to_all.20 = bf16[96,4,128]{2,1,0:T(4,128)(2,1)S(1)} all-to-all(bf16[96,4,128]{2,1,0:T(4,128)(2,1)S(1)} %bitcast.23), channel_id=1, replica_groups=mesh['gx'=4,'gy'=8] {'gx','gy'}, dimensions={0} | all-to-all | bytes 196608 | tf_op jit(solution)/shard_map/all_to_all | solution.py:373
  17.1 0.0 copy-done
  17.1 0.0 copy-done.1
  17.1 0.0 copy-done.2
  17.1 2.8 %mix.1 = (bf16[384,128]{1,0:T(8,128)(2,1)S(1)}, f32[6,64,128]{2,1,0:T(8,128)S(1)}, bf16[6,2048,128]{2,1,0:T(8,128)(2,1)S(1)}) custom-call(bf16[384,128]{1,0:T(8,128)(2,1)S(1)} %bitcast.14, bf16[1728,2048]{1,0:T(8,128)(2,1)S(1)} %bitcast.13, bf16[512,256]{1,0:T(8,128)(2,1)S(1)} %copy-done.2, bf16[256,512]{1,0:T(8,128)(2,1)S(1)} %copy-done.1), custom_call_target="tpu_custom_call" | custom-call | tf_op jit(solution)/shard_map/mix/pallas_call | solution.py:389
  19.9 9.5 %all_to_all.21 = bf16[96,4,128]{2,1,0:T(4,128)(2,1)S(1)} all-to-all(bf16[96,4,128]{2,1,0:T(4,128)(2,1)S(1)} %bitcast.21), channel_id=1, replica_groups=mesh['gx'=4,'gy'=8] {'gx','gy'}, dimensions={0} | all-to-all | bytes 196608 | tf_op jit(solution)/shard_map/all_to_all | solution.py:373
  29.3 0.0 copy-done.3
  29.3 0.0 copy-done.4
  29.3 0.0 copy-done.5
  29.4 0.0 copy-done.6
  29.4 0.7 %slope.1 = (bf16[256,512]{1,0:T(8,128)(2,1)S(1)}, bf16[384,128]{1,0:T(8,128)(2,1)S(1)}) custom-call(bf16[384,128]{1,0:T(8,128)(2,1)S(1)} %bitcast.16, bf16[192,512]{1,0:T(8,128)(2,1)S(1)} %copy-done.3, bf16[256,512]{1,0:T(8,128)(2,1)S(1)} %bitcast.19, bf16[256,512]{1,0:T(8,128)(2,1)S(1)} %bitcast.20, bf16[32,32]{1,0:T(8,128)(2,1)S(1)} %copy-done.6), custom_call_target="tpu_custom_call" | custom-call | tf_op jit(solution)/shard_map/slope/pallas_call | solution.py:396
  30.1 9.5 %all_to_all.22 = bf16[96,4,128]{2,1,0:T(4,128)(2,1)S(1)} all-to-all(bf16[96,4,128]{2,1,0:T(4,128)(2,1)S(1)} %bitcast.22), channel_id=1, replica_groups=mesh['gx'=4,'gy'=8] {'gx','gy'}, dimensions={0} | all-to-all | bytes 196608 | tf_op jit(solution)/shard_map/all_to_all | solution.py:373
  39.6 2.3 %adjoint.1 = (bf16[384,128]{1,0:T(8,128)(2,1)}, f32[6,64,128]{2,1,0:T(8,128)S(1)}) custom-call(bf16[384,128]{1,0:T(8,128)(2,1)S(1)} %bitcast.17, bf16[6,2048,128]{2,1,0:T(8,128)(2,1)S(1)} %get-tuple-element.13.turned_ref, bf16[512,256]{1,0:T(8,128)(2,1)S(1)} %copy-done.2, bf16[256,512]{1,0:T(8,128)(2,1)S(1)} %copy-done.1), custom_call_target="tpu_custom_call" | custom-call | tf_op jit(solution)/shard_map/adjoint/pallas_call | solution.py:403
  41.9 2.6 %all-to-all-start.3 = ((bf16[96,4,128]{2,1,0:T(4,128)(2,1)}), bf16[96,4,128]{2,1,0:T(4,128)(2,1)S(1)}, u32[]{:S(2)}, u32[]{:S(2)}) async-start(bf16[96,4,128]{2,1,0:T(4,128)(2,1)} %bitcast.9), calls=%async_computation.3 | async-start | bytes 196608 | tf_op jit(solution)/shard_map/all_to_all | solution.py:373
  44.4 5.6 %outer.1 = (f32[1728,2048]{1,0:T(8,128)}, f32[256,512]{1,0:T(8,128)S(1)}) custom-call(f32[6,64,128]{2,1,0:T(8,128)S(1)} %get-tuple-element.15.in_ref, f32[6,64,128]{2,1,0:T(8,128)S(1)} %get-tuple-element.16.back_ref, bf16[256,512]{1,0:T(8,128)(2,1)S(1)} %get-tuple-element.17.slope_ref, bf16[32,32]{1,0:T(8,128)(2,1)S(1)} %copy-done.6), custom_call_target="tpu_custom_call" | custom-call | flops 905969664 | bytes 14155776 | tf_op jit(solution)/shard_map/outer/pallas_call | solution.py:410
  50.0 2.2 %all-to-all-done.3 = bf16[96,4,128]{2,1,0:T(4,128)(2,1)S(1)} async-done(((bf16[96,4,128]{2,1,0:T(4,128)(2,1)}), bf16[96,4,128]{2,1,0:T(4,128)(2,1)S(1)}, u32[]{:S(2)}, u32[]{:S(2)}) %all-to-all-start.3) | async-done | bytes 98336 | tf_op jit(solution)/shard_map/all_to_all | solution.py:373
  52.2 1.0 %final.1 = bf16[256,512]{1,0:T(8,128)(2,1)} custom-call(bf16[384,128]{1,0:T(8,128)(2,1)S(1)} %bitcast.15, bf16[192,512]{1,0:T(8,128)(2,1)S(1)} %copy-done.3, f32[256,512]{1,0:T(8,128)S(1)} %get-tuple-element.18.pointwise_ref), custom_call_target="tpu_custom_call" | custom-call | tf_op jit(solution)/shard_map/final/pallas_call | solution.py:425
Async XLA Ops:
  0.6 16.4 %copy-start = (bf16[72,24,2048]{2,1,0:T(8,128)(2,1)S(1)}, bf16[72,24,2048]{2,1,0:T(8,128)(2,1)}, u32[]{:S(2)}) copy-start(bf16[72,24,2048]{2,1,0:T(8,128)(2,1)} %param.11) | copy-start | bytes 21233668
  0.6 16.4 %copy-start.1 = (bf16[256,512]{1,0:T(8,128)(2,1)S(1)}, bf16[256,512]{1,0:T(8,128)(2,1)}, u32[]{:S(2)}) copy-start(bf16[256,512]{1,0:T(8,128)(2,1)} %constant.8.clone.inverse_ref) | copy-start | bytes 786436
  0.7 16.4 %copy-start.2 = (bf16[512,256]{1,0:T(8,128)(2,1)S(1)}, bf16[512,256]{1,0:T(8,128)(2,1)}, u32[]{:S(2)}) copy-start(bf16[512,256]{1,0:T(8,128)(2,1)} %constant.7.clone.forward_ref) | copy-start | bytes 786436
  2.1 27.2 %copy-start.3 = (bf16[192,512]{1,0:T(8,128)(2,1)S(1)}, bf16[192,512]{1,0:T(8,128)(2,1)}, u32[]{:S(2)}) copy-start(bf16[192,512]{1,0:T(8,128)(2,1)} %constant.6.clone.table_ref) | copy-start | bytes 589828
  2.1 27.2 %copy-start.4 = (bf16[4,2,32,512]{3,2,1,0:T(8,128)(2,1)S(1)}, bf16[4,2,32,512]{3,2,1,0:T(8,128)(2,1)}, u32[]{:S(2)}) copy-start(bf16[4,2,32,512]{3,2,1,0:T(8,128)(2,1)} %param.8) | copy-start | bytes 786436
  2.1 27.2 %copy-start.5 = (bf16[4,2,32,512]{3,2,1,0:T(8,128)(2,1)S(1)}, bf16[4,2,32,512]{3,2,1,0:T(8,128)(2,1)}, u32[]{:S(2)}) copy-start(bf16[4,2,32,512]{3,2,1,0:T(8,128)(2,1)} %param.9) | copy-start | bytes 786436
  2.2 27.2 %copy-start.6 = (bf16[32,32]{1,0:T(8,128)(2,1)S(1)}, bf16[32,32]{1,0:T(8,128)(2,1)}, u32[]{:S(2)}) copy-start(bf16[32,32]{1,0:T(8,128)(2,1)} %point_ref.3) | copy-start | bytes 6148
  41.9 10.4 %all-to-all-start.3 = ((bf16[96,4,128]{2,1,0:T(4,128)(2,1)}), bf16[96,4,128]{2,1,0:T(4,128)(2,1)S(1)}, u32[]{:S(2)}, u32[]{:S(2)}) async-start(bf16[96,4,128]{2,1,0:T(4,128)(2,1)} %bitcast.9), calls=%async_computation.3 | async-start | bytes 196608 | tf_op jit(solution)/shard_map/all_to_all | solution.py:373

commit v5 on v4

--- a/solution.py
+++ b/solution.py
@@ -100,7 +100,7 @@
     slots = received_slots(arrived_ref, halves, 2 * share * halves, wide_ref)
     devices = wide_ref.shape[0] // (2 * share * halves)
     lanes = slots.shape[1]
-    turned = slots.T
+    turned = slots.astype(jnp.bfloat16).T
     blocks = []
     for slot in range(2 * share):
         pieces = [
@@ -112,7 +112,7 @@
     for k in range(share):
         real, imag = blocks[2 * k], blocks[2 * k + 1]
         rows += [jnp.concatenate([real, imag], 1), jnp.concatenate([imag, -real], 1)]
-    modes = dot(jnp.concatenate(rows, 0).astype(jnp.bfloat16), forward_ref[...])
+    modes = dot(jnp.concatenate(rows, 0), forward_ref[...])
     each = modes_ref.shape[0] // share
     for k in range(share):
         for j in range(each):
@@ -147,17 +147,17 @@
 
 def fold_rows(weight_ref, mode, first, count, columns):
     row = lax.broadcasted_iota(jnp.int32, (8, LANES), 0)
-    low = jnp.where(row < 4, 1.0, 0.0)
-    high = 1.0 - low
+    low = jnp.where(row < 4, 1.0, 0.0).astype(jnp.bfloat16)
+    high = jnp.bfloat16(1) - low
     folded = []
     for residue in range(first, first + count):
         total = None
         for kx in modes_of(residue):
             rows = pl.ds(pl.multiple_of((mode * KX + kx) * KY, 8), KY)
-            block = weight_ref[rows, columns].astype(jnp.float32)
+            block = weight_ref[rows, columns]
             total = block if total is None else total + block
         folded += [total[:8] + high * total[8:16], total[16:] + low * total[8:16]]
-    return jnp.concatenate(folded, 0).astype(jnp.bfloat16)
+    return jnp.concatenate(folded, 0)
 
 
 def mix_kernel(
@@ -169,8 +169,7 @@
     each = modes_ref.shape[0] // share
     per_tile = LANES // LENGTH
 
-    @pl.loop(0, share)
-    def _(k):
+    for k in range(share):
         for j in range(each):
             tile = k * each + j
             by_real = jnp.zeros((wide, LANES), jnp.float32)
@@ -221,8 +220,7 @@
     to_plane_modes(share, channels, halves, arrived_ref, forward_ref, wide_ref, modes_ref)
     wide = 2 * channels
 
-    @pl.loop(0, modes_ref.shape[0])
-    def _(tile):
+    for tile in range(modes_ref.shape[0]):
         real, imag = modes_ref[tile, :channels, :], modes_ref[tile, channels:, :]
         here = jnp.concatenate([real, imag], 0).astype(jnp.bfloat16)
         turn = jnp.concatenate([imag, -real], 0).astype(jnp.bfloat16)

time: 53.4 us -> 52.8 us (0.989)
  Pallas kernels: 13.8 us -> 13.2 us
  transfers between devices with their start and end apart: 1 -> 1, of which waited for: 1 -> 1; matrix products, arithmetic and copies ran while one was open for 0% -> 0% of each run, Pallas kernels for 10% -> 11%
where the time goes in v5:
time: 52.8 us; the launch traced here: 52.6 us
  blocking collectives  33.8 us (64%)
  Pallas kernels  13.2 us (25%)
  starting transfers between devices  2.57 us (5%)
  waiting for transfers between devices  2.21 us (4%)
  between operations  0.74 us (1%)
    all_to_all x3, blocking collectives, exchange(): lax.all_to_all(blocks, GRID_AXES, split_axis=0, concat_axis=0, tiled=True)  33.8 us
    pallas_call x1, Pallas kernels, per_device(): pl.pallas_call(functools.partial(outer_kernel, share, channels), in_specs...  5.57 us
    all_to_all x1, starting transfers between devices, exchange(): lax.all_to_all(blocks, GRID_AXES, split_axis=0, concat_axis=0, tiled=True)  2.57 us
    pallas_call x1, Pallas kernels, per_device(): pl.pallas_call(functools.partial(mix_kernel, share, channels, halves), in...  2.29 us
    all_to_all x1, waiting for transfers between devices, exchange(): lax.all_to_all(blocks, GRID_AXES, split_axis=0, concat_axis=0, tiled=True)  2.21 us
    pallas_call x1, Pallas kernels, per_device(): pl.pallas_call(functools.partial(adjoint_kernel, share, channels, halves)...  2.17 us
    pallas_call x1, Pallas kernels, per_device(): pl.pallas_call(functools.partial(depth_kernel, inner, units), in_specs=[I...  1.45 us
  transfers between devices with their start and end apart: 1, of which 1 were waited for; matrix products, arithmetic and copies ran while one was open for 0% of the time, Pallas kernels for 11%

profile of v5, /device:TPU:0, one launch (start us, length us, event | category | flops | bytes accessed | tf_op | source)
XLA Modules:
  0.0 52.6 jit_solution(13267663058075752141)
XLA Ops:
  0.6 0.0 copy-start
  0.6 0.0 copy-start.1
  0.7 0.0 copy-start.2
  0.7 1.4 %depth.1 = bf16[384,128]{1,0:T(8,128)(2,1)S(1)} custom-call(bf16[192,512]{1,0:T(8,128)(2,1)} %constant.6.clone.table_ref, bf16[256,512]{1,0:T(8,128)(2,1)} %bitcast.18), custom_call_target="tpu_custom_call" | custom-call | flops 99999997952 | tf_op jit(solution)/shard_map/depth/pallas_call | solution.py:378
  2.1 0.0 copy-start.3
  2.1 0.0 copy-start.4
  2.1 0.0 copy-start.5
  2.2 0.0 copy-start.6
  2.2 14.9 %all_to_all.20 = bf16[96,4,128]{2,1,0:T(4,128)(2,1)S(1)} all-to-all(bf16[96,4,128]{2,1,0:T(4,128)(2,1)S(1)} %bitcast.23), channel_id=1, replica_groups=mesh['gx'=4,'gy'=8] {'gx','gy'}, dimensions={0} | all-to-all | bytes 196608 | tf_op jit(solution)/shard_map/all_to_all | solution.py:371
  17.1 0.0 copy-done
  17.1 0.0 copy-done.1
  17.1 0.0 copy-done.2
  17.1 2.3 %mix.1 = (bf16[384,128]{1,0:T(8,128)(2,1)S(1)}, f32[6,64,128]{2,1,0:T(8,128)S(1)}, bf16[6,2048,128]{2,1,0:T(8,128)(2,1)S(1)}) custom-call(bf16[384,128]{1,0:T(8,128)(2,1)S(1)} %bitcast.14, bf16[1728,2048]{1,0:T(8,128)(2,1)S(1)} %bitcast.13, bf16[512,256]{1,0:T(8,128)(2,1)S(1)} %copy-done.2, bf16[256,512]{1,0:T(8,128)(2,1)S(1)} %copy-done.1), custom_call_target="tpu_custom_call" | custom-call | tf_op jit(solution)/shard_map/mix/pallas_call | solution.py:387
  19.4 9.5 %all_to_all.21 = bf16[96,4,128]{2,1,0:T(4,128)(2,1)S(1)} all-to-all(bf16[96,4,128]{2,1,0:T(4,128)(2,1)S(1)} %bitcast.21), channel_id=1, replica_groups=mesh['gx'=4,'gy'=8] {'gx','gy'}, dimensions={0} | all-to-all | bytes 196608 | tf_op jit(solution)/shard_map/all_to_all | solution.py:371
  28.8 0.0 copy-done.3
  28.8 0.0 copy-done.4
  28.8 0.0 copy-done.5
  28.8 0.0 copy-done.6
  28.8 0.7 %slope.1 = (bf16[256,512]{1,0:T(8,128)(2,1)S(1)}, bf16[384,128]{1,0:T(8,128)(2,1)S(1)}) custom-call(bf16[384,128]{1,0:T(8,128)(2,1)S(1)} %bitcast.16, bf16[192,512]{1,0:T(8,128)(2,1)S(1)} %copy-done.3, bf16[256,512]{1,0:T(8,128)(2,1)S(1)} %bitcast.19, bf16[256,512]{1,0:T(8,128)(2,1)S(1)} %bitcast.20, bf16[32,32]{1,0:T(8,128)(2,1)S(1)} %copy-done.6), custom_call_target="tpu_custom_call" | custom-call | tf_op jit(solution)/shard_map/slope/pallas_call | solution.py:394
  29.6 9.5 %all_to_all.22 = bf16[96,4,128]{2,1,0:T(4,128)(2,1)S(1)} all-to-all(bf16[96,4,128]{2,1,0:T(4,128)(2,1)S(1)} %bitcast.22), channel_id=1, replica_groups=mesh['gx'=4,'gy'=8] {'gx','gy'}, dimensions={0} | all-to-all | bytes 196608 | tf_op jit(solution)/shard_map/all_to_all | solution.py:371
  39.1 2.2 %adjoint.1 = (bf16[384,128]{1,0:T(8,128)(2,1)}, f32[6,64,128]{2,1,0:T(8,128)S(1)}) custom-call(bf16[384,128]{1,0:T(8,128)(2,1)S(1)} %bitcast.17, bf16[6,2048,128]{2,1,0:T(8,128)(2,1)S(1)} %get-tuple-element.13.turned_ref, bf16[512,256]{1,0:T(8,128)(2,1)S(1)} %copy-done.2, bf16[256,512]{1,0:T(8,128)(2,1)S(1)} %copy-done.1), custom_call_target="tpu_custom_call" | custom-call | tf_op jit(solution)/shard_map/adjoint/pallas_call | solution.py:401
  41.2 2.6 %all-to-all-start.3 = ((bf16[96,4,128]{2,1,0:T(4,128)(2,1)}), bf16[96,4,128]{2,1,0:T(4,128)(2,1)S(1)}, u32[]{:S(2)}, u32[]{:S(2)}) async-start(bf16[96,4,128]{2,1,0:T(4,128)(2,1)} %bitcast.9), calls=%async_computation.3 | async-start | bytes 196608 | tf_op jit(solution)/shard_map/all_to_all | solution.py:371
  43.8 5.6 %outer.1 = (f32[1728,2048]{1,0:T(8,128)}, f32[256,512]{1,0:T(8,128)S(1)}) custom-call(f32[6,64,128]{2,1,0:T(8,128)S(1)} %get-tuple-element.15.in_ref, f32[6,64,128]{2,1,0:T(8,128)S(1)} %get-tuple-element.16.back_ref, bf16[256,512]{1,0:T(8,128)(2,1)S(1)} %get-tuple-element.17.slope_ref, bf16[32,32]{1,0:T(8,128)(2,1)S(1)} %copy-done.6), custom_call_target="tpu_custom_call" | custom-call | flops 905969664 | bytes 14155776 | tf_op jit(solution)/shard_map/outer/pallas_call | solution.py:408
  49.4 2.2 %all-to-all-done.3 = bf16[96,4,128]{2,1,0:T(4,128)(2,1)S(1)} async-done(((bf16[96,4,128]{2,1,0:T(4,128)(2,1)}), bf16[96,4,128]{2,1,0:T(4,128)(2,1)S(1)}, u32[]{:S(2)}, u32[]{:S(2)}) %all-to-all-start.3) | async-done | bytes 98336 | tf_op jit(solution)/shard_map/all_to_all | solution.py:371
  51.6 1.0 %final.1 = bf16[256,512]{1,0:T(8,128)(2,1)} custom-call(bf16[384,128]{1,0:T(8,128)(2,1)S(1)} %bitcast.15, bf16[192,512]{1,0:T(8,128)(2,1)S(1)} %copy-done.3, f32[256,512]{1,0:T(8,128)S(1)} %get-tuple-element.18.pointwise_ref), custom_call_target="tpu_custom_call" | custom-call | tf_op jit(solution)/shard_map/final/pallas_call | solution.py:423
Async XLA Ops:
  0.6 16.4 %copy-start = (bf16[72,24,2048]{2,1,0:T(8,128)(2,1)S(1)}, bf16[72,24,2048]{2,1,0:T(8,128)(2,1)}, u32[]{:S(2)}) copy-start(bf16[72,24,2048]{2,1,0:T(8,128)(2,1)} %param.11) | copy-start | bytes 21233668
  0.6 16.4 %copy-start.1 = (bf16[256,512]{1,0:T(8,128)(2,1)S(1)}, bf16[256,512]{1,0:T(8,128)(2,1)}, u32[]{:S(2)}) copy-start(bf16[256,512]{1,0:T(8,128)(2,1)} %constant.8.clone.inverse_ref) | copy-start | bytes 786436
  0.7 16.4 %copy-start.2 = (bf16[512,256]{1,0:T(8,128)(2,1)S(1)}, bf16[512,256]{1,0:T(8,128)(2,1)}, u32[]{:S(2)}) copy-start(bf16[512,256]{1,0:T(8,128)(2,1)} %constant.7.clone.forward_ref) | copy-start | bytes 786436
  2.1 26.7 %copy-start.3 = (bf16[192,512]{1,0:T(8,128)(2,1)S(1)}, bf16[192,512]{1,0:T(8,128)(2,1)}, u32[]{:S(2)}) copy-start(bf16[192,512]{1,0:T(8,128)(2,1)} %constant.6.clone.table_ref) | copy-start | bytes 589828
  2.1 26.7 %copy-start.4 = (bf16[4,2,32,512]{3,2,1,0:T(8,128)(2,1)S(1)}, bf16[4,2,32,512]{3,2,1,0:T(8,128)(2,1)}, u32[]{:S(2)}) copy-start(bf16[4,2,32,512]{3,2,1,0:T(8,128)(2,1)} %param.8) | copy-start | bytes 786436
  2.1 26.7 %copy-start.5 = (bf16[4,2,32,512]{3,2,1,0:T(8,128)(2,1)S(1)}, bf16[4,2,32,512]{3,2,1,0:T(8,128)(2,1)}, u32[]{:S(2)}) copy-start(bf16[4,2,32,512]{3,2,1,0:T(8,128)(2,1)} %param.9) | copy-start | bytes 786436
  2.2 26.7 %copy-start.6 = (bf16[32,32]{1,0:T(8,128)(2,1)S(1)}, bf16[32,32]{1,0:T(8,128)(2,1)}, u32[]{:S(2)}) copy-start(bf16[32,32]{1,0:T(8,128)(2,1)} %point_ref.3) | copy-start | bytes 6148
  41.2 10.4 %all-to-all-start.3 = ((bf16[96,4,128]{2,1,0:T(4,128)(2,1)}), bf16[96,4,128]{2,1,0:T(4,128)(2,1)S(1)}, u32[]{:S(2)}, u32[]{:S(2)}) async-start(bf16[96,4,128]{2,1,0:T(4,128)(2,1)} %bitcast.9), calls=%async_computation.3 | async-start | bytes 196608 | tf_op jit(solution)/shard_map/all_to_all | solution.py:371

commit v6 on v5

--- a/solution.py
+++ b/solution.py
@@ -18,7 +18,7 @@
 LANES = 128
 LENGTH = 16
 GROUP = 4
-READ_AHEAD_FLOPS = 10**11
+READ_AHEAD_FLOPS = 10**10
 GRID_AXES = ("gx", "gy")
 
 
@@ -126,29 +126,24 @@
     pair_ref[tile, channels:, LANES:] = real.astype(jnp.bfloat16)
 
 
-def to_cells(share, channels, halves, pair_ref, inverse_ref, wide_ref, sent_ref):
+def to_cells(k, share, channels, halves, pair_ref, inverse_ref, out_ref):
     units = 2 * share * halves
-    devices = wide_ref.shape[0] // units
+    devices = out_ref.shape[0] // units
     each = pair_ref.shape[0] // share
-    spectra = []
-    for k in range(share):
-        cosine = jnp.concatenate([pair_ref[k * each + j, :, :LANES] for j in range(each)], 1)
-        sine = jnp.concatenate([pair_ref[k * each + j, :, LANES:] for j in range(each)], 1)
-        spectra.append(jnp.concatenate([cosine, sine], 1))
-    total = dot(inverse_ref[...], jnp.concatenate(spectra, 0), 1, 1)
+    cosine = jnp.concatenate([pair_ref[k * each + j, :, :LANES] for j in range(each)], 1)
+    sine = jnp.concatenate([pair_ref[k * each + j, :, LANES:] for j in range(each)], 1)
+    total = dot(inverse_ref[...], jnp.concatenate([cosine, sine], 1), 1, 1)
     per_half = LANES // channels
-    for unit in range(units):
-        slot, h = divmod(unit, halves)
-        columns = slice(slot * channels, (slot + 1) * channels)
-        pieces = [total[c * devices : (c + 1) * devices, columns] for c in range(h * per_half, (h + 1) * per_half)]
-        wide_ref[unit_rows(unit, wide_ref, units), :] = jnp.concatenate(pieces, 1)
-    sent_ref[...] = wide_ref[...].astype(jnp.bfloat16)
+    for part in range(2):
+        columns = slice(part * channels, (part + 1) * channels)
+        for h in range(halves):
+            pieces = [total[c * devices : (c + 1) * devices, columns] for c in range(h * per_half, (h + 1) * per_half)]
+            unit = (2 * k + part) * halves + h
+            out_ref[unit_rows(unit, out_ref, units), :] = jnp.concatenate(pieces, 1)
 
 
 def fold_rows(weight_ref, mode, first, count, columns):
     row = lax.broadcasted_iota(jnp.int32, (8, LANES), 0)
-    low = jnp.where(row < 4, 1.0, 0.0).astype(jnp.bfloat16)
-    high = jnp.bfloat16(1) - low
     folded = []
     for residue in range(first, first + count):
         total = None
@@ -156,13 +151,13 @@
             rows = pl.ds(pl.multiple_of((mode * KX + kx) * KY, 8), KY)
             block = weight_ref[rows, columns]
             total = block if total is None else total + block
-        folded += [total[:8] + high * total[8:16], total[16:] + low * total[8:16]]
+        folded += [total[:8] + jnp.where(row < 4, jnp.bfloat16(0), total[8:16]), total[16:] + jnp.where(row < 4, total[8:16], jnp.bfloat16(0))]
     return jnp.concatenate(folded, 0)
 
 
 def mix_kernel(
     share, channels, halves, arrived_ref, weight_ref, forward_ref, inverse_ref, sent_ref, modes_ref, turned_ref,
-    wide_ref, pair_ref,
+    wide_ref, out_ref, pair_ref,
 ):
     to_plane_modes(share, channels, halves, arrived_ref, forward_ref, wide_ref, modes_ref)
     wide = 2 * channels
@@ -195,8 +190,9 @@
                 tile, channels, by_real[:channels] - by_imag[channels:],
                 by_real[channels:] + by_imag[:channels], pair_ref,
             )
-
-    to_cells(share, channels, halves, pair_ref, inverse_ref, wide_ref, sent_ref)
+        to_cells(k, share, channels, halves, pair_ref, inverse_ref, out_ref)
+
+    sent_ref[...] = out_ref[...].astype(jnp.bfloat16)
 
 
 def row_sums(blocks):
@@ -215,10 +211,11 @@
 
 def adjoint_kernel(
     share, channels, halves, arrived_ref, turned_ref, forward_ref, inverse_ref, sent_ref, modes_ref, wide_ref,
-    pair_ref,
+    out_ref, pair_ref,
 ):
     to_plane_modes(share, channels, halves, arrived_ref, forward_ref, wide_ref, modes_ref)
     wide = 2 * channels
+    each = modes_ref.shape[0] // share
 
     for tile in range(modes_ref.shape[0]):
         real, imag = modes_ref[tile, :channels, :], modes_ref[tile, channels:, :]
@@ -237,8 +234,10 @@
             for part in range(2):
                 sums[part].append(row_sums(blocks[part]))
         store_pair(tile, channels, jnp.concatenate(sums[0], 0), jnp.concatenate(sums[1], 0), pair_ref)
-
-    to_cells(share, channels, halves, pair_ref, inverse_ref, wide_ref, sent_ref)
+        if (tile + 1) % each == 0:
+            to_cells(tile // each, share, channels, halves, pair_ref, inverse_ref, out_ref)
+
+    sent_ref[...] = out_ref[...].astype(jnp.bfloat16)
 
 
 def outer_kernel(share, channels, in_ref, back_ref, slope_ref, point_ref, grad_ref, pointwise_ref, held_ref, sems):
@@ -383,7 +382,7 @@
         name="depth",
     )(off_chip(jnp.asarray(depth_table(share))), off_chip(inputs.reshape(lanes, depth)))
     arrived = exchange(sent)
-    scratch = [unpacked, pltpu.VMEM((tiles, wide, 2 * LANES), jnp.bfloat16)]
+    scratch = [unpacked, unpacked, pltpu.VMEM((tiles, wide, 2 * LANES), jnp.bfloat16)]
     sent, modes_in, turned = pl.pallas_call(
         functools.partial(mix_kernel, share, channels, halves),
         in_specs=[IN_VMEM] * 4, out_specs=[IN_VMEM] * 3,

time: 52.8 us -> 52.7 us (level)
  no operation moved by 1% of the time
where the time goes in v6:
time: 52.7 us; the launch traced here: 52.4 us
  blocking collectives  33.8 us (64%)
  Pallas kernels  13.1 us (25%)
  starting transfers between devices  2.57 us (5%)
  waiting for transfers between devices  2.21 us (4%)
  between operations  0.74 us (1%)
    all_to_all x3, blocking collectives, exchange(): lax.all_to_all(blocks, GRID_AXES, split_axis=0, concat_axis=0, tiled=True)  33.8 us
    pallas_call x1, Pallas kernels, per_device(): pl.pallas_call(functools.partial(outer_kernel, share, channels), in_specs...  5.57 us
    all_to_all x1, starting transfers between devices, exchange(): lax.all_to_all(blocks, GRID_AXES, split_axis=0, concat_axis=0, tiled=True)  2.57 us
    all_to_all x1, waiting for transfers between devices, exchange(): lax.all_to_all(blocks, GRID_AXES, split_axis=0, concat_axis=0, tiled=True)  2.21 us
    pallas_call x1, Pallas kernels, per_device(): pl.pallas_call(functools.partial(mix_kernel, share, channels, halves), in...  2.2 us
    pallas_call x1, Pallas kernels, per_device(): pl.pallas_call(functools.partial(adjoint_kernel, share, channels, halves)...  2.14 us
    pallas_call x1, Pallas kernels, per_device(): pl.pallas_call(functools.partial(depth_kernel, inner, units), in_specs=[I...  1.45 us
  transfers between devices with their start and end apart: 1, of which 1 were waited for; matrix products, arithmetic and copies ran while one was open for 0% of the time, Pallas kernels for 11%

profile of v6, /device:TPU:0, one launch (start us, length us, event | category | flops | bytes accessed | tf_op | source)
XLA Modules:
  0.0 52.4 jit_solution(2755665131096171195)
XLA Ops:
  0.6 0.0 copy-start
  0.6 0.0 copy-start.1
  0.7 0.0 copy-start.2
  0.7 1.4 %depth.1 = bf16[384,128]{1,0:T(8,128)(2,1)S(1)} custom-call(bf16[192,512]{1,0:T(8,128)(2,1)} %constant.6.clone.table_ref, bf16[256,512]{1,0:T(8,128)(2,1)} %bitcast.18), custom_call_target="tpu_custom_call" | custom-call | flops 10000000000 | tf_op jit(solution)/shard_map/depth/pallas_call | solution.py:377
  2.1 0.0 copy-start.3
  2.1 0.0 copy-start.4
  2.1 0.0 copy-start.5
  2.2 0.0 copy-start.6
  2.2 14.9 %all_to_all.20 = bf16[96,4,128]{2,1,0:T(4,128)(2,1)S(1)} all-to-all(bf16[96,4,128]{2,1,0:T(4,128)(2,1)S(1)} %bitcast.23), channel_id=1, replica_groups=mesh['gx'=4,'gy'=8] {'gx','gy'}, dimensions={0} | all-to-all | bytes 196608 | tf_op jit(solution)/shard_map/all_to_all | solution.py:370
  17.1 0.0 copy-done
  17.1 0.0 copy-done.1
  17.1 0.0 copy-done.2
  17.1 2.2 %mix.1 = (bf16[384,128]{1,0:T(8,128)(2,1)S(1)}, f32[6,64,128]{2,1,0:T(8,128)S(1)}, bf16[6,2048,128]{2,1,0:T(8,128)(2,1)S(1)}) custom-call(bf16[384,128]{1,0:T(8,128)(2,1)S(1)} %bitcast.14, bf16[1728,2048]{1,0:T(8,128)(2,1)S(1)} %bitcast.13, bf16[512,256]{1,0:T(8,128)(2,1)S(1)} %copy-done.2, bf16[256,512]{1,0:T(8,128)(2,1)S(1)} %copy-done.1), custom_call_target="tpu_custom_call" | custom-call | tf_op jit(solution)/shard_map/mix/pallas_call | solution.py:386
  19.3 9.5 %all_to_all.21 = bf16[96,4,128]{2,1,0:T(4,128)(2,1)S(1)} all-to-all(bf16[96,4,128]{2,1,0:T(4,128)(2,1)S(1)} %bitcast.21), channel_id=1, replica_groups=mesh['gx'=4,'gy'=8] {'gx','gy'}, dimensions={0} | all-to-all | bytes 196608 | tf_op jit(solution)/shard_map/all_to_all | solution.py:370
  28.7 0.0 copy-done.3
  28.7 0.0 copy-done.4
  28.7 0.0 copy-done.5
  28.7 0.0 copy-done.6
  28.8 0.7 %slope.1 = (bf16[256,512]{1,0:T(8,128)(2,1)S(1)}, bf16[384,128]{1,0:T(8,128)(2,1)S(1)}) custom-call(bf16[384,128]{1,0:T(8,128)(2,1)S(1)} %bitcast.16, bf16[192,512]{1,0:T(8,128)(2,1)S(1)} %copy-done.3, bf16[256,512]{1,0:T(8,128)(2,1)S(1)} %bitcast.19, bf16[256,512]{1,0:T(8,128)(2,1)S(1)} %bitcast.20, bf16[32,32]{1,0:T(8,128)(2,1)S(1)} %copy-done.6), custom_call_target="tpu_custom_call" | custom-call | tf_op jit(solution)/shard_map/slope/pallas_call | solution.py:393
  29.5 9.5 %all_to_all.22 = bf16[96,4,128]{2,1,0:T(4,128)(2,1)S(1)} all-to-all(bf16[96,4,128]{2,1,0:T(4,128)(2,1)S(1)} %bitcast.22), channel_id=1, replica_groups=mesh['gx'=4,'gy'=8] {'gx','gy'}, dimensions={0} | all-to-all | bytes 196608 | tf_op jit(solution)/shard_map/all_to_all | solution.py:370
  39.0 2.1 %adjoint.1 = (bf16[384,128]{1,0:T(8,128)(2,1)}, f32[6,64,128]{2,1,0:T(8,128)S(1)}) custom-call(bf16[384,128]{1,0:T(8,128)(2,1)S(1)} %bitcast.17, bf16[6,2048,128]{2,1,0:T(8,128)(2,1)S(1)} %get-tuple-element.13.turned_ref, bf16[512,256]{1,0:T(8,128)(2,1)S(1)} %copy-done.2, bf16[256,512]{1,0:T(8,128)(2,1)S(1)} %copy-done.1), custom_call_target="tpu_custom_call" | custom-call | tf_op jit(solution)/shard_map/adjoint/pallas_call | solution.py:400
  41.1 2.6 %all-to-all-start.3 = ((bf16[96,4,128]{2,1,0:T(4,128)(2,1)}), bf16[96,4,128]{2,1,0:T(4,128)(2,1)S(1)}, u32[]{:S(2)}, u32[]{:S(2)}) async-start(bf16[96,4,128]{2,1,0:T(4,128)(2,1)} %bitcast.9), calls=%async_computation.3 | async-start | bytes 196608 | tf_op jit(solution)/shard_map/all_to_all | solution.py:370
  43.7 5.6 %outer.1 = (f32[1728,2048]{1,0:T(8,128)}, f32[256,512]{1,0:T(8,128)S(1)}) custom-call(f32[6,64,128]{2,1,0:T(8,128)S(1)} %get-tuple-element.15.in_ref, f32[6,64,128]{2,1,0:T(8,128)S(1)} %get-tuple-element.16.back_ref, bf16[256,512]{1,0:T(8,128)(2,1)S(1)} %get-tuple-element.17.slope_ref, bf16[32,32]{1,0:T(8,128)(2,1)S(1)} %copy-done.6), custom_call_target="tpu_custom_call" | custom-call | flops 905969664 | bytes 14155776 | tf_op jit(solution)/shard_map/outer/pallas_call | solution.py:407
  49.3 2.2 %all-to-all-done.3 = bf16[96,4,128]{2,1,0:T(4,128)(2,1)S(1)} async-done(((bf16[96,4,128]{2,1,0:T(4,128)(2,1)}), bf16[96,4,128]{2,1,0:T(4,128)(2,1)S(1)}, u32[]{:S(2)}, u32[]{:S(2)}) %all-to-all-start.3) | async-done | bytes 98336 | tf_op jit(solution)/shard_map/all_to_all | solution.py:370
  51.5 1.0 %final.1 = bf16[256,512]{1,0:T(8,128)(2,1)} custom-call(bf16[384,128]{1,0:T(8,128)(2,1)S(1)} %bitcast.15, bf16[192,512]{1,0:T(8,128)(2,1)S(1)} %copy-done.3, f32[256,512]{1,0:T(8,128)S(1)} %get-tuple-element.18.pointwise_ref), custom_call_target="tpu_custom_call" | custom-call | tf_op jit(solution)/shard_map/final/pallas_call | solution.py:422
Async XLA Ops:
  0.6 16.4 %copy-start = (bf16[72,24,2048]{2,1,0:T(8,128)(2,1)S(1)}, bf16[72,24,2048]{2,1,0:T(8,128)(2,1)}, u32[]{:S(2)}) copy-start(bf16[72,24,2048]{2,1,0:T(8,128)(2,1)} %param.11) | copy-start | bytes 21233668
  0.6 16.4 %copy-start.1 = (bf16[256,512]{1,0:T(8,128)(2,1)S(1)}, bf16[256,512]{1,0:T(8,128)(2,1)}, u32[]{:S(2)}) copy-start(bf16[256,512]{1,0:T(8,128)(2,1)} %constant.8.clone.inverse_ref) | copy-start | bytes 786436
  0.7 16.4 %copy-start.2 = (bf16[512,256]{1,0:T(8,128)(2,1)S(1)}, bf16[512,256]{1,0:T(8,128)(2,1)}, u32[]{:S(2)}) copy-start(bf16[512,256]{1,0:T(8,128)(2,1)} %constant.7.clone.forward_ref) | copy-start | bytes 786436
  2.1 26.6 %copy-start.3 = (bf16[192,512]{1,0:T(8,128)(2,1)S(1)}, bf16[192,512]{1,0:T(8,128)(2,1)}, u32[]{:S(2)}) copy-start(bf16[192,512]{1,0:T(8,128)(2,1)} %constant.6.clone.table_ref) | copy-start | bytes 589828
  2.1 26.6 %copy-start.4 = (bf16[4,2,32,512]{3,2,1,0:T(8,128)(2,1)S(1)}, bf16[4,2,32,512]{3,2,1,0:T(8,128)(2,1)}, u32[]{:S(2)}) copy-start(bf16[4,2,32,512]{3,2,1,0:T(8,128)(2,1)} %param.8) | copy-start | bytes 786436
  2.1 26.6 %copy-start.5 = (bf16[4,2,32,512]{3,2,1,0:T(8,128)(2,1)S(1)}, bf16[4,2,32,512]{3,2,1,0:T(8,128)(2,1)}, u32[]{:S(2)}) copy-start(bf16[4,2,32,512]{3,2,1,0:T(8,128)(2,1)} %param.9) | copy-start | bytes 786436
  2.2 26.6 %copy-start.6 = (bf16[32,32]{1,0:T(8,128)(2,1)S(1)}, bf16[32,32]{1,0:T(8,128)(2,1)}, u32[]{:S(2)}) copy-start(bf16[32,32]{1,0:T(8,128)(2,1)} %point_ref.3) | copy-start | bytes 6148
  41.1 10.4 %all-to-all-start.3 = ((bf16[96,4,128]{2,1,0:T(4,128)(2,1)}), bf16[96,4,128]{2,1,0:T(4,128)(2,1)S(1)}, u32[]{:S(2)}, u32[]{:S(2)}) async-start(bf16[96,4,128]{2,1,0:T(4,128)(2,1)} %bitcast.9), calls=%async_computation.3 | async-start | bytes 196608 | tf_op jit(solution)/shard_map/all_to_all | solution.py:370

commit v7 on v6

--- a/solution.py
+++ b/solution.py
@@ -17,7 +17,7 @@
 KT = 8
 LANES = 128
 LENGTH = 16
-GROUP = 4
+GROUP = 8
 READ_AHEAD_FLOPS = 10**10
 GRID_AXES = ("gx", "gy")
 

time: 52.7 us -> 52.6 us (level)
  no operation moved by 1% of the time
where the time goes in v7:
time: 52.6 us; the launch traced here: 52.4 us
  blocking collectives  33.8 us (64%)
  Pallas kernels  13 us (25%)
  starting transfers between devices  2.57 us (5%)
  waiting for transfers between devices  2.21 us (4%)
  between operations  0.74 us (1%)
    all_to_all x3, blocking collectives, exchange(): lax.all_to_all(blocks, GRID_AXES, split_axis=0, concat_axis=0, tiled=True)  33.8 us
    pallas_call x1, Pallas kernels, per_device(): pl.pallas_call(functools.partial(outer_kernel, share, channels), in_specs...  5.57 us
    all_to_all x1, starting transfers between devices, exchange(): lax.all_to_all(blocks, GRID_AXES, split_axis=0, concat_axis=0, tiled=True)  2.57 us
    all_to_all x1, waiting for transfers between devices, exchange(): lax.all_to_all(blocks, GRID_AXES, split_axis=0, concat_axis=0, tiled=True)  2.21 us
    pallas_call x1, Pallas kernels, per_device(): pl.pallas_call(functools.partial(adjoint_kernel, share, channels, halves)...  2.14 us
    pallas_call x1, Pallas kernels, per_device(): pl.pallas_call(functools.partial(mix_kernel, share, channels, halves), in...  2.14 us
    pallas_call x1, Pallas kernels, per_device(): pl.pallas_call(functools.partial(depth_kernel, inner, units), in_specs=[I...  1.45 us
  transfers between devices with their start and end apart: 1, of which 1 were waited for; matrix products, arithmetic and copies ran while one was open for 0% of the time, Pallas kernels for 11%

profile of v7, /device:TPU:0, one launch (start us, length us, event | category | flops | bytes accessed | tf_op | source)
XLA Modules:
  0.0 52.4 jit_solution(5782941451416304392)
XLA Ops:
  0.6 0.0 copy-start
  0.6 0.0 copy-start.1
  0.7 0.0 copy-start.2
  0.7 1.4 %depth.1 = bf16[384,128]{1,0:T(8,128)(2,1)S(1)} custom-call(bf16[192,512]{1,0:T(8,128)(2,1)} %constant.6.clone.table_ref, bf16[256,512]{1,0:T(8,128)(2,1)} %bitcast.18), custom_call_target="tpu_custom_call" | custom-call | flops 10000000000 | tf_op jit(solution)/shard_map/depth/pallas_call | solution.py:377
  2.1 0.0 copy-start.3
  2.1 0.0 copy-start.4
  2.1 0.0 copy-start.5
  2.2 0.0 copy-start.6
  2.2 14.9 %all_to_all.20 = bf16[96,4,128]{2,1,0:T(4,128)(2,1)S(1)} all-to-all(bf16[96,4,128]{2,1,0:T(4,128)(2,1)S(1)} %bitcast.23), channel_id=1, replica_groups=mesh['gx'=4,'gy'=8] {'gx','gy'}, dimensions={0} | all-to-all | bytes 196608 | tf_op jit(solution)/shard_map/all_to_all | solution.py:370
  17.1 0.0 copy-done
  17.1 0.0 copy-done.1
  17.1 0.0 copy-done.2
  17.1 2.1 %mix.1 = (bf16[384,128]{1,0:T(8,128)(2,1)S(1)}, f32[6,64,128]{2,1,0:T(8,128)S(1)}, bf16[6,2048,128]{2,1,0:T(8,128)(2,1)S(1)}) custom-call(bf16[384,128]{1,0:T(8,128)(2,1)S(1)} %bitcast.14, bf16[1728,2048]{1,0:T(8,128)(2,1)S(1)} %bitcast.13, bf16[512,256]{1,0:T(8,128)(2,1)S(1)} %copy-done.2, bf16[256,512]{1,0:T(8,128)(2,1)S(1)} %copy-done.1), custom_call_target="tpu_custom_call" | custom-call | tf_op jit(solution)/shard_map/mix/pallas_call | solution.py:386
  19.2 9.5 %all_to_all.21 = bf16[96,4,128]{2,1,0:T(4,128)(2,1)S(1)} all-to-all(bf16[96,4,128]{2,1,0:T(4,128)(2,1)S(1)} %bitcast.21), channel_id=1, replica_groups=mesh['gx'=4,'gy'=8] {'gx','gy'}, dimensions={0} | all-to-all | bytes 196608 | tf_op jit(solution)/shard_map/all_to_all | solution.py:370
  28.7 0.0 copy-done.3
  28.7 0.0 copy-done.4
  28.7 0.0 copy-done.5
  28.7 0.0 copy-done.6
  28.7 0.7 %slope.1 = (bf16[256,512]{1,0:T(8,128)(2,1)S(1)}, bf16[384,128]{1,0:T(8,128)(2,1)S(1)}) custom-call(bf16[384,128]{1,0:T(8,128)(2,1)S(1)} %bitcast.16, bf16[192,512]{1,0:T(8,128)(2,1)S(1)} %copy-done.3, bf16[256,512]{1,0:T(8,128)(2,1)S(1)} %bitcast.19, bf16[256,512]{1,0:T(8,128)(2,1)S(1)} %bitcast.20, bf16[32,32]{1,0:T(8,128)(2,1)S(1)} %copy-done.6), custom_call_target="tpu_custom_call" | custom-call | tf_op jit(solution)/shard_map/slope/pallas_call | solution.py:393
  29.4 9.5 %all_to_all.22 = bf16[96,4,128]{2,1,0:T(4,128)(2,1)S(1)} all-to-all(bf16[96,4,128]{2,1,0:T(4,128)(2,1)S(1)} %bitcast.22), channel_id=1, replica_groups=mesh['gx'=4,'gy'=8] {'gx','gy'}, dimensions={0} | all-to-all | bytes 196608 | tf_op jit(solution)/shard_map/all_to_all | solution.py:370
  38.9 2.1 %adjoint.1 = (bf16[384,128]{1,0:T(8,128)(2,1)}, f32[6,64,128]{2,1,0:T(8,128)S(1)}) custom-call(bf16[384,128]{1,0:T(8,128)(2,1)S(1)} %bitcast.17, bf16[6,2048,128]{2,1,0:T(8,128)(2,1)S(1)} %get-tuple-element.13.turned_ref, bf16[512,256]{1,0:T(8,128)(2,1)S(1)} %copy-done.2, bf16[256,512]{1,0:T(8,128)(2,1)S(1)} %copy-done.1), custom_call_target="tpu_custom_call" | custom-call | tf_op jit(solution)/shard_map/adjoint/pallas_call | solution.py:400
  41.1 2.6 %all-to-all-start.3 = ((bf16[96,4,128]{2,1,0:T(4,128)(2,1)}), bf16[96,4,128]{2,1,0:T(4,128)(2,1)S(1)}, u32[]{:S(2)}, u32[]{:S(2)}) async-start(bf16[96,4,128]{2,1,0:T(4,128)(2,1)} %bitcast.9), calls=%async_computation.3 | async-start | bytes 196608 | tf_op jit(solution)/shard_map/all_to_all | solution.py:370
  43.6 5.6 %outer.1 = (f32[1728,2048]{1,0:T(8,128)}, f32[256,512]{1,0:T(8,128)S(1)}) custom-call(f32[6,64,128]{2,1,0:T(8,128)S(1)} %get-tuple-element.15.in_ref, f32[6,64,128]{2,1,0:T(8,128)S(1)} %get-tuple-element.16.back_ref, bf16[256,512]{1,0:T(8,128)(2,1)S(1)} %get-tuple-element.17.slope_ref, bf16[32,32]{1,0:T(8,128)(2,1)S(1)} %copy-done.6), custom_call_target="tpu_custom_call" | custom-call | flops 905969664 | bytes 14155776 | tf_op jit(solution)/shard_map/outer/pallas_call | solution.py:407
  49.2 2.2 %all-to-all-done.3 = bf16[96,4,128]{2,1,0:T(4,128)(2,1)S(1)} async-done(((bf16[96,4,128]{2,1,0:T(4,128)(2,1)}), bf16[96,4,128]{2,1,0:T(4,128)(2,1)S(1)}, u32[]{:S(2)}, u32[]{:S(2)}) %all-to-all-start.3) | async-done | bytes 98336 | tf_op jit(solution)/shard_map/all_to_all | solution.py:370
  51.4 1.0 %final.1 = bf16[256,512]{1,0:T(8,128)(2,1)} custom-call(bf16[384,128]{1,0:T(8,128)(2,1)S(1)} %bitcast.15, bf16[192,512]{1,0:T(8,128)(2,1)S(1)} %copy-done.3, f32[256,512]{1,0:T(8,128)S(1)} %get-tuple-element.18.pointwise_ref), custom_call_target="tpu_custom_call" | custom-call | tf_op jit(solution)/shard_map/final/pallas_call | solution.py:422
Async XLA Ops:
  0.6 16.4 %copy-start = (bf16[72,24,2048]{2,1,0:T(8,128)(2,1)S(1)}, bf16[72,24,2048]{2,1,0:T(8,128)(2,1)}, u32[]{:S(2)}) copy-start(bf16[72,24,2048]{2,1,0:T(8,128)(2,1)} %param.11) | copy-start | bytes 21233668
  0.6 16.4 %copy-start.1 = (bf16[256,512]{1,0:T(8,128)(2,1)S(1)}, bf16[256,512]{1,0:T(8,128)(2,1)}, u32[]{:S(2)}) copy-start(bf16[256,512]{1,0:T(8,128)(2,1)} %constant.8.clone.inverse_ref) | copy-start | bytes 786436
  0.7 16.4 %copy-start.2 = (bf16[512,256]{1,0:T(8,128)(2,1)S(1)}, bf16[512,256]{1,0:T(8,128)(2,1)}, u32[]{:S(2)}) copy-start(bf16[512,256]{1,0:T(8,128)(2,1)} %constant.7.clone.forward_ref) | copy-start | bytes 786436
  2.1 26.6 %copy-start.3 = (bf16[192,512]{1,0:T(8,128)(2,1)S(1)}, bf16[192,512]{1,0:T(8,128)(2,1)}, u32[]{:S(2)}) copy-start(bf16[192,512]{1,0:T(8,128)(2,1)} %constant.6.clone.table_ref) | copy-start | bytes 589828
  2.1 26.6 %copy-start.4 = (bf16[4,2,32,512]{3,2,1,0:T(8,128)(2,1)S(1)}, bf16[4,2,32,512]{3,2,1,0:T(8,128)(2,1)}, u32[]{:S(2)}) copy-start(bf16[4,2,32,512]{3,2,1,0:T(8,128)(2,1)} %param.8) | copy-start | bytes 786436
  2.1 26.5 %copy-start.5 = (bf16[4,2,32,512]{3,2,1,0:T(8,128)(2,1)S(1)}, bf16[4,2,32,512]{3,2,1,0:T(8,128)(2,1)}, u32[]{:S(2)}) copy-start(bf16[4,2,32,512]{3,2,1,0:T(8,128)(2,1)} %param.9) | copy-start | bytes 786436
  2.2 26.5 %copy-start.6 = (bf16[32,32]{1,0:T(8,128)(2,1)S(1)}, bf16[32,32]{1,0:T(8,128)(2,1)}, u32[]{:S(2)}) copy-start(bf16[32,32]{1,0:T(8,128)(2,1)} %point_ref.3) | copy-start | bytes 6148
  41.1 10.4 %all-to-all-start.3 = ((bf16[96,4,128]{2,1,0:T(4,128)(2,1)}), bf16[96,4,128]{2,1,0:T(4,128)(2,1)S(1)}, u32[]{:S(2)}, u32[]{:S(2)}) async-start(bf16[96,4,128]{2,1,0:T(4,128)(2,1)} %bitcast.9), calls=%async_computation.3 | async-start | bytes 196608 | tf_op jit(solution)/shard_map/all_to_all | solution.py:370

commit v8 on v6

--- a/solution.py
+++ b/solution.py
@@ -210,8 +210,8 @@
 
 
 def adjoint_kernel(
-    share, channels, halves, arrived_ref, turned_ref, forward_ref, inverse_ref, sent_ref, modes_ref, wide_ref,
-    out_ref, pair_ref,
+    share, channels, halves, arrived_ref, turned_ref, forward_ref, inverse_ref, sent_hbm, modes_ref, wide_ref,
+    out_ref, pair_ref, sent_ref, sems,
 ):
     to_plane_modes(share, channels, halves, arrived_ref, forward_ref, wide_ref, modes_ref)
     wide = 2 * channels
@@ -237,7 +237,16 @@
         if (tile + 1) % each == 0:
             to_cells(tile // each, share, channels, halves, pair_ref, inverse_ref, out_ref)
 
-    sent_ref[...] = out_ref[...].astype(jnp.bfloat16)
+    count = sems.shape[0]
+    rows = sent_ref.shape[0] // count
+    copies = []
+    for part in range(count):
+        here = pl.ds(part * rows, rows)
+        sent_ref[here, :] = out_ref[here, :].astype(jnp.bfloat16)
+        copies.append(pltpu.make_async_copy(sent_ref.at[here], sent_hbm.at[here], sems.at[part]))
+        copies[-1].start()
+    for copy in copies:
+        copy.wait()
 
 
 def outer_kernel(share, channels, in_ref, back_ref, slope_ref, point_ref, grad_ref, pointwise_ref, held_ref, sems):
@@ -399,8 +408,9 @@
     arrived = exchange(sent)
     sent, modes_back = pl.pallas_call(
         functools.partial(adjoint_kernel, share, channels, halves),
-        in_specs=[IN_VMEM] * 4, out_specs=[IN_VMEM] * 2, out_shape=[packet, spectra],
-        scratch_shapes=scratch,
+        in_specs=[IN_VMEM] * 4, out_specs=[pl.BlockSpec(memory_space=pl.ANY), IN_VMEM],
+        out_shape=[jax.ShapeDtypeStruct((devices * units, LANES), jnp.bfloat16), spectra],
+        scratch_shapes=scratch + [packet, pltpu.SemaphoreType.DMA((2,))],
         compiler_params=params(12), name="adjoint",
     )(arrived, on_chip(turned), forward, inverse)
     arrived = exchange(sent)

time: 52.7 us -> 52.7 us (level)
  no operation moved by 1% of the time
where the time goes in v8:
time: 52.7 us; the launch traced here: 52.5 us
  blocking collectives  33.8 us (64%)
  Pallas kernels  13.1 us (25%)
  starting transfers between devices  2.59 us (5%)
  waiting for transfers between devices  2.21 us (4%)
  between operations  0.75 us (1%)
    all_to_all x3, blocking collectives, exchange(): lax.all_to_all(blocks, GRID_AXES, split_axis=0, concat_axis=0, tiled=True)  33.8 us
    pallas_call x1, Pallas kernels, per_device(): pl.pallas_call(functools.partial(outer_kernel, share, channels), in_specs...  5.57 us
    all_to_all x1, starting transfers between devices, exchange(): lax.all_to_all(blocks, GRID_AXES, split_axis=0, concat_axis=0, tiled=True)  2.59 us
    all_to_all x1, waiting for transfers between devices, exchange(): lax.all_to_all(blocks, GRID_AXES, split_axis=0, concat_axis=0, tiled=True)  2.21 us
    pallas_call x1, Pallas kernels, per_device(): pl.pallas_call(functools.partial(mix_kernel, share, channels, halves), in...  2.2 us
    pallas_call x1, Pallas kernels, per_device(): pl.pallas_call(functools.partial(adjoint_kernel, share, channels, halves)...  2.15 us
    pallas_call x1, Pallas kernels, per_device(): pl.pallas_call(functools.partial(depth_kernel, inner, units), in_specs=[I...  1.45 us
  transfers between devices with their start and end apart: 1, of which 1 were waited for; matrix products, arithmetic and copies ran while one was open for 0% of the time, Pallas kernels for 11%

profile of v8, /device:TPU:0, one launch (start us, length us, event | category | flops | bytes accessed | tf_op | source)
XLA Modules:
  0.0 52.5 jit_solution(4782775325522385540)
XLA Ops:
  0.6 0.0 copy-start
  0.6 0.0 copy-start.1
  0.7 0.0 copy-start.2
  0.7 1.4 %depth.1 = bf16[384,128]{1,0:T(8,128)(2,1)S(1)} custom-call(bf16[192,512]{1,0:T(8,128)(2,1)} %constant.6.clone.table_ref, bf16[256,512]{1,0:T(8,128)(2,1)} %bitcast.18), custom_call_target="tpu_custom_call" | custom-call | flops 10000000000 | tf_op jit(solution)/shard_map/depth/pallas_call | solution.py:386
  2.1 0.0 copy-start.3
  2.1 0.0 copy-start.4
  2.1 0.0 copy-start.5
  2.2 0.0 copy-start.6
  2.2 14.9 %all_to_all.20 = bf16[96,4,128]{2,1,0:T(4,128)(2,1)S(1)} all-to-all(bf16[96,4,128]{2,1,0:T(4,128)(2,1)S(1)} %bitcast.23), channel_id=1, replica_groups=mesh['gx'=4,'gy'=8] {'gx','gy'}, dimensions={0} | all-to-all | bytes 196608 | tf_op jit(solution)/shard_map/all_to_all | solution.py:379
  17.1 0.0 copy-done
  17.1 0.0 copy-done.1
  17.1 0.0 copy-done.2
  17.1 2.2 %mix.1 = (bf16[384,128]{1,0:T(8,128)(2,1)S(1)}, f32[6,64,128]{2,1,0:T(8,128)S(1)}, bf16[6,2048,128]{2,1,0:T(8,128)(2,1)S(1)}) custom-call(bf16[384,128]{1,0:T(8,128)(2,1)S(1)} %bitcast.14, bf16[1728,2048]{1,0:T(8,128)(2,1)S(1)} %bitcast.13, bf16[512,256]{1,0:T(8,128)(2,1)S(1)} %copy-done.2, bf16[256,512]{1,0:T(8,128)(2,1)S(1)} %copy-done.1), custom_call_target="tpu_custom_call" | custom-call | tf_op jit(solution)/shard_map/mix/pallas_call | solution.py:395
  19.3 9.5 %all_to_all.21 = bf16[96,4,128]{2,1,0:T(4,128)(2,1)S(1)} all-to-all(bf16[96,4,128]{2,1,0:T(4,128)(2,1)S(1)} %bitcast.21), channel_id=1, replica_groups=mesh['gx'=4,'gy'=8] {'gx','gy'}, dimensions={0} | all-to-all | bytes 196608 | tf_op jit(solution)/shard_map/all_to_all | solution.py:379
  28.7 0.0 copy-done.3
  28.7 0.0 copy-done.4
  28.7 0.0 copy-done.5
  28.7 0.0 copy-done.6
  28.8 0.7 %slope.1 = (bf16[256,512]{1,0:T(8,128)(2,1)S(1)}, bf16[384,128]{1,0:T(8,128)(2,1)S(1)}) custom-call(bf16[384,128]{1,0:T(8,128)(2,1)S(1)} %bitcast.16, bf16[192,512]{1,0:T(8,128)(2,1)S(1)} %copy-done.3, bf16[256,512]{1,0:T(8,128)(2,1)S(1)} %bitcast.19, bf16[256,512]{1,0:T(8,128)(2,1)S(1)} %bitcast.20, bf16[32,32]{1,0:T(8,128)(2,1)S(1)} %copy-done.6), custom_call_target="tpu_custom_call" | custom-call | tf_op jit(solution)/shard_map/slope/pallas_call | solution.py:402
  29.5 9.5 %all_to_all.22 = bf16[96,4,128]{2,1,0:T(4,128)(2,1)S(1)} all-to-all(bf16[96,4,128]{2,1,0:T(4,128)(2,1)S(1)} %bitcast.22), channel_id=1, replica_groups=mesh['gx'=4,'gy'=8] {'gx','gy'}, dimensions={0} | all-to-all | bytes 196608 | tf_op jit(solution)/shard_map/all_to_all | solution.py:379
  39.0 2.1 %adjoint.1 = (bf16[384,128]{1,0:T(8,128)(2,1)}, f32[6,64,128]{2,1,0:T(8,128)S(1)}) custom-call(bf16[384,128]{1,0:T(8,128)(2,1)S(1)} %bitcast.17, bf16[6,2048,128]{2,1,0:T(8,128)(2,1)S(1)} %get-tuple-element.13.turned_ref, bf16[512,256]{1,0:T(8,128)(2,1)S(1)} %copy-done.2, bf16[256,512]{1,0:T(8,128)(2,1)S(1)} %copy-done.1), custom_call_target="tpu_custom_call" | custom-call | tf_op jit(solution)/shard_map/adjoint/pallas_call | solution.py:409
  41.1 2.6 %all-to-all-start.3 = ((bf16[96,4,128]{2,1,0:T(4,128)(2,1)}), bf16[96,4,128]{2,1,0:T(4,128)(2,1)S(1)}, u32[]{:S(2)}, u32[]{:S(2)}) async-start(bf16[96,4,128]{2,1,0:T(4,128)(2,1)} %bitcast.9), calls=%async_computation.3 | async-start | bytes 196608 | tf_op jit(solution)/shard_map/all_to_all | solution.py:379
  43.7 5.6 %outer.1 = (f32[1728,2048]{1,0:T(8,128)}, f32[256,512]{1,0:T(8,128)S(1)}) custom-call(f32[6,64,128]{2,1,0:T(8,128)S(1)} %get-tuple-element.15.in_ref, f32[6,64,128]{2,1,0:T(8,128)S(1)} %get-tuple-element.16.back_ref, bf16[256,512]{1,0:T(8,128)(2,1)S(1)} %get-tuple-element.17.slope_ref, bf16[32,32]{1,0:T(8,128)(2,1)S(1)} %copy-done.6), custom_call_target="tpu_custom_call" | custom-call | flops 905969664 | bytes 14155776 | tf_op jit(solution)/shard_map/outer/pallas_call | solution.py:417
  49.3 2.2 %all-to-all-done.3 = bf16[96,4,128]{2,1,0:T(4,128)(2,1)S(1)} async-done(((bf16[96,4,128]{2,1,0:T(4,128)(2,1)}), bf16[96,4,128]{2,1,0:T(4,128)(2,1)S(1)}, u32[]{:S(2)}, u32[]{:S(2)}) %all-to-all-start.3) | async-done | bytes 98336 | tf_op jit(solution)/shard_map/all_to_all | solution.py:379
  51.5 1.0 %final.1 = bf16[256,512]{1,0:T(8,128)(2,1)} custom-call(bf16[384,128]{1,0:T(8,128)(2,1)S(1)} %bitcast.15, bf16[192,512]{1,0:T(8,128)(2,1)S(1)} %copy-done.3, f32[256,512]{1,0:T(8,128)S(1)} %get-tuple-element.18.pointwise_ref), custom_call_target="tpu_custom_call" | custom-call | tf_op jit(solution)/shard_map/final/pallas_call | solution.py:432
Async XLA Ops:
  0.6 16.4 %copy-start = (bf16[72,24,2048]{2,1,0:T(8,128)(2,1)S(1)}, bf16[72,24,2048]{2,1,0:T(8,128)(2,1)}, u32[]{:S(2)}) copy-start(bf16[72,24,2048]{2,1,0:T(8,128)(2,1)} %param.11) | copy-start | bytes 21233668
  0.6 16.4 %copy-start.1 = (bf16[256,512]{1,0:T(8,128)(2,1)S(1)}, bf16[256,512]{1,0:T(8,128)(2,1)}, u32[]{:S(2)}) copy-start(bf16[256,512]{1,0:T(8,128)(2,1)} %constant.8.clone.inverse_ref) | copy-start | bytes 786436
  0.7 16.4 %copy-start.2 = (bf16[512,256]{1,0:T(8,128)(2,1)S(1)}, bf16[512,256]{1,0:T(8,128)(2,1)}, u32[]{:S(2)}) copy-start(bf16[512,256]{1,0:T(8,128)(2,1)} %constant.7.clone.forward_ref) | copy-start | bytes 786436
  2.1 26.6 %copy-start.3 = (bf16[192,512]{1,0:T(8,128)(2,1)S(1)}, bf16[192,512]{1,0:T(8,128)(2,1)}, u32[]{:S(2)}) copy-start(bf16[192,512]{1,0:T(8,128)(2,1)} %constant.6.clone.table_ref) | copy-start | bytes 589828
  2.1 26.6 %copy-start.4 = (bf16[4,2,32,512]{3,2,1,0:T(8,128)(2,1)S(1)}, bf16[4,2,32,512]{3,2,1,0:T(8,128)(2,1)}, u32[]{:S(2)}) copy-start(bf16[4,2,32,512]{3,2,1,0:T(8,128)(2,1)} %param.8) | copy-start | bytes 786436
  2.1 26.6 %copy-start.5 = (bf16[4,2,32,512]{3,2,1,0:T(8,128)(2,1)S(1)}, bf16[4,2,32,512]{3,2,1,0:T(8,128)(2,1)}, u32[]{:S(2)}) copy-start(bf16[4,2,32,512]{3,2,1,0:T(8,128)(2,1)} %param.9) | copy-start | bytes 786436
  2.2 26.6 %copy-start.6 = (bf16[32,32]{1,0:T(8,128)(2,1)S(1)}, bf16[32,32]{1,0:T(8,128)(2,1)}, u32[]{:S(2)}) copy-start(bf16[32,32]{1,0:T(8,128)(2,1)} %point_ref.3) | copy-start | bytes 6148
  41.1 10.4 %all-to-all-start.3 = ((bf16[96,4,128]{2,1,0:T(4,128)(2,1)}), bf16[96,4,128]{2,1,0:T(4,128)(2,1)S(1)}, u32[]{:S(2)}, u32[]{:S(2)}) async-start(bf16[96,4,128]{2,1,0:T(4,128)(2,1)} %bitcast.9), calls=%async_computation.3 | async-start | bytes 196608 | tf_op jit(solution)/shard_map/all_to_all | solution.py:379

commit v9 on v6

--- a/solution.py
+++ b/solution.py
@@ -320,10 +320,20 @@
     send_slots(sent * factor, units, wide_ref, sent_ref)
 
 
-def final_kernel(factor, halves, units, arrived_ref, table_ref, pointwise_ref, grad_ref, wide_ref):
-    arrived = received_slots(arrived_ref, halves, units, wide_ref)
-    spectral = dot(arrived.astype(jnp.bfloat16), table_ref[...], 0, 0)
-    grad_ref[...] = (pointwise_ref[...] + spectral * factor).astype(jnp.bfloat16)
+def final_kernel(factor, halves, units, arrived_ref, table_ref, pointwise_ref, grad_hbm, wide_ref, grad_ref, sems):
+    arrived = received_slots(arrived_ref, halves, units, wide_ref).astype(jnp.bfloat16)
+    count = sems.shape[0]
+    rows = grad_ref.shape[0] // count
+    copies = []
+    for part in range(count):
+        here = slice(part * rows, (part + 1) * rows)
+        spectral = dot(arrived[:, here], table_ref[...], 0, 0)
+        grad_ref[here, :] = (pointwise_ref[here, :] + spectral * factor).astype(jnp.bfloat16)
+        place = pl.ds(part * rows, rows)
+        copies.append(pltpu.make_async_copy(grad_ref.at[place], grad_hbm.at[place], sems.at[part]))
+        copies[-1].start()
+    for copy in copies:
+        copy.wait()
 
 
 def params(mebibytes, semantics=None):
@@ -421,8 +431,9 @@
     )(on_chip(modes_in), on_chip(modes_back), on_chip(slope), point)
     grad_input = pl.pallas_call(
         functools.partial(final_kernel, inner, halves, units),
-        in_specs=[IN_VMEM] * 3, out_specs=IN_VMEM, out_shape=jax.ShapeDtypeStruct((lanes, depth), jnp.bfloat16),
-        scratch_shapes=[unpacked],
+        in_specs=[IN_VMEM] * 3, out_specs=pl.BlockSpec(memory_space=pl.ANY),
+        out_shape=jax.ShapeDtypeStruct((lanes, depth), jnp.bfloat16),
+        scratch_shapes=[unpacked, pltpu.VMEM((lanes, depth), jnp.bfloat16), pltpu.SemaphoreType.DMA((2,))],
         compiler_params=params(8), name="final",
     )(arrived, table, on_chip(pointwise))
     return grad_input.reshape(inputs.shape), grad_spectral.reshape(spectral_weight.shape)

time: 52.7 us -> 52.7 us (level)
  no operation moved by 1% of the time
where the time goes in v9:
time: 52.7 us; the launch traced here: 52.4 us
  blocking collectives  33.8 us (64%)
  Pallas kernels  13 us (25%)
  starting transfers between devices  2.57 us (5%)
  waiting for transfers between devices  2.21 us (4%)
  between operations  0.74 us (1%)
    all_to_all x3, blocking collectives, exchange(): lax.all_to_all(blocks, GRID_AXES, split_axis=0, concat_axis=0, tiled=True)  33.8 us
    pallas_call x1, Pallas kernels, per_device(): pl.pallas_call(functools.partial(outer_kernel, share, channels), in_specs...  5.57 us
    all_to_all x1, starting transfers between devices, exchange(): lax.all_to_all(blocks, GRID_AXES, split_axis=0, concat_axis=0, tiled=True)  2.57 us
    all_to_all x1, waiting for transfers between devices, exchange(): lax.all_to_all(blocks, GRID_AXES, split_axis=0, concat_axis=0, tiled=True)  2.21 us
    pallas_call x1, Pallas kernels, per_device(): pl.pallas_call(functools.partial(mix_kernel, share, channels, halves), in...  2.2 us
    pallas_call x1, Pallas kernels, per_device(): pl.pallas_call(functools.partial(adjoint_kernel, share, channels, halves)...  2.14 us
    pallas_call x1, Pallas kernels, per_device(): pl.pallas_call(functools.partial(depth_kernel, inner, units), in_specs=[I...  1.45 us
  transfers between devices with their start and end apart: 1, of which 1 were waited for; matrix products, arithmetic and copies ran while one was open for 0% of the time, Pallas kernels for 11%

profile of v9, /device:TPU:0, one launch (start us, length us, event | category | flops | bytes accessed | tf_op | source)
XLA Modules:
  0.0 52.4 jit_solution(4463158444409695198)
XLA Ops:
  0.6 0.0 copy-start
  0.6 0.0 copy-start.1
  0.7 0.0 copy-start.2
  0.7 1.4 %depth.1 = bf16[384,128]{1,0:T(8,128)(2,1)S(1)} custom-call(bf16[192,512]{1,0:T(8,128)(2,1)} %constant.6.clone.table_ref, bf16[256,512]{1,0:T(8,128)(2,1)} %bitcast.18), custom_call_target="tpu_custom_call" | custom-call | flops 10000000000 | tf_op jit(solution)/shard_map/depth/pallas_call | solution.py:387
  2.1 0.0 copy-start.3
  2.1 0.0 copy-start.4
  2.1 0.0 copy-start.5
  2.2 0.0 copy-start.6
  2.2 14.9 %all_to_all.20 = bf16[96,4,128]{2,1,0:T(4,128)(2,1)S(1)} all-to-all(bf16[96,4,128]{2,1,0:T(4,128)(2,1)S(1)} %bitcast.23), channel_id=1, replica_groups=mesh['gx'=4,'gy'=8] {'gx','gy'}, dimensions={0} | all-to-all | bytes 196608 | tf_op jit(solution)/shard_map/all_to_all | solution.py:380
  17.1 0.0 copy-done
  17.1 0.0 copy-done.1
  17.1 0.0 copy-done.2
  17.1 2.2 %mix.1 = (bf16[384,128]{1,0:T(8,128)(2,1)S(1)}, f32[6,64,128]{2,1,0:T(8,128)S(1)}, bf16[6,2048,128]{2,1,0:T(8,128)(2,1)S(1)}) custom-call(bf16[384,128]{1,0:T(8,128)(2,1)S(1)} %bitcast.14, bf16[1728,2048]{1,0:T(8,128)(2,1)S(1)} %bitcast.13, bf16[512,256]{1,0:T(8,128)(2,1)S(1)} %copy-done.2, bf16[256,512]{1,0:T(8,128)(2,1)S(1)} %copy-done.1), custom_call_target="tpu_custom_call" | custom-call | tf_op jit(solution)/shard_map/mix/pallas_call | solution.py:396
  19.3 9.5 %all_to_all.21 = bf16[96,4,128]{2,1,0:T(4,128)(2,1)S(1)} all-to-all(bf16[96,4,128]{2,1,0:T(4,128)(2,1)S(1)} %bitcast.21), channel_id=1, replica_groups=mesh['gx'=4,'gy'=8] {'gx','gy'}, dimensions={0} | all-to-all | bytes 196608 | tf_op jit(solution)/shard_map/all_to_all | solution.py:380
  28.7 0.0 copy-done.3
  28.7 0.0 copy-done.4
  28.7 0.0 copy-done.5
  28.7 0.0 copy-done.6
  28.8 0.7 %slope.1 = (bf16[256,512]{1,0:T(8,128)(2,1)S(1)}, bf16[384,128]{1,0:T(8,128)(2,1)S(1)}) custom-call(bf16[384,128]{1,0:T(8,128)(2,1)S(1)} %bitcast.16, bf16[192,512]{1,0:T(8,128)(2,1)S(1)} %copy-done.3, bf16[256,512]{1,0:T(8,128)(2,1)S(1)} %bitcast.19, bf16[256,512]{1,0:T(8,128)(2,1)S(1)} %bitcast.20, bf16[32,32]{1,0:T(8,128)(2,1)S(1)} %copy-done.6), custom_call_target="tpu_custom_call" | custom-call | tf_op jit(solution)/shard_map/slope/pallas_call | solution.py:403
  29.5 9.5 %all_to_all.22 = bf16[96,4,128]{2,1,0:T(4,128)(2,1)S(1)} all-to-all(bf16[96,4,128]{2,1,0:T(4,128)(2,1)S(1)} %bitcast.22), channel_id=1, replica_groups=mesh['gx'=4,'gy'=8] {'gx','gy'}, dimensions={0} | all-to-all | bytes 196608 | tf_op jit(solution)/shard_map/all_to_all | solution.py:380
  39.0 2.1 %adjoint.1 = (bf16[384,128]{1,0:T(8,128)(2,1)}, f32[6,64,128]{2,1,0:T(8,128)S(1)}) custom-call(bf16[384,128]{1,0:T(8,128)(2,1)S(1)} %bitcast.17, bf16[6,2048,128]{2,1,0:T(8,128)(2,1)S(1)} %get-tuple-element.13.turned_ref, bf16[512,256]{1,0:T(8,128)(2,1)S(1)} %copy-done.2, bf16[256,512]{1,0:T(8,128)(2,1)S(1)} %copy-done.1), custom_call_target="tpu_custom_call" | custom-call | tf_op jit(solution)/shard_map/adjoint/pallas_call | solution.py:410
  41.1 2.6 %all-to-all-start.3 = ((bf16[96,4,128]{2,1,0:T(4,128)(2,1)}), bf16[96,4,128]{2,1,0:T(4,128)(2,1)S(1)}, u32[]{:S(2)}, u32[]{:S(2)}) async-start(bf16[96,4,128]{2,1,0:T(4,128)(2,1)} %bitcast.9), calls=%async_computation.3 | async-start | bytes 196608 | tf_op jit(solution)/shard_map/all_to_all | solution.py:380
  43.7 5.6 %outer.1 = (f32[1728,2048]{1,0:T(8,128)}, f32[256,512]{1,0:T(8,128)S(1)}) custom-call(f32[6,64,128]{2,1,0:T(8,128)S(1)} %get-tuple-element.15.in_ref, f32[6,64,128]{2,1,0:T(8,128)S(1)} %get-tuple-element.16.back_ref, bf16[256,512]{1,0:T(8,128)(2,1)S(1)} %get-tuple-element.17.slope_ref, bf16[32,32]{1,0:T(8,128)(2,1)S(1)} %copy-done.6), custom_call_target="tpu_custom_call" | custom-call | flops 905969664 | bytes 14155776 | tf_op jit(solution)/shard_map/outer/pallas_call | solution.py:417
  49.3 2.2 %all-to-all-done.3 = bf16[96,4,128]{2,1,0:T(4,128)(2,1)S(1)} async-done(((bf16[96,4,128]{2,1,0:T(4,128)(2,1)}), bf16[96,4,128]{2,1,0:T(4,128)(2,1)S(1)}, u32[]{:S(2)}, u32[]{:S(2)}) %all-to-all-start.3) | async-done | bytes 98336 | tf_op jit(solution)/shard_map/all_to_all | solution.py:380
  51.5 1.0 %final.1 = bf16[256,512]{1,0:T(8,128)(2,1)} custom-call(bf16[384,128]{1,0:T(8,128)(2,1)S(1)} %bitcast.15, bf16[192,512]{1,0:T(8,128)(2,1)S(1)} %copy-done.3, f32[256,512]{1,0:T(8,128)S(1)} %get-tuple-element.18.pointwise_ref), custom_call_target="tpu_custom_call" | custom-call | tf_op jit(solution)/shard_map/final/pallas_call | solution.py:432
Async XLA Ops:
  0.6 16.4 %copy-start = (bf16[72,24,2048]{2,1,0:T(8,128)(2,1)S(1)}, bf16[72,24,2048]{2,1,0:T(8,128)(2,1)}, u32[]{:S(2)}) copy-start(bf16[72,24,2048]{2,1,0:T(8,128)(2,1)} %param.11) | copy-start | bytes 21233668
  0.6 16.4 %copy-start.1 = (bf16[256,512]{1,0:T(8,128)(2,1)S(1)}, bf16[256,512]{1,0:T(8,128)(2,1)}, u32[]{:S(2)}) copy-start(bf16[256,512]{1,0:T(8,128)(2,1)} %constant.8.clone.inverse_ref) | copy-start | bytes 786436
  0.7 16.4 %copy-start.2 = (bf16[512,256]{1,0:T(8,128)(2,1)S(1)}, bf16[512,256]{1,0:T(8,128)(2,1)}, u32[]{:S(2)}) copy-start(bf16[512,256]{1,0:T(8,128)(2,1)} %constant.7.clone.forward_ref) | copy-start | bytes 786436
  2.1 26.6 %copy-start.3 = (bf16[192,512]{1,0:T(8,128)(2,1)S(1)}, bf16[192,512]{1,0:T(8,128)(2,1)}, u32[]{:S(2)}) copy-start(bf16[192,512]{1,0:T(8,128)(2,1)} %constant.6.clone.table_ref) | copy-start | bytes 589828
  2.1 26.6 %copy-start.4 = (bf16[4,2,32,512]{3,2,1,0:T(8,128)(2,1)S(1)}, bf16[4,2,32,512]{3,2,1,0:T(8,128)(2,1)}, u32[]{:S(2)}) copy-start(bf16[4,2,32,512]{3,2,1,0:T(8,128)(2,1)} %param.8) | copy-start | bytes 786436
  2.1 26.6 %copy-start.5 = (bf16[4,2,32,512]{3,2,1,0:T(8,128)(2,1)S(1)}, bf16[4,2,32,512]{3,2,1,0:T(8,128)(2,1)}, u32[]{:S(2)}) copy-start(bf16[4,2,32,512]{3,2,1,0:T(8,128)(2,1)} %param.9) | copy-start | bytes 786436
  2.2 26.6 %copy-start.6 = (bf16[32,32]{1,0:T(8,128)(2,1)S(1)}, bf16[32,32]{1,0:T(8,128)(2,1)}, u32[]{:S(2)}) copy-start(bf16[32,32]{1,0:T(8,128)(2,1)} %point_ref.3) | copy-start | bytes 6148
  41.1 10.4 %all-to-all-start.3 = ((bf16[96,4,128]{2,1,0:T(4,128)(2,1)}), bf16[96,4,128]{2,1,0:T(4,128)(2,1)S(1)}, u32[]{:S(2)}, u32[]{:S(2)}) async-start(bf16[96,4,128]{2,1,0:T(4,128)(2,1)} %bitcast.9), calls=%async_computation.3 | async-start | bytes 196608 | tf_op jit(solution)/shard_map/all_to_all | solution.py:380
